TPU v7x, 32 devices: a whole 2x2x4 slice. The times are simulated.
32 devices in a mesh: wide: 8 (over z, y), narrow: 4 (over x, core).
Axes of the slice: x: 2, y: 2, z: 4, core: 2. Of those that a mesh axis runs over, the one named last changes fastest.
Arguments:
- populations: float32 [19, 16, 128, 512], P(None, 'wide', None, 'narrow'), may hold values from 0 to 1, as said below
- conformation: float32 [6, 16, 128, 512], P(None, 'wide', None, 'narrow'), may hold values from -0.3 to 3, as said below
Outputs:
- read: float32 [19, 16, 128, 512], P(None, 'wide', None, 'narrow')
- new_conformation: float32 [6, 16, 128, 512], P(None, 'wide', None, 'narrow')
Inputs may be any that keep to these rules, and one draw needn't show every extreme that they name: Every population is positive, and the populations of a cell sum to between 0.6 and 1.4. Each cell's conformation tensor is symmetric and diagonally dominant with positive diagonal, its trace at most 9.
All inputs are finite; a program needn't handle non-finite values.
Results may differ from a plain program's by a relative error of at most 0.00002.
Values sent between devices are 32-bit elements; how exact they have to be, the bound alone decides.
No kernel may reach another device: no remote copies, remote signals or barrier semaphores. Data moves between devices by JAX's collectives and lax.ppermute only.
A program may use at most 192 MiB of HBM per device.

v0:
```python
import jax
import jax.numpy as jnp
from jax import lax
from jax.sharding import PartitionSpec as P

VELOCITIES = (
    (0, 0, 0),
    (1, 0, 0),
    (-1, 0, 0),
    (0, 1, 0),
    (0, -1, 0),
    (0, 0, 1),
    (0, 0, -1),
    (1, 1, 0),
    (-1, -1, 0),
    (1, -1, 0),
    (-1, 1, 0),
    (1, 0, 1),
    (-1, 0, -1),
    (1, 0, -1),
    (-1, 0, 1),
    (0, 1, 1),
    (0, -1, -1),
    (0, 1, -1),
    (0, -1, 1),
)
LATTICE_WEIGHTS = (1.0 / 3.0,) + (1.0 / 18.0,) * 6 + (1.0 / 36.0,) * 12
OPPOSITE = (0, 2, 1, 4, 3, 6, 5, 8, 7, 10, 9, 12, 11, 14, 13, 16, 15, 18, 17)
SYMMETRIC_INDEX = ((0, 3, 4), (3, 1, 5), (4, 5, 2))
COMPONENT_PAIRS = ((0, 0), (1, 1), (2, 2), (0, 1), (0, 2), (1, 2))
SOLVENT_TIME = 0.8
RELAX_TIME = 20.0
POLYMER_VISC = 1.0
EXTENSION_SQ = 100.0
DIFFUSIVITY = 0.05
DRIVE_FORCE = 1e-05


def padded_2(shard, sides, width):
    for axis, dim in sides:
        peers, length = (lax.axis_size(axis), shard.shape[dim])
        up = [(i, (i + 1) % peers) for i in range(peers)]
        down = [(j, i) for i, j in up]
        last = lax.slice_in_dim(shard, length - width, length, axis=dim)
        initial = lax.slice_in_dim(shard, 0, width, axis=dim)
        before = lax.ppermute(last, axis, up)
        after = lax.ppermute(initial, axis, down)
        shard = jnp.concatenate([before, shard, after], axis=dim)
    return shard


def wall_pad(field, odd):
    lower = field[:, :, :1]
    upper = field[:, :, -1:]
    if odd:
        lower, upper = (-lower, -upper)
    return jnp.concatenate([lower, field, upper], axis=2)


def gradients(padded, odd):
    centre = padded[:, 1:-1, :, 1:-1]
    walled = wall_pad(centre, odd)
    along_x = 0.5 * (padded[:, 2:, :, 1:-1] - padded[:, :-2, :, 1:-1])
    along_y = 0.5 * (walled[:, :, 2:] - walled[:, :, :-2])
    along_z = 0.5 * (padded[:, 1:-1, :, 2:] - padded[:, 1:-1, :, :-2])
    return (along_x, along_y, along_z)


def laplacian(padded):
    centre = padded[:, 1:-1, :, 1:-1]
    walled = wall_pad(centre, False)
    total = padded[:, 2:, :, 1:-1] + padded[:, :-2, :, 1:-1]
    total = total + walled[:, :, 2:] + walled[:, :, :-2]
    total = total + padded[:, 1:-1, :, 2:] + padded[:, 1:-1, :, :-2]
    return total - 6.0 * centre


def peterlin_of(conform):
    trace = conform[0] + conform[1] + conform[2]
    return (EXTENSION_SQ - 3.0) / (EXTENSION_SQ - trace)


def relaxed_part(conform, peterlin):
    parts = []
    for number in range(6):
        term = peterlin * conform[number]
        if number < 3:
            term = term - 1.0
        parts.append(term)
    return jnp.stack(parts)


def polymer_force(padded_conf):
    stress = POLYMER_VISC / RELAX_TIME * relaxed_part(padded_conf, peterlin_of(padded_conf))
    along_x, along_y, along_z = gradients(stress, False)
    parts = []
    for first in range(3):
        row = SYMMETRIC_INDEX[first]
        term = along_x[row[0]] + along_y[row[1]] + along_z[row[2]]
        if first == 0:
            term = term + DRIVE_FORCE
        parts.append(term)
    return jnp.stack(parts)


def momentum_sums(popul):
    density = jnp.sum(popul, axis=0)
    parts = [density]
    for axis_num in range(3):
        moment = jnp.zeros_like(density)
        for number in range(19):
            weight_c = VELOCITIES[number][axis_num]
            if weight_c == 1:
                moment = moment + popul[number]
            elif weight_c == -1:
                moment = moment - popul[number]
        parts.append(moment)
    return jnp.stack(parts)


def moments(popul, force):
    sums = momentum_sums(popul)
    velocity = jnp.stack(
        [(sums[1 + axis_num] + 0.5 * force[axis_num]) / sums[0] for axis_num in range(3)]
    )
    return (sums[0], velocity)


def conform_update(padded_conf, velocity, padded_velocity):
    conform = padded_conf[:, 1:-1, :, 1:-1]
    grad_c = gradients(padded_conf, False)
    grad_v = gradients(padded_velocity, True)
    advect = velocity[0] * grad_c[0] + velocity[1] * grad_c[1] + velocity[2] * grad_c[2]
    stretch_list = []
    for first, second in COMPONENT_PAIRS:
        term = jnp.zeros_like(conform[0])
        for inner in range(3):
            term = term + conform[SYMMETRIC_INDEX[first][inner]] * grad_v[inner][second]
            term = term + grad_v[inner][first] * conform[SYMMETRIC_INDEX[inner][second]]
        stretch_list.append(term)
    stretch = jnp.stack(stretch_list)
    relax = relaxed_part(conform, peterlin_of(conform)) / RELAX_TIME
    return conform - advect + stretch - relax + DIFFUSIVITY * laplacian(padded_conf)


def collide(popul, density, velocity, force):
    speed_sq = velocity[0] * velocity[0] + velocity[1] * velocity[1] + velocity[2] * velocity[2]
    factor = 1.0 - 0.5 / SOLVENT_TIME
    parts = []
    for number in range(19):
        vec = VELOCITIES[number]
        weight = LATTICE_WEIGHTS[number]
        along = vec[0] * velocity[0] + vec[1] * velocity[1] + vec[2] * velocity[2]
        equil = weight * density * (1.0 + 3.0 * along + 4.5 * along * along - 1.5 * speed_sq)
        push = 0.0
        for axis_num in range(3):
            push = push + 3.0 * (vec[axis_num] - velocity[axis_num]) * force[axis_num]
            push = push + 9.0 * along * vec[axis_num] * force[axis_num]
        parts.append(
            popul[number] - (popul[number] - equil) / SOLVENT_TIME + factor * weight * push
        )
    return jnp.stack(parts)


def wall_walk(shifted, bounced, step_y):
    if step_y == 1:
        return jnp.concatenate([bounced[:, :1], shifted[:, :-1]], axis=1)
    if step_y == -1:
        return jnp.concatenate([shifted[:, 1:], bounced[:, -1:]], axis=1)
    return shifted


def body(populations, conformation):
    padded_conf = padded_2(conformation, (("wide", 1), ("narrow", 3)), 1)
    force = polymer_force(padded_conf)
    density, velocity = moments(populations, force)
    padded_velocity = padded_2(velocity, (("wide", 1), ("narrow", 3)), 1)
    new_conformation = conform_update(padded_conf, velocity, padded_velocity)
    post = collide(populations, density, velocity, force)
    planes_x = post.shape[1]
    planes_z = post.shape[3]
    parts = []
    padded_post = padded_2(post, (("wide", 1), ("narrow", 3)), 1)
    for number in range(19):
        vec = VELOCITIES[number]
        start_x = 1 - vec[0]
        start_z = 1 - vec[2]
        shifted = padded_post[number, start_x : start_x + planes_x, :, start_z : start_z + planes_z]
        parts.append(wall_walk(shifted, post[OPPOSITE[number]], vec[1]))
    return (jnp.stack(parts), new_conformation)


def solution(mesh):
    placed = (P(None, "wide", None, "narrow"), P(None, "wide", None, "narrow"))
    return jax.shard_map(
        body,
        mesh=mesh,
        in_specs=placed,
        out_specs=(P(None, "wide", None, "narrow"), P(None, "wide", None, "narrow")),
        check_vma=False,
    )
```

profile of v0, /device:TPU:0, one launch (start us, length us, event | category | flops | bytes accessed | tf_op | source)
XLA Modules:
  0.0 159.9 jit_solution(11620180451846342644)
XLA Ops:
  0.6 1.2 fusion.306
  1.9 3.0 %collective-permute-start = (f32[6,1,128,128]{3,2,1,0:T(8,128)S(1)}, f32[6,1,128,128]{3,2,1,0:T(8,128)S(1)}, u32[]{:S(2)}, u32[]{:S(2)}) collective-permute-start(f32[6,1,128,128]{3,2,1,0:T(8,128)S(1)} %get-tuple-element.77), channel_id=1, source_target_pairs={{0,4},{4,8},{8,12},{12,16},{16,20},{20,24},{24,28},{28,0},{1,5},{5... | collective-permute-start | bytes 1179656 | tf_op jit(solution)/shard_map/ppermute | solution.py:46
  4.9 3.1 %collective-permute-start.1 = (f32[6,1,128,128]{3,2,1,0:T(8,128)S(1)}, f32[6,1,128,128]{3,2,1,0:T(8,128)S(1)}, u32[]{:S(2)}, u32[]{:S(2)}) collective-permute-start(f32[6,1,128,128]{3,2,1,0:T(8,128)S(1)} %get-tuple-element.76), channel_id=1, source_target_pairs={{4,0},{8,4},{12,8},{16,12},{20,16},{24,20},{28,24},{0,28},{5,1},{9... | collective-permute-start | bytes 1179656 | tf_op jit(solution)/shard_map/ppermute | solution.py:47
  8.0 13.7 %collective-permute-done = f32[6,1,128,128]{3,2,1,0:T(8,128)S(1)} collective-permute-done((f32[6,1,128,128]{3,2,1,0:T(8,128)S(1)}, f32[6,1,128,128]{3,2,1,0:T(8,128)S(1)}, u32[]{:S(2)}, u32[]{:S(2)}) %collective-permute-start) | collective-permute-done | bytes 393248 | tf_op jit(solution)/shard_map/ppermute | solution.py:46
  21.7 0.8 copy-done.11
  22.6 1.3 collective-permute-done.1
  23.9 0.7 copy-done.13
  24.7 2.2 %fusion.303 = (f32[6,4,128,1]{3,2,1,0:T(8,128)}, f32[6,4,128,1]{3,2,1,0:T(8,128)}) fusion(f32[6,4,128,128]{3,2,1,0:T(8,128)S(1)} %constant_dynamic-update-slice_fusion), kind=kLoop, calls=%fused_computation.549 | loop fusion | bytes 49152 | tf_op jit(solution)/shard_map/slice | solution.py:44
  26.9 2.0 %copy.44 = f32[6,4,128,1]{2,1,3,0:T(4,128)S(1)} copy(f32[6,4,128,1]{3,2,1,0:T(8,128)} %get-tuple-element.67) | data formatting | bytes 24576 | tf_op jit(solution)/shard_map/slice | solution.py:44
  28.9 1.9 %copy.45 = f32[6,4,128,1]{2,1,3,0:T(4,128)S(1)} copy(f32[6,4,128,1]{3,2,1,0:T(8,128)} %get-tuple-element.68) | data formatting | bytes 24576 | tf_op jit(solution)/shard_map/slice | solution.py:45
  31.5 2.6 %collective-permute-done.2 = f32[6,4,128,1]{2,1,3,0:T(4,128)S(1)} collective-permute-done((f32[6,4,128,1]{2,1,3,0:T(4,128)S(1)}, f32[6,4,128,1]{2,1,3,0:T(4,128)S(1)}, u32[]{:S(2)}, u32[]{:S(2)}) %collective-permute-start.2) | collective-permute-done | bytes 12320 | tf_op jit(solution)/shard_map/ppermute | solution.py:46
  34.1 1.7 %copy.46 = f32[6,4,128,1]{3,2,1,0:T(8,128)} copy(f32[6,4,128,1]{2,1,3,0:T(4,128)S(1)} %collective-permute-done.2) | data formatting | bytes 24576 | tf_op jit(solution)/shard_map/ppermute | solution.py:46
  35.9 1.7 %copy.47 = f32[6,4,128,1]{3,2,1,0:T(8,128)} copy(f32[6,4,128,1]{2,1,3,0:T(4,128)S(1)} %collective-permute-done.3) | data formatting | bytes 24576 | tf_op jit(solution)/shard_map/ppermute | solution.py:47
  37.5 3.6 %pad_maximum_fusion.1 = f32[6,4,128,130]{3,2,1,0:T(8,128)S(1)} fusion(f32[6,4,128,1]{3,2,1,0:T(8,128)} %copy.47, f32[6,4,128,128]{3,2,1,0:T(8,128)} %copy-done.5, f32[6,4,128,1]{3,2,1,0:T(8,128)} %copy.46), kind=kLoop, calls=%fused_computation.1 | loop fusion | flops 798720 | bytes 3194880 | tf_op jit(solution)/shard_map/concatenate | solution.py:48
  42.1 0.9 fusion.3
  43.1 0.8 multiply_bitcast_fusion
  43.9 0.7 multiply_bitcast_fusion.1
  44.6 0.7 multiply_bitcast_fusion.2
  45.7 1.4 copy-done.2
  47.8 0.7 slice.672
  48.5 0.7 slice.674
  49.2 1.2 collective-permute-start.9
  50.4 3.5 %collective-permute-start.8 = (f32[3,1,128,128]{3,2,1,0:T(8,128)S(1)}, f32[3,1,128,128]{3,2,1,0:T(8,128)S(1)}, u32[]{:S(2)}, u32[]{:S(2)}) collective-permute-start(f32[3,1,128,128]{3,2,1,0:T(8,128)S(1)} %get-tuple-element.97), channel_id=1, source_target_pairs={{4,0},{8,4},{12,8},{16,12},{20,16},{24,20},{28,24},{0,28},{5,1},{9... | collective-permute-start | bytes 589832 | tf_op jit(solution)/shard_map/ppermute | solution.py:47
  54.0 1.5 copy.83
  59.6 1.6 %fusion.302 = (f32[19,1,128,128]{3,2,1,0:T(8,128)}, f32[19,1,128,128]{3,2,1,0:T(8,128)}) fusion(f32[19,2,128,128]{3,2,1,0:T(8,128)S(1)} %fusion.163), kind=kLoop, calls=%fused_computation.548 | loop fusion | bytes 4980736 | tf_op jit(solution)/shard_map/slice | solution.py:45
  61.2 1.5 collective-permute-start.5
  64.2 0.6 multiply_add_fusion.12
  64.9 1.5 fusion.305
  66.4 1.4 copy.54
  67.8 1.4 copy.56
  69.2 1.7 %collective-permute-start.10 = (f32[3,4,128,1]{2,1,3,0:T(4,128)S(1)}, f32[3,4,128,1]{2,1,3,0:T(4,128)S(1)}, u32[]{:S(2)}, u32[]{:S(2)}) collective-permute-start(f32[3,4,128,1]{2,1,3,0:T(4,128)S(1)} %copy.54), channel_id=1, source_target_pairs={{1,0},{2,1},{3,2},{0,3},{5,4},{6,5},{7,6},{4,7},{9,8},{10,9},{11,1... | collective-permute-start | bytes 18440 | tf_op jit(solution)/shard_map/ppermute | solution.py:47
  70.9 1.8 %fusion.12 = (f32[3,2,128,128]{3,2,1,0:T(8,128)S(1)}, f32[3,2,128,128]{3,2,1,0:T(8,128)}) fusion(f32[3,1,128,128]{3,2,1,0:T(8,128)S(1)} %collective-permute-done.9, f32[1,2,128,128]{3,2,1,0:T(8,128)S(1)} %get-tuple-element.11, f32[1,2,128,128]{3,2,1,0:T(8,128)S(1)} %get-tuple-element.8, f32[1,2,128,128]{3,2,1,0:T(8,128)S(1)} %get-tuple-element.5, ...), kind=kLoop, calls=%fused_computation.51 | loop fusion | flops 1572864 | bytes 1579008 | tf_op jit(solution)/shard_map/mul | solution.py:63
  72.7 1.3 copy.55
  74.0 1.2 copy.57
  75.2 1.6 fusion.8
  78.0 0.6 copy-done.6
  79.7 1.8 %multiply_add_fusion = f32[6,2,128,128]{3,2,1,0:T(8,128)} fusion(f32[6,2,128,128]{3,2,1,0:T(8,128)S(1)} %copy-done.4, f32[6,2,128,128]{3,2,1,0:T(8,128)S(1)} %multiply_dynamic-update-slice_fusion, f32[6,2,128,128]{3,2,1,0:T(8,128)S(1)} %get-tuple-element.71, f32[6,4,128,1]{3,2,1,0:T(8,128)S(1)} %copy-done.8, f32[6,4,128,128]{3,2,1,0:T(8,128)S(1)} %copy-done.6, ...), kind=kLoop, calls=%fused_computation.18 | loop fusion | flops 5308416 | bytes 5935104 | tf_op jit(solution)/shard_map/add | solution.py:143
  81.5 34.7 %collective-permute-done.5 = f32[19,1,128,128]{3,2,1,0:T(8,128)} collective-permute-done((f32[19,1,128,128]{3,2,1,0:T(8,128)}, f32[19,1,128,128]{3,2,1,0:T(8,128)}, u32[]{:S(2)}, u32[]{:S(2)}) %collective-permute-start.5) | collective-permute-done | bytes 1245216 | tf_op jit(solution)/shard_map/ppermute | solution.py:47
  116.2 2.2 %pad_maximum_fusion = f32[19,4,128,128]{3,2,1,0:T(8,128)S(1)} fusion(f32[19,1,128,128]{3,2,1,0:T(8,128)} %collective-permute-done.5, f32[19,2,128,128]{3,2,1,0:T(8,128)S(1)} %fusion.163, f32[19,1,128,128]{3,2,1,0:T(8,128)} %collective-permute-done.4), kind=kLoop, calls=%fused_computation | loop fusion | flops 2490368 | bytes 9961472 | tf_op jit(solution)/shard_map/concatenate | solution.py:48
  118.4 5.7 %fusion.300 = (f32[19,4,128,1]{3,2,1,0:T(8,128)}, f32[19,4,128,1]{3,2,1,0:T(8,128)}) fusion(f32[19,4,128,128]{3,2,1,0:T(8,128)S(1)} %pad_maximum_fusion), kind=kLoop, calls=%fused_computation.546 | loop fusion | bytes 155648 | tf_op jit(solution)/shard_map/slice | solution.py:45
  124.0 3.5 %copy.50 = f32[19,4,128,1]{2,0,3,1:T(8,128)S(1)} copy(f32[19,4,128,1]{3,2,1,0:T(8,128)} %get-tuple-element.42) | data formatting | bytes 77824 | tf_op jit(solution)/shard_map/slice | solution.py:45
  127.6 3.3 %copy.48 = f32[19,4,128,1]{2,1,3,0:T(4,128)S(1)} copy(f32[19,4,128,1]{3,2,1,0:T(8,128)} %get-tuple-element.43) | data formatting | bytes 77824 | tf_op jit(solution)/shard_map/slice | solution.py:44
  131.0 1.7 %collective-permute-start.7 = (f32[19,4,128,1]{2,0,3,1:T(8,128)S(1)}, f32[19,4,128,1]{2,0,3,1:T(8,128)S(1)}, u32[]{:S(2)}, u32[]{:S(2)}) collective-permute-start(f32[19,4,128,1]{2,0,3,1:T(8,128)S(1)} %copy.50), channel_id=1, source_target_pairs={{1,0},{2,1},{3,2},{0,3},{5,4},{6,5},{7,6},{4,7},{9,8},{10,9},{11,1... | collective-permute-start | bytes 116744 | tf_op jit(solution)/shard_map/ppermute | solution.py:47
  132.7 1.5 maximum_dynamic-update-slice_fusion.7
  134.2 1.6 maximum_dynamic-update-slice_fusion.6
  135.8 0.7 fusion.194
  136.4 0.7 fusion.195
  137.1 3.0 %copy.51 = f32[19,4,128,1]{3,2,1,0:T(8,128)} copy(f32[19,4,128,1]{2,0,3,1:T(8,128)S(1)} %collective-permute-done.7) | data formatting | bytes 77824 | tf_op jit(solution)/shard_map/ppermute | solution.py:47
  140.1 3.1 %copy.49 = f32[19,4,128,1]{3,2,1,0:T(8,128)} copy(f32[19,4,128,1]{2,1,3,0:T(4,128)S(1)} %collective-permute-done.6) | data formatting | bytes 77824 | tf_op jit(solution)/shard_map/ppermute | solution.py:46
  143.3 1.8 %maximum_dynamic-update-slice_fusion.5 = f32[19,2,128,128]{3,2,1,0:T(8,128)} fusion(f32[19,2,128,128]{3,2,1,0:T(8,128)} %fusion.195, f32[19,4,128,1]{3,2,1,0:T(8,128)} %copy.49, f32[19,1,128,128]{3,2,1,0:T(8,128)} %collective-permute-done.5, f32[19,2,128,128]{3,2,1,0:T(8,128)S(1)} %fusion.163, f32[19,1,128,128]{3,2,1,0:T(8,128)} %collective-permute-done.4), kind=kLoop, calls=%fused_computation.290 | loop fusion | flops 98304 | bytes 10092544
  145.1 0.7 copy-done
  145.8 2.0 %fusion.191 = (f32[2,128,128]{2,1,0:T(8,128)S(1)}, f32[2,128,128]{2,1,0:T(8,128)S(1)}, f32[19,2,128,128]{3,2,1,0:T(8,128)}, f32[2,128,128]{2,1,0:T(8,128)S(1)}, f32[2,128,128]{2,1,0:T(8,128)S(1)}) fusion(f32[19,1,128,128]{3,2,1,0:T(8,128)} %collective-permute-done.5, f32[19,2,128,128]{3,2,1,0:T(8,128)S(1)} %fusion.163, ...), kind=kLoop, calls=%fused_computation.284 | loop fusion | flops 229376 | bytes 5675008 | tf_op jit(solution)/shard_map/squeeze | solution.py:188
  147.8 0.7 fusion.196
  148.5 0.7 fusion.197
  149.1 0.7 fusion.198
  149.8 0.7 fusion.199
  150.5 1.6 %maximum_dynamic-update-slice_fusion.3 = f32[19,2,128,128]{3,2,1,0:T(8,128)} fusion(f32[19,2,128,128]{3,2,1,0:T(8,128)} %fusion.199, f32[19,4,128,1]{3,2,1,0:T(8,128)S(1)} %bitcast.371, f32[19,1,128,128]{3,2,1,0:T(8,128)} %collective-permute-done.5, f32[19,2,128,128]{3,2,1,0:T(8,128)S(1)} %fusion.163, f32[19,1,128,128]{3,2,1,0:T(8,128)} %collective-permute-done.4), kind=kLoop, calls=%fused_computation.282 | loop fusion | flops 98304 | bytes 5150720
  152.1 1.6 %maximum_dynamic-update-slice_fusion.2 = f32[19,2,128,128]{3,2,1,0:T(8,128)} fusion(f32[19,2,128,128]{3,2,1,0:T(8,128)} %maximum_dynamic-update-slice_fusion.3, f32[19,4,128,1]{3,2,1,0:T(8,128)S(1)} %copy-done, f32[19,1,128,128]{3,2,1,0:T(8,128)} %collective-permute-done.5, f32[19,2,128,128]{3,2,1,0:T(8,128)S(1)} %fusion.163, ...), kind=kLoop, calls=%fused_computation.281 | loop fusion | flops 98304 | bytes 5150720
  153.8 1.8 %fusion.190 = (f32[2,128,128]{2,1,0:T(8,128)S(1)}, f32[2,128,128]{2,1,0:T(8,128)S(1)}, f32[19,2,128,128]{3,2,1,0:T(8,128)}) fusion(f32[19,4,128,1]{3,2,1,0:T(8,128)S(1)} %copy-done, f32[19,1,128,128]{3,2,1,0:T(8,128)} %collective-permute-done.5, f32[19,2,128,128]{3,2,1,0:T(8,128)S(1)} %fusion.163, f32[19,1,128,128]{3,2,1,0:T(8,128)} %collective-permute-done.4, ...), kind=kLoop, calls=%fused_computation.274 | loop fusion | flops 294912 | bytes 5412864 | tf_op jit(solution)/shard_map/squeeze | solution.py:188
  155.5 1.6 %fusion.189 = (f32[2,128,128]{2,1,0:T(8,128)S(1)}, f32[2,128,128]{2,1,0:T(8,128)S(1)}, f32[19,2,128,128]{3,2,1,0:T(8,128)}) fusion(f32[19,4,128,1]{3,2,1,0:T(8,128)S(1)} %bitcast.371, f32[19,1,128,128]{3,2,1,0:T(8,128)} %collective-permute-done.5, f32[19,2,128,128]{3,2,1,0:T(8,128)S(1)} %fusion.163, f32[19,1,128,128]{3,2,1,0:T(8,128)} %collective-permute-done.4, ...), kind=kLoop, calls=%fused_computation.270 | loop fusion | flops 294912 | bytes 5412864 | tf_op jit(solution)/shard_map/squeeze | solution.py:188
  157.2 0.7 fusion.200
  157.9 0.7 fusion.201
  158.6 0.7 fusion.202
  159.2 0.7 fusion.203
  (129 shorter events, 10.8 us)
Async XLA Ops:
  0.6 21.9 %copy-start.3 = (f32[6,2,128,128]{3,2,1,0:T(8,128)S(1)}, f32[6,2,128,128]{3,2,1,0:T(8,128)}, u32[]{:S(2)}) copy-start(f32[6,2,128,128]{3,2,1,0:T(8,128)} %param.3) | copy-start | bytes 2359300
  1.9 19.8 %collective-permute-start = (f32[6,1,128,128]{3,2,1,0:T(8,128)S(1)}, f32[6,1,128,128]{3,2,1,0:T(8,128)S(1)}, u32[]{:S(2)}, u32[]{:S(2)}) collective-permute-start(f32[6,1,128,128]{3,2,1,0:T(8,128)S(1)} %get-tuple-element.77), channel_id=1, source_target_pairs={{0,4},{4,8},{8,12},{12,16},{16,20},{20,24},{24,28},{28,0},{1,5},{5... | collective-permute-start | bytes 1179656 | tf_op jit(solution)/shard_map/ppermute | solution.py:46
  4.9 19.0 %collective-permute-start.1 = (f32[6,1,128,128]{3,2,1,0:T(8,128)S(1)}, f32[6,1,128,128]{3,2,1,0:T(8,128)S(1)}, u32[]{:S(2)}, u32[]{:S(2)}) collective-permute-start(f32[6,1,128,128]{3,2,1,0:T(8,128)S(1)} %get-tuple-element.76), channel_id=1, source_target_pairs={{4,0},{8,4},{12,8},{16,12},{20,16},{24,20},{28,24},{0,28},{5,1},{9... | collective-permute-start | bytes 1179656 | tf_op jit(solution)/shard_map/ppermute | solution.py:47
  21.7 0.8 copy-start.11
  23.9 0.7 copy-start.13
  24.7 2.2 %copy-start.5 = (f32[6,4,128,128]{3,2,1,0:T(8,128)}, f32[6,4,128,128]{3,2,1,0:T(8,128)S(1)}, u32[]{:S(2)}) copy-start(f32[6,4,128,128]{3,2,1,0:T(8,128)S(1)} %constant_dynamic-update-slice_fusion) | copy-start | bytes 4718596
  26.9 4.5 %copy-start.1 = (f32[19,2,128,128]{3,2,1,0:T(8,128)S(1)}, f32[19,2,128,128]{3,2,1,0:T(8,128)}, u32[]{:S(2)}) copy-start(f32[19,2,128,128]{3,2,1,0:T(8,128)} %param.2) | copy-start | bytes 7471108
  30.8 5.0 %collective-permute-start.3 = (f32[6,4,128,1]{2,1,3,0:T(4,128)S(1)}, f32[6,4,128,1]{2,1,3,0:T(4,128)S(1)}, u32[]{:S(2)}, u32[]{:S(2)}) collective-permute-start(f32[6,4,128,1]{2,1,3,0:T(4,128)S(1)} %copy.45), channel_id=1, source_target_pairs={{1,0},{2,1},{3,2},{0,3},{5,4},{6,5},{7,6},{4,7},{9,8},{10,9},{11,1... | collective-permute-start | bytes 36872 | tf_op jit(solution)/shard_map/ppermute | solution.py:47
  30.9 3.3 %collective-permute-start.2 = (f32[6,4,128,1]{2,1,3,0:T(4,128)S(1)}, f32[6,4,128,1]{2,1,3,0:T(4,128)S(1)}, u32[]{:S(2)}, u32[]{:S(2)}) collective-permute-start(f32[6,4,128,1]{2,1,3,0:T(4,128)S(1)} %copy.44), channel_id=1, source_target_pairs={{0,1},{1,2},{2,3},{3,0},{4,5},{5,6},{6,7},{7,4},{8,9},{9,10},{10,1... | collective-permute-start | bytes 36872 | tf_op jit(solution)/shard_map/ppermute | solution.py:46
  45.4 1.7 %copy-start.2 = (f32[19,2,128,128]{3,2,1,0:T(8,128)S(1)}, f32[19,2,128,128]{3,2,1,0:T(8,128)}, u32[]{:S(2)}) copy-start(f32[19,2,128,128]{3,2,1,0:T(8,128)} %param.2) | copy-start | bytes 7471108
  47.8 11.2 %copy-start.15 = (f32[2,128,128]{2,1,0:T(8,128)}, f32[2,128,128]{2,1,0:T(8,128)S(1)}, u32[]{:S(2)}) copy-start(f32[2,128,128]{2,1,0:T(8,128)S(1)} %get-tuple-element.86) | copy-start | bytes 393220
  49.2 15.6 %collective-permute-start.9 = (f32[3,1,128,128]{3,2,1,0:T(8,128)S(1)}, f32[3,1,128,128]{3,2,1,0:T(8,128)S(1)}, u32[]{:S(2)}, u32[]{:S(2)}) collective-permute-start(f32[3,1,128,128]{3,2,1,0:T(8,128)S(1)} %get-tuple-element.96), channel_id=1, source_target_pairs={{0,4},{4,8},{8,12},{12,16},{16,20},{20,24},{24,28},{28,0},{1,5},{5... | collective-permute-start | bytes 589832 | tf_op jit(solution)/shard_map/ppermute | solution.py:46
  50.4 14.4 %collective-permute-start.8 = (f32[3,1,128,128]{3,2,1,0:T(8,128)S(1)}, f32[3,1,128,128]{3,2,1,0:T(8,128)S(1)}, u32[]{:S(2)}, u32[]{:S(2)}) collective-permute-start(f32[3,1,128,128]{3,2,1,0:T(8,128)S(1)} %get-tuple-element.97), channel_id=1, source_target_pairs={{4,0},{8,4},{12,8},{16,12},{20,16},{24,20},{28,24},{0,28},{5,1},{9... | collective-permute-start | bytes 589832 | tf_op jit(solution)/shard_map/ppermute | solution.py:47
  61.2 54.9 %collective-permute-start.5 = (f32[19,1,128,128]{3,2,1,0:T(8,128)}, f32[19,1,128,128]{3,2,1,0:T(8,128)}, u32[]{:S(2)}, u32[]{:S(2)}) collective-permute-start(f32[19,1,128,128]{3,2,1,0:T(8,128)} %get-tuple-element.65), channel_id=1, source_target_pairs={{4,0},{8,4},{12,8},{16,12},{20,16},{24,20},{28,24},{0,28},{5,1},{9... | collective-permute-start | bytes 3735560 | tf_op jit(solution)/shard_map/ppermute | solution.py:47
  62.8 53.4 %collective-permute-start.4 = (f32[19,1,128,128]{3,2,1,0:T(8,128)}, f32[19,1,128,128]{3,2,1,0:T(8,128)}, u32[]{:S(2)}, u32[]{:S(2)}) collective-permute-start(f32[19,1,128,128]{3,2,1,0:T(8,128)} %get-tuple-element.66), channel_id=1, source_target_pairs={{0,4},{4,8},{8,12},{12,16},{16,20},{20,24},{24,28},{28,0},{1,5},{5... | collective-permute-start | bytes 3735560 | tf_op jit(solution)/shard_map/ppermute | solution.py:46
  64.8 2.9 %copy-start.10 = (f32[3,1,128,128]{3,2,1,0:T(8,128)}, f32[3,1,128,128]{3,2,1,0:T(8,128)S(1)}, u32[]{:S(2)}) copy-start(f32[3,1,128,128]{3,2,1,0:T(8,128)S(1)} %collective-permute-done.8) | copy-start | bytes 589828
  69.2 4.8 %collective-permute-start.11 = (f32[3,4,128,1]{2,1,3,0:T(4,128)S(1)}, f32[3,4,128,1]{2,1,3,0:T(4,128)S(1)}, u32[]{:S(2)}, u32[]{:S(2)}) collective-permute-start(f32[3,4,128,1]{2,1,3,0:T(4,128)S(1)} %copy.56), channel_id=1, source_target_pairs={{0,1},{1,2},{2,3},{3,0},{4,5},{5,6},{6,7},{7,4},{8,9},{9,10},{10,1... | collective-permute-start | bytes 18440 | tf_op jit(solution)/shard_map/ppermute | solution.py:46
  69.2 3.5 %collective-permute-start.10 = (f32[3,4,128,1]{2,1,3,0:T(4,128)S(1)}, f32[3,4,128,1]{2,1,3,0:T(4,128)S(1)}, u32[]{:S(2)}, u32[]{:S(2)}) collective-permute-start(f32[3,4,128,1]{2,1,3,0:T(4,128)S(1)} %copy.54), channel_id=1, source_target_pairs={{1,0},{2,1},{3,2},{0,3},{5,4},{6,5},{7,6},{4,7},{9,8},{10,9},{11,1... | collective-permute-start | bytes 18440 | tf_op jit(solution)/shard_map/ppermute | solution.py:47
  75.2 1.6 copy-start.4
  75.2 1.6 %copy-start.9 = (f32[3,2,128,128]{3,2,1,0:T(8,128)S(1)}, f32[3,2,128,128]{3,2,1,0:T(8,128)}, u32[]{:S(2)}) copy-start(f32[3,2,128,128]{3,2,1,0:T(8,128)} %get-tuple-element.93) | copy-start | bytes 1179652
  77.0 1.0 copy-start.14
  77.0 1.0 copy-start.19
  77.1 1.5 copy-start.6
  77.1 2.0 %copy-start.7 = (f32[6,4,128,1]{3,2,1,0:T(8,128)S(1)}, f32[6,4,128,1]{3,2,1,0:T(8,128)}, u32[]{:S(2)}) copy-start(f32[6,4,128,1]{3,2,1,0:T(8,128)} %copy.46) | copy-start | bytes 36868
  77.1 2.5 %copy-start.8 = (f32[6,4,128,1]{3,2,1,0:T(8,128)S(1)}, f32[6,4,128,1]{3,2,1,0:T(8,128)}, u32[]{:S(2)}) copy-start(f32[6,4,128,1]{3,2,1,0:T(8,128)} %copy.47) | copy-start | bytes 36868
  77.1 2.5 %copy-start.12 = (f32[6,1,128,128]{3,2,1,0:T(8,128)S(1)}, f32[6,1,128,128]{3,2,1,0:T(8,128)}, u32[]{:S(2)}) copy-start(f32[6,1,128,128]{3,2,1,0:T(8,128)} %copy-done.11) | copy-start | bytes 1179652
  77.1 2.5 %copy-start.17 = (f32[2,128,128]{2,1,0:T(8,128)S(1)}, f32[2,128,128]{2,1,0:T(8,128)}, u32[]{:S(2)}) copy-start(f32[2,128,128]{2,1,0:T(8,128)} %get-tuple-element.10) | copy-start | bytes 393220
  77.1 2.5 %copy-start.18 = (f32[2,128,128]{2,1,0:T(8,128)S(1)}, f32[2,128,128]{2,1,0:T(8,128)}, u32[]{:S(2)}) copy-start(f32[2,128,128]{2,1,0:T(8,128)} %get-tuple-element.7) | copy-start | bytes 393220
  130.9 9.2 %collective-permute-start.6 = (f32[19,4,128,1]{2,1,3,0:T(4,128)S(1)}, f32[19,4,128,1]{2,1,3,0:T(4,128)S(1)}, u32[]{:S(2)}, u32[]{:S(2)}) collective-permute-start(f32[19,4,128,1]{2,1,3,0:T(4,128)S(1)} %copy.48), channel_id=1, source_target_pairs={{0,1},{1,2},{2,3},{3,0},{4,5},{5,6},{6,7},{7,4},{8,9},{9,10},{10,1... | collective-permute-start | bytes 116744 | tf_op jit(solution)/shard_map/ppermute | solution.py:46
  131.0 6.1 %collective-permute-start.7 = (f32[19,4,128,1]{2,0,3,1:T(8,128)S(1)}, f32[19,4,128,1]{2,0,3,1:T(8,128)S(1)}, u32[]{:S(2)}, u32[]{:S(2)}) collective-permute-start(f32[19,4,128,1]{2,0,3,1:T(8,128)S(1)} %copy.50), channel_id=1, source_target_pairs={{1,0},{2,1},{3,2},{0,3},{5,4},{6,5},{7,6},{4,7},{9,8},{10,9},{11,1... | collective-permute-start | bytes 116744 | tf_op jit(solution)/shard_map/ppermute | solution.py:47
  134.2 1.6 copy-start.16
  134.2 1.6 copy-start.21
  134.2 2.2 %copy-start.20 = (f32[2,127,128]{2,1,0:T(8,128)S(1)}, f32[2,127,128]{2,1,0:T(8,128)}, u32[]{:S(2)}) copy-start(f32[2,127,128]{2,1,0:T(8,128)} %slice.674) | copy-start | bytes 390148
  134.2 2.2 %copy-start.22 = (f32[2,1,128]{2,1,0:T(1,128)S(1)}, f32[2,1,128]{2,1,0:T(1,128)}, u32[]{:S(2)}) copy-start(f32[2,1,128]{2,1,0:T(1,128)} %slice.675) | copy-start | bytes 3076
  143.3 2.5 %copy-start = (f32[19,4,128,1]{3,2,1,0:T(8,128)S(1)}, f32[19,4,128,1]{3,2,1,0:T(8,128)}, u32[]{:S(2)}) copy-start(f32[19,4,128,1]{3,2,1,0:T(8,128)} %copy.51) | copy-start | bytes 116740
  143.3 7.2 %slice-start = ((s8[4980736]{0:T(1024)(128)(4,1)}), s8[4194304]{0:T(1024)(128)(4,1)S(1)}, s32[]{:S(2)}) async-start(s8[4980736]{0:T(1024)(128)(4,1)} %bitcast.370), calls=%async_computation | async-start | bytes 8388608
  145.8 4.7 %slice-start.1 = ((s8[4980736]{0:T(1024)(128)(4,1)}), s8[786432]{0:T(1024)(128)(4,1)S(1)}, s32[]{:S(2)}) async-start(s8[4980736]{0:T(1024)(128)(4,1)} %bitcast.370), calls=%async_computation.1 | async-start | bytes 1572864
  155.5 1.7 %copy-start.23 = (f32[2,1,128]{2,1,0:T(1,128)S(1)}, f32[2,1,128]{2,1,0:T(1,128)}, u32[]{:S(2)}) copy-start(f32[2,1,128]{2,1,0:T(1,128)} %multiply_add_fusion.13) | copy-start | bytes 3076
  155.5 2.4 %copy-start.24 = (f32[2,1,128]{2,1,0:T(1,128)S(1)}, f32[2,1,128]{2,1,0:T(1,128)}, u32[]{:S(2)}) copy-start(f32[2,1,128]{2,1,0:T(1,128)} %multiply_add_fusion.12) | copy-start | bytes 3076
where the time goes:
time: 161 us; the launch traced here: 160 us
  waiting for transfers between devices  52.4 us (33%)
  local copies, waits for them, and re-layouts  47.3 us (29%)
  other arithmetic  42 us (26%)
  starting transfers between devices  17 us (11%)
    ppermute x6, waiting for transfers between devices, padded_2(): after = lax.ppermute(initial, axis, down)  36 us
    unnamed x45, other arithmetic  18.2 us
    slice x7, local copies, waits for them, and re-layouts, padded_2(): initial = lax.slice_in_dim(shard, 0, width, axis=dim)  16.8 us
    ppermute x6, waiting for transfers between devices, padded_2(): before = lax.ppermute(last, axis, up)  16.3 us
    ppermute x6, starting transfers between devices, padded_2(): after = lax.ppermute(initial, axis, down)  11.7 us
    slice x5, local copies, waits for them, and re-layouts, padded_2(): last = lax.slice_in_dim(shard, length - width, length, axis=dim)  9 us
    unnamed x57, local copies, waits for them, and re-layouts  7.45 us
    ppermute x3, local copies, waits for them, and re-layouts, padded_2(): before = lax.ppermute(last, axis, up)  6.03 us
  transfers between devices with their start and end apart: 12, of which 4 were waited for; matrix products, arithmetic and copies ran while one was open for 19% of the time, Pallas kernels for 0%

commit v1 on v0

v1 whole, which is shorter than its diff:
```python
import functools

import jax
import jax.numpy as jnp
from jax import lax
from jax.experimental import pallas as pl
from jax.experimental.pallas import tpu as pltpu
from jax.sharding import PartitionSpec as P

VELOCITIES = (
    (0, 0, 0),
    (1, 0, 0),
    (-1, 0, 0),
    (0, 1, 0),
    (0, -1, 0),
    (0, 0, 1),
    (0, 0, -1),
    (1, 1, 0),
    (-1, -1, 0),
    (1, -1, 0),
    (-1, 1, 0),
    (1, 0, 1),
    (-1, 0, -1),
    (1, 0, -1),
    (-1, 0, 1),
    (0, 1, 1),
    (0, -1, -1),
    (0, 1, -1),
    (0, -1, 1),
)
LATTICE_WEIGHTS = (1.0 / 3.0,) + (1.0 / 18.0,) * 6 + (1.0 / 36.0,) * 12
OPPOSITE = (0, 2, 1, 4, 3, 6, 5, 8, 7, 10, 9, 12, 11, 14, 13, 16, 15, 18, 17)
SYMMETRIC_INDEX = ((0, 3, 4), (3, 1, 5), (4, 5, 2))
COMPONENT_PAIRS = ((0, 0), (1, 1), (2, 2), (0, 1), (0, 2), (1, 2))
SOLVENT_TIME = 0.8
RELAX_TIME = 20.0
POLYMER_VISC = 1.0
EXTENSION_SQ = 100.0
DIFFUSIVITY = 0.05
DRIVE_FORCE = 1e-05
STRESS_SCALE = POLYMER_VISC / RELAX_TIME

SLOT_SHIFTS = ((0, 0), (1, 0), (-1, 0), (0, 1), (0, -1))
PLUS = tuple(VELOCITIES.index((1, cy, cz)) for cy, cz in SLOT_SHIFTS)
MINUS = tuple(VELOCITIES.index((-1, cy, cz)) for cy, cz in SLOT_SHIFTS)
Z_UP = tuple(VELOCITIES.index(v) for v in ((0, 0, 1), (0, 1, 1), (0, -1, 1), (1, 0, 1), (-1, 0, 1)))
Z_DOWN = tuple(
    VELOCITIES.index(v) for v in ((0, 0, -1), (0, 1, -1), (0, -1, -1), (1, 0, -1), (-1, 0, -1))
)
ROWS = 8
F32 = jnp.float32
VMEM = pltpu.VMEM


def vmem_spec():
    return pl.BlockSpec(memory_space=pltpu.VMEM)


def any_spec():
    return pl.BlockSpec(memory_space=pl.ANY)


def params():
    return pltpu.CompilerParams(vmem_limit_bytes=48 << 20)


def lanes_of(like):
    return lax.broadcasted_iota(jnp.int32, like.shape, 1)


def rolled(value, shift, axis=1):
    shift = shift % value.shape[axis]
    return value if shift == 0 else pltpu.roll(value, shift, axis)


def pack_columns(values, source, packed=None, base=0):
    lane = lanes_of(values[0])
    if packed is None:
        packed = jnp.zeros_like(values[0])
    for number, value in enumerate(values, base):
        packed = jnp.where(lane == number, rolled(value, number - source), packed)
    return packed


def for_rows(total, body):
    def step(number, carry):
        body(pl.multiple_of(number * ROWS, ROWS))
        return carry

    lax.fori_loop(0, total // ROWS, step, 0)


def peterlin_of(c_xx, c_yy, c_zz):
    return (EXTENSION_SQ - 3.0) / (EXTENSION_SQ - (c_xx + c_yy + c_zz))


def edge_kernel(far_ref, conf_ref, up_ref, down_ref, far_out):
    height, width = conf_ref.shape[2:]
    far = far_ref[0]

    def rows(start):
        at = pl.ds(start, ROWS)
        values = [conf_ref[f, p, at, :] for p in range(2) for f in range(6)]
        up_ref[at, :] = pack_columns(values, width - 1)
        down_ref[at, :] = pack_columns(values, 0)
        for f in range(6):
            far_out[f, at, :] = conf_ref[f, far, at, :]

    for_rows(height, rows)


def edges(far, conform):
    height, width = conform.shape[2:]
    tile = jax.ShapeDtypeStruct((height, width), F32)
    return pl.pallas_call(
        edge_kernel,
        out_shape=(tile, tile, jax.ShapeDtypeStruct((6, height, width), F32)),
        in_specs=[pl.BlockSpec(memory_space=pltpu.SMEM), vmem_spec()],
        out_specs=(vmem_spec(), vmem_spec(), vmem_spec()),
        compiler_params=params(),
        name="edges",
    )(far, conform)


def prepare_kernel(conf_ref, popul_ref, low_ref, high_ref, pre_ref, tall):
    height, width = conf_ref.shape[2:]

    def stress(fields, at_of):
        trace_parts = [at_of(f) for f in range(3)]
        peterlin = STRESS_SCALE * peterlin_of(*trace_parts)
        out = {}
        for f in fields:
            value = trace_parts[f] if f < 3 else at_of(f)
            out[f] = peterlin * value - (STRESS_SCALE if f < 3 else 0.0)
        return out

    for p in range(2):
        sign = 2 * p - 1

        def first(start, p=p, sign=sign):
            at = pl.ds(start, ROWS)
            own = stress(range(6), lambda f: conf_ref[f, p, at, :])
            other = stress((0, 3, 4), lambda f: conf_ref[f, 1 - p, at, :])
            low_pack = low_ref[at, :]
            high_pack = high_ref[at, :]
            low = stress((2, 4, 5), lambda f: rolled(low_pack, -(6 * p + f)))
            high = stress((2, 4, 5), lambda f: rolled(high_pack, width - 1 - (6 * p + f)))
            lane = lanes_of(low_pack)
            for number, f in enumerate((3, 1, 5)):
                tall[number, p, pl.ds(start + 8, ROWS), :] = own[f]
            for number in range(3):
                across = SYMMETRIC_INDEX[number][2]
                below = jnp.where(lane == 0, low[across], rolled(own[across], 1))
                above = jnp.where(lane == width - 1, high[across], rolled(own[across], -1))
                term = 0.5 * (above - below) - (0.5 * sign) * other[SYMMETRIC_INDEX[number][0]]
                if number == 0:
                    term = term + DRIVE_FORCE
                pre_ref[number, p, at, :] = term
            values = [popul_ref[i, p, at, :] for i in range(19)]
            density = values[0]
            for i in range(1, 19):
                density = density + values[i]
            pre_ref[3, p, at, :] = density
            for axis in range(3):
                moment = None
                for i in range(19):
                    if VELOCITIES[i][axis] == 1:
                        moment = values[i] if moment is None else moment + values[i]
                for i in range(19):
                    if VELOCITIES[i][axis] == -1:
                        moment = moment - values[i]
                pre_ref[4 + axis, p, at, :] = moment

        for_rows(height, first)
        for number in range(3):
            tall[number, p, 7:8, :] = tall[number, p, 8:9, :]
            tall[number, p, height + 8 : height + 9, :] = tall[number, p, height + 7 : height + 8, :]

        def second(start, p=p):
            at = pl.ds(start, ROWS)
            for number in range(3):
                above = tall[number, p, pl.ds(start + 9, ROWS), :]
                below = tall[number, p, pl.ds(start + 7, ROWS), :]
                pre_ref[number, p, at, :] = pre_ref[number, p, at, :] + 0.5 * (above - below)

        for_rows(height, second)


def prepare(conform, popul, low, high):
    height, width = conform.shape[2:]
    return pl.pallas_call(
        prepare_kernel,
        out_shape=jax.ShapeDtypeStruct((7, 2, height, width), F32),
        in_specs=[vmem_spec()] * 4,
        out_specs=vmem_spec(),
        scratch_shapes=[VMEM((3, 2, height + 16, width), F32)],
        compiler_params=params(),
        name="prepare",
    )(conform, popul, low, high)


def collide_kernel(second, plane_ref, popul_ref, pre_ref, halo_ref, *refs):
    if second:
        _, up_in, down_in, post_ref, message_ref, up_ref, down_ref = refs
    else:
        post_ref, message_ref, up_ref, down_ref = refs
    height, width = halo_ref.shape[1:]
    plane = plane_ref[0]
    outward_plus = plane == 1
    half_sign = jnp.where(outward_plus, 0.5, -0.5).astype(F32)
    factor = 1.0 - 0.5 / SOLVENT_TIME
    keep = 1.0 - 1.0 / SOLVENT_TIME
    base = 8 if second else 0

    def rows(start):
        at = pl.ds(start, ROWS)
        halo = [halo_ref[f, at, :] for f in range(5)]
        peterlin = STRESS_SCALE * peterlin_of(halo[0], halo[1], halo[2])
        stress = (peterlin * halo[0] - STRESS_SCALE, peterlin * halo[3], peterlin * halo[4])
        force = [pre_ref[a, 0, at, :] + half_sign * stress[a] for a in range(3)]
        density = pre_ref[3, 0, at, :]
        inverse = 1.0 / density
        velocity = [(pre_ref[4 + a, 0, at, :] + 0.5 * force[a]) * inverse for a in range(3)]
        speed_sq = (
            velocity[0] * velocity[0] + velocity[1] * velocity[1] + velocity[2] * velocity[2]
        )
        push = velocity[0] * force[0] + velocity[1] * force[1] + velocity[2] * force[2]
        rate = density * (1.0 / SOLVENT_TIME)
        common = rate * (1.0 - 1.5 * speed_sq) - (3.0 * factor) * push
        flow = [rate * velocity[a] for a in range(3)]
        drag = [factor * force[a] for a in range(3)]
        post = [None] * 19
        post[0] = keep * popul_ref[0, 0, at, :] + LATTICE_WEIGHTS[0] * common

        def along(vec, parts):
            total = None
            for axis in range(3):
                if vec[axis] == 1:
                    total = parts[axis] if total is None else total + parts[axis]
                elif vec[axis] == -1:
                    total = total - parts[axis]
            return total

        for i in range(1, 19, 2):
            vec = VELOCITIES[i]
            weight = LATTICE_WEIGHTS[i]
            c_u = along(vec, velocity)
            c_flow = along(vec, flow)
            c_drag = along(vec, drag)
            total = c_flow + c_drag
            even = weight * common + (4.5 * weight) * (c_u * (total + c_drag))
            odd = (3.0 * weight) * total
            post[i] = keep * popul_ref[i, 0, at, :] + (even + odd)
            post[i + 1] = keep * popul_ref[i + 1, 0, at, :] + (even - odd)
        for i in range(19):
            post_ref[i, 0, at, :] = post[i]
        for a in range(3):
            message_ref[a, at, :] = velocity[a]
        for slot in range(5):
            message_ref[3 + slot, at, :] = jnp.where(
                outward_plus, post[PLUS[slot]], post[MINUS[slot]]
            )
        up = up_in[at, :] if second else None
        down = down_in[at, :] if second else None
        up_ref[at, :] = pack_columns(
            velocity + [post[i] for i in Z_UP], width - 1, up, base
        )
        down_ref[at, :] = pack_columns(velocity + [post[i] for i in Z_DOWN], 0, down, base)

    for_rows(height, rows)


def collide(plane, popul, pre, halo, earlier=None):
    height, width = popul.shape[2:]
    block = min(32, height)
    second = earlier is not None
    tile = jax.ShapeDtypeStruct((height, width), F32)
    tile_spec = pl.BlockSpec((block, width), lambda g, s: (g, 0))

    def plane_spec(count):
        return pl.BlockSpec((count, 1, block, width), lambda g, s: (0, s[0], g, 0))

    in_specs = [
        plane_spec(19),
        plane_spec(7),
        pl.BlockSpec((6, block, width), lambda g, s: (0, g, 0)),
    ]
    operands = [plane, popul, pre, halo]
    aliases = {}
    if second:
        in_specs += [any_spec(), tile_spec, tile_spec]
        operands += list(earlier)
        aliases = {4: 0}
    return pl.pallas_call(
        functools.partial(collide_kernel, second),
        grid_spec=pltpu.PrefetchScalarGridSpec(
            num_scalar_prefetch=1,
            grid=(height // block,),
            in_specs=in_specs,
            out_specs=(
                plane_spec(19),
                pl.BlockSpec((8, block, width), lambda g, s: (0, g, 0)),
                tile_spec,
                tile_spec,
            ),
        ),
        out_shape=(
            jax.ShapeDtypeStruct(popul.shape, F32),
            jax.ShapeDtypeStruct((8, height, width), F32),
            tile,
            tile,
        ),
        input_output_aliases=aliases,
        compiler_params=params(),
        name="collide_odd" if second else "collide_even",
    )(*operands)


def corner_kernel(low_ref, high_ref, even_ref, odd_ref):
    low = low_ref[...].T
    high = high_ref[...].T
    even_ref[0:8, :] = low[0:8]
    even_ref[8:16, :] = high[0:8]
    odd_ref[0:8, :] = low[8:16]
    odd_ref[8:16, :] = high[8:16]


def corners(low, high):
    height = low.shape[0]
    out = jax.ShapeDtypeStruct((16, height), F32)
    return pl.pallas_call(
        corner_kernel,
        out_shape=(out, out),
        in_specs=[vmem_spec()] * 2,
        out_specs=(vmem_spec(), vmem_spec()),
        compiler_params=params(),
        name="corners",
    )(low, high)


def inner_kernel(
    planes_ref,
    conf_ref,
    halo_e,
    halo_o,
    conf_low,
    conf_high,
    low_ref,
    high_ref,
    post_ref,
    velo_e,
    velo_o,
    read_ref,
    part_ref,
    conf_tall,
    velo_tall,
    halo,
):
    height, width = conf_ref.shape[2:]
    planes = (planes_ref[0], planes_ref[1])
    for face, (velo, half) in enumerate(((velo_e, halo_e), (velo_o, halo_o))):
        p = planes[face]
        for a in range(3):
            velo_tall[a, p, 8 : 8 + height, :] = velo[a]
            velo_tall[a, p, 7:8, :] = -velo[a, 0:1, :]
            velo_tall[a, p, height + 8 : height + 9, :] = -velo[a, height - 1 : height, :]
        for f in range(6):
            halo[p, f] = half[f]
    for p in range(2):
        for f in range(6):
            conf_tall[f, p, 8 : 8 + height, :] = conf_ref[f, p]
            conf_tall[f, p, 7:8, :] = conf_ref[f, p, 0:1, :]
            conf_tall[f, p, height + 8 : height + 9, :] = conf_ref[f, p, height - 1 : height, :]

    even_first = planes[0] == 0

    def lane_of(p, field):
        return (field, 8 + field) if p == 0 else (8 + field, field)

    def edge_value(pack, p, field, target):
        when_first, otherwise = lane_of(p, field)
        return jnp.where(
            even_first, rolled(pack, target - when_first), rolled(pack, target - otherwise)
        )

    for p in range(2):
        sign = 2 * p - 1

        def rows(start, p=p, sign=sign):
            at = pl.ds(start, ROWS)
            upper = pl.ds(start + 9, ROWS)
            lower = pl.ds(start + 7, ROWS)
            cl_pack = conf_low[at, :]
            ch_pack = conf_high[at, :]
            l_pack = low_ref[at, :]
            h_pack = high_ref[at, :]
            lane = lanes_of(cl_pack)
            first = lane == 0
            final = lane == width - 1
            velocity = [velo_tall[a, p, pl.ds(start + 8, ROWS), :] for a in range(3)]
            grad = [[None] * 3 for _ in range(3)]
            for a in range(3):
                grad[0][a] = (-0.5 * sign) * velo_tall[a, 1 - p, pl.ds(start + 8, ROWS), :]
                grad[1][a] = 0.5 * (velo_tall[a, p, upper, :] - velo_tall[a, p, lower, :])
                above = jnp.where(
                    final, edge_value(h_pack, p, a, width - 1), rolled(velocity[a], -1)
                )
                below = jnp.where(first, edge_value(l_pack, p, a, 0), rolled(velocity[a], 1))
                grad[2][a] = 0.5 * (above - below)
            own = [conf_ref[f, p, at, :] for f in range(6)]
            peterlin = (1.0 / RELAX_TIME) * peterlin_of(own[0], own[1], own[2])
            for f in range(6):
                i, j = COMPONENT_PAIRS[f]
                x_in = conf_ref[f, 1 - p, at, :]
                x_out = halo[p, f, at, :]
                y_up = conf_tall[f, p, upper, :]
                y_low = conf_tall[f, p, lower, :]
                lane_number = 6 * p + f
                z_up = jnp.where(
                    final, rolled(ch_pack, width - 1 - lane_number), rolled(own[f], -1)
                )
                z_low = jnp.where(first, rolled(cl_pack, -lane_number), rolled(own[f], 1))
                around = (x_in + x_out) + (y_up + y_low) + (z_up + z_low)
                advect = (
                    (sign * velocity[0]) * (x_out - x_in)
                    + velocity[1] * (y_up - y_low)
                    + velocity[2] * (z_up - z_low)
                )
                stretch = None
                for k in range(3):
                    term = own[SYMMETRIC_INDEX[i][k]] * grad[k][j]
                    if i != j:
                        term = term + grad[k][i] * own[SYMMETRIC_INDEX[k][j]]
                    stretch = term if stretch is None else stretch + term
                if i == j:
                    stretch = 2.0 * stretch
                relax = peterlin * own[f]
                if f < 3:
                    relax = relax - 1.0 / RELAX_TIME
                part_ref[f, p, at, :] = (
                    own[f]
                    - 0.5 * advect
                    + stretch
                    - relax
                    + DIFFUSIVITY * (around - 6.0 * own[f])
                )

        for_rows(height, rows)

    full_low = low_ref[...]
    full_high = high_ref[...]
    lane = lanes_of(full_low)
    for i in range(19):
        step_x, step_y, step_z = VELOCITIES[i]
        for p in range(2):
            q = p - step_x
            if q not in (0, 1):
                continue
            value = post_ref[i, q]
            if step_z == 1:
                edge = edge_value(full_low, q, 3 + Z_UP.index(i), 0)
                value = jnp.where(lane == 0, edge, rolled(value, 1))
            elif step_z == -1:
                edge = edge_value(full_high, q, 3 + Z_DOWN.index(i), width - 1)
                value = jnp.where(lane == width - 1, edge, rolled(value, -1))
            back = OPPOSITE[i]
            if step_y == 1:
                read_ref[i, p, 1:height, :] = value[: height - 1]
                read_ref[i, p, 0:1, :] = post_ref[back, p, 0:1, :]
            elif step_y == -1:
                read_ref[i, p, 0 : height - 1, :] = value[1:]
                read_ref[i, p, height - 1 : height, :] = post_ref[back, p, height - 1 : height, :]
            else:
                read_ref[i, p] = value


def inner(planes, conform, halo_e, halo_o, conf_low, conf_high, low, high, post, velo_e, velo_o):
    height, width = conform.shape[2:]
    velo_spec = pl.BlockSpec((3, height, width), lambda g: (0, 0, 0))
    whole = lambda shape: pl.BlockSpec(shape, lambda g: (0,) * len(shape))
    return pl.pallas_call(
        inner_kernel,
        grid=(1,),
        out_shape=(
            jax.ShapeDtypeStruct(post.shape, F32),
            jax.ShapeDtypeStruct(conform.shape, F32),
        ),
        in_specs=[
            pl.BlockSpec(memory_space=pltpu.SMEM),
            whole(conform.shape),
            whole(halo_e.shape),
            whole(halo_o.shape),
            whole(conf_low.shape),
            whole(conf_low.shape),
            whole(conf_low.shape),
            whole(conf_low.shape),
            whole(post.shape),
            velo_spec,
            velo_spec,
        ],
        out_specs=(whole(post.shape), whole(conform.shape)),
        scratch_shapes=[
            VMEM((6, 2, height + 16, width), F32),
            VMEM((3, 2, height + 16, width), F32),
            VMEM((2, 6, height, width), F32),
        ],
        compiler_params=params(),
        name="inner",
    )(planes, conform, halo_e, halo_o, conf_low, conf_high, low, high, post, velo_e, velo_o)


def finish_kernel(
    second,
    plane_ref,
    part_ref,
    conf_ref,
    got_ref,
    bottom_ref,
    top_ref,
    corner_ref,
    *refs,
):
    if second:
        _, _, read_ref, new_ref, read_tile, new_tile, sems = refs
    else:
        _, read_ref, new_ref, read_tile, new_tile, sems = refs
    height, width = got_ref.shape[1:]
    plane = plane_ref[0]
    half_sign = jnp.where(plane == 1, 0.5, -0.5).astype(F32)
    copies = []

    def send(slot):
        target = jnp.where(plane == 1, MINUS[slot], PLUS[slot])
        copy = pltpu.make_async_copy(
            read_tile.at[slot], read_ref.at[target, plane], sems.at[slot]
        )
        copy.start()
        copies.append(copy)

    lane = lax.broadcasted_iota(jnp.int32, (height, width), 1)
    low = jnp.broadcast_to(corner_ref[pl.ds(6 + plane, 1), :], (width, height)).T
    high = jnp.broadcast_to(corner_ref[pl.ds(14 + plane, 1), :], (width, height)).T
    read_tile[0] = got_ref[3]
    send(0)
    read_tile[1, 1:height, :] = got_ref[4, 0 : height - 1, :]
    read_tile[1, 0:1, :] = bottom_ref[0, 0:1, :]
    send(1)
    read_tile[2, 0 : height - 1, :] = got_ref[5, 1:height, :]
    read_tile[2, height - 1 : height, :] = top_ref[0, 7:8, :]
    send(2)
    read_tile[3] = jnp.where(lane == 0, low, rolled(got_ref[6], 1))
    send(3)
    read_tile[4] = jnp.where(lane == width - 1, high, rolled(got_ref[7], -1))
    send(4)

    def rows(start):
        at = pl.ds(start, ROWS)
        slope = [half_sign * got_ref[a, at, :] for a in range(3)]
        row = [conf_ref[f, 0, at, :] for f in (0, 3, 4)]
        for f in range(6):
            i, j = COMPONENT_PAIRS[f]
            if i == j:
                term = 2.0 * (row[i] * slope[j])
            else:
                term = row[i] * slope[j] + slope[i] * row[j]
            new_tile[f, at, :] = part_ref[f, 0, at, :] + term

    for_rows(height, rows)
    for f in range(6):
        copy = pltpu.make_async_copy(new_tile.at[f], new_ref.at[f, plane], sems.at[5 + f])
        copy.start()
        copies.append(copy)
    for copy in copies:
        copy.wait()


def finish(plane, part, conform, got, sent, corner, read, new=None):
    height, width = conform.shape[2:]
    second = new is not None
    plane_spec = pl.BlockSpec((6, 1, height, width), lambda g, s: (0, s[0], 0, 0))
    in_specs = [
        plane_spec,
        plane_spec,
        pl.BlockSpec((8, height, width), lambda g, s: (0, 0, 0)),
        pl.BlockSpec((1, 8, width), lambda g, s: (5, 0, 0)),
        pl.BlockSpec((1, 8, width), lambda g, s: (4, height // 8 - 1, 0)),
        pl.BlockSpec((16, height), lambda g, s: (0, 0)),
        any_spec(),
    ]
    operands = [plane, part, conform, got, sent, sent, corner, read]
    aliases = {7: 0}
    if second:
        in_specs.append(any_spec())
        operands.append(new)
        aliases[8] = 1
    return pl.pallas_call(
        functools.partial(finish_kernel, second),
        grid_spec=pltpu.PrefetchScalarGridSpec(
            num_scalar_prefetch=1,
            grid=(1,),
            in_specs=in_specs,
            out_specs=(any_spec(), any_spec()),
            scratch_shapes=[
                VMEM((5, height, width), F32),
                VMEM((6, height, width), F32),
                pltpu.SemaphoreType.DMA((11,)),
            ],
        ),
        out_shape=(
            jax.ShapeDtypeStruct(read.shape, F32),
            jax.ShapeDtypeStruct(conform.shape, F32),
        ),
        input_output_aliases=aliases,
        compiler_params=params(),
        name="finish_odd" if second else "finish_even",
    )(*operands)


def body(popul, conform):
    wide = lax.axis_size("wide")
    narrow = lax.axis_size("narrow")
    odd = lax.rem(lax.axis_index("wide"), 2)
    plane_e = (1 - odd).astype(jnp.int32).reshape(1)
    plane_o = odd.astype(jnp.int32).reshape(1)
    even_pairs = [(i, i ^ 1) for i in range(wide)]
    odd_pairs = [(i, (i + 1) % wide if i % 2 else (i - 1) % wide) for i in range(wide)]
    up = [(i, (i + 1) % narrow) for i in range(narrow)]
    down = [(j, i) for i, j in up]

    near = lax.dynamic_index_in_dim(conform, plane_e[0], axis=1, keepdims=False)
    halo_e = lax.ppermute(near, "wide", even_pairs)
    conf_up, conf_down, far = edges(plane_o, conform)
    halo_o = lax.ppermute(far, "wide", odd_pairs)
    conf_low = lax.ppermute(conf_up, "narrow", up)
    conf_high = lax.ppermute(conf_down, "narrow", down)
    pre = prepare(conform, popul, conf_low, conf_high)
    post, sent_e, z_up, z_down = collide(plane_e, popul, pre, halo_e)
    got_e = lax.ppermute(sent_e, "wide", even_pairs)
    post, sent_o, z_up, z_down = collide(plane_o, popul, pre, halo_o, (post, z_up, z_down))
    got_o = lax.ppermute(sent_o, "wide", odd_pairs)
    low = lax.ppermute(z_up, "narrow", up)
    high = lax.ppermute(z_down, "narrow", down)
    corner_e, corner_o = corners(low, high)
    corner_e = lax.ppermute(corner_e, "wide", even_pairs)
    corner_o = lax.ppermute(corner_o, "wide", odd_pairs)
    read, part = inner(
        jnp.concatenate([plane_e, plane_o]),
        conform,
        halo_e,
        halo_o,
        conf_low,
        conf_high,
        low,
        high,
        post,
        sent_e,
        sent_o,
    )
    read, new = finish(plane_e, part, conform, got_e, sent_e, corner_e, read)
    return finish(plane_o, part, conform, got_o, sent_o, corner_o, read, new)


def solution(mesh):
    placed = P(None, "wide", None, "narrow")
    return jax.shard_map(
        body, mesh=mesh, in_specs=(placed, placed), out_specs=(placed, placed), check_vma=False
    )
```

time: 161 us -> 54.2 us (0.34)
  waiting for transfers between devices: 52.4 us -> 9.86 us
  local copies, waits for them, and re-layouts: 47.3 us -> 5 us
  other arithmetic: 42 us -> 0.07 us
  Pallas kernels: 0 us -> 20.7 us
    ppermute x12 -> x10, waiting for transfers between devices: 52.4 us -> 9.86 us  [the longest x1 4.32 us: body(): corner_e = lax.ppermute(corner_e, 'wide', even_pairs)]
    slice x21 -> x0, local copies, waits for them, and re-layouts: 27.9 us -> none  [the longest x7 16.8 us: padded_2(): initial = lax.slice_in_dim(shard, 0, width, axis=dim)]
    pallas_call x0 -> x8, Pallas kernels: none -> 20.7 us  [the longest x2 7.12 us: collide(): pl.pallas_call(functools.partial(collide_kernel, second), grid_spec=pltpu...]
    unnamed x45 -> x0, other arithmetic: 18.2 us -> none
    ppermute x6 -> x0, local copies, waits for them, and re-layouts: 12 us -> none  [the longest x3 6.03 us: padded_2(): before = lax.ppermute(last, axis, up)]
    mul x13 -> x0, other arithmetic: 7.19 us -> none  [the longest x2 2.68 us: gradients(): along_x = 0.5 * (padded[:, 2:, :, 1:-1] - padded[:, :-2, :, 1:-1])]
    concatenate x3 -> x1, other arithmetic: 5.86 us -> 0.07 us  [body(): jnp.concatenate([plane_e, plane_o])]
    squeeze x4 -> x0, other arithmetic: 5.64 us -> none  [the longest x3 5.42 us: body(): padded_post[number, start_x:start_x + planes_x, :, start_z:start_z + plan...]
  transfers between devices with their start and end apart: 12 -> 10, of which waited for: 4 -> 4; matrix products, arithmetic and copies ran while one was open for 19% -> 0% of each run, Pallas kernels for 0% -> 36%
where the time goes in v1:
time: 54.2 us; the launch traced here: 53.9 us
  Pallas kernels  20.7 us (38%)
  starting transfers between devices  17.5 us (32%)
  waiting for transfers between devices  9.86 us (18%)
  local copies, waits for them, and re-layouts  5 us (9%)
  between operations  0.72 us (1%)
    pallas_call x2, Pallas kernels, collide(): pl.pallas_call(functools.partial(collide_kernel, second), grid_spec=pltpu...  7.12 us
    pallas_call x1, Pallas kernels, inner(): pl.pallas_call(inner_kernel, grid=(1,), out_shape=(jax.ShapeDtypeStruct(p...  6.64 us
    ppermute x1, waiting for transfers between devices, body(): corner_e = lax.ppermute(corner_e, 'wide', even_pairs)  4.32 us
    unnamed x8, local copies, waits for them, and re-layouts  3.97 us
    ppermute x1, starting transfers between devices, body(): got_o = lax.ppermute(sent_o, 'wide', odd_pairs)  3.61 us
    ppermute x1, starting transfers between devices, body(): halo_o = lax.ppermute(far, 'wide', odd_pairs)  3.61 us
    pallas_call x1, Pallas kernels, prepare(): pl.pallas_call(prepare_kernel, out_shape=jax.ShapeDtypeStruct((7, 2, heig...  3.13 us
    ppermute x1, starting transfers between devices, body(): halo_e = lax.ppermute(near, 'wide', even_pairs)  3.03 us
  transfers between devices with their start and end apart: 10, of which 4 were waited for; matrix products, arithmetic and copies ran while one was open for 0% of the time, Pallas kernels for 36%

profile of v1, /device:TPU:0, one launch (start us, length us, event | category | flops | bytes accessed | tf_op | source)
XLA Modules:
  0.0 53.9 jit_solution(18013107175382050787)
XLA Ops:
  0.6 1.0 %dynamic-slice_bitcast_fusion = f32[6,128,128]{2,1,0:T(8,128)S(1)} fusion(f32[6,2,128,128]{3,2,1,0:T(8,128)} %conf_ref.9, s32[]{:T(128)S(6)} %select_n.4), kind=kLoop, calls=%fused_computation | loop fusion | bytes 786436 | tf_op jit(solution)/shard_map/jit(dynamic_index_in_dim)/squeeze | solution.py:630
  1.7 3.0 %collective-permute-start = (f32[6,128,128]{2,1,0:T(8,128)S(1)}, f32[6,128,128]{2,1,0:T(8,128)S(1)}, u32[]{:S(2)}, u32[]{:S(2)}) collective-permute-start(f32[6,128,128]{2,1,0:T(8,128)S(1)} %dynamic-slice_bitcast_fusion), channel_id=1, source_target_pairs={{0,4},{4,0},{8,12},{12,8},{16,20},{20,16},{24,28},{28,24},{1,5},{5... | collective-permute-start | bytes 1179656 | tf_op jit(solution)/shard_map/ppermute | solution.py:631
  4.7 0.0 copy-start
  4.7 1.1 %copy-done = f32[6,2,128,128]{3,2,1,0:T(8,128)S(1)} copy-done((f32[6,2,128,128]{3,2,1,0:T(8,128)S(1)}, f32[6,2,128,128]{3,2,1,0:T(8,128)}, u32[]{:S(2)}) %copy-start) | copy-done | bytes 786456
  5.8 1.5 %edges.1 = (f32[128,128]{1,0:T(8,128)S(1)}, f32[128,128]{1,0:T(8,128)S(1)}, f32[6,128,128]{2,1,0:T(8,128)S(1)}) custom-call(s32[1]{0:T(128)} %bitcast.far_ref.plane_ref, f32[6,2,128,128]{3,2,1,0:T(8,128)S(1)} %copy-done), custom_call_target="tpu_custom_call" | custom-call | tf_op jit(solution)/shard_map/edges/pallas_call | solution.py:115
  7.3 3.6 %collective-permute-start.1 = (f32[6,128,128]{2,1,0:T(8,128)S(1)}, f32[6,128,128]{2,1,0:T(8,128)S(1)}, u32[]{:S(2)}, u32[]{:S(2)}) collective-permute-start(f32[6,128,128]{2,1,0:T(8,128)S(1)} %get-tuple-element.19), channel_id=1, source_target_pairs={{0,28},{4,8},{8,4},{12,16},{16,12},{20,24},{24,20},{28,0},{1,29},{... | collective-permute-start | bytes 1179656 | tf_op jit(solution)/shard_map/ppermute | solution.py:633
  10.9 0.0 collective-permute-start.2
  10.9 1.7 %collective-permute-start.3 = (f32[128,128]{1,0:T(8,128)S(1)}, f32[128,128]{1,0:T(8,128)S(1)}, u32[]{:S(2)}, u32[]{:S(2)}) collective-permute-start(f32[128,128]{1,0:T(8,128)S(1)} %get-tuple-element.21), channel_id=1, source_target_pairs={{1,0},{2,1},{3,2},{0,3},{5,4},{6,5},{7,6},{4,7},{9,8},{10,9},{11,1... | collective-permute-start | bytes 196616 | tf_op jit(solution)/shard_map/ppermute | solution.py:635
  12.7 1.9 %collective-permute-done.2.low_ref.conf_low = f32[128,128]{1,0:T(8,128)S(1)} collective-permute-done((f32[128,128]{1,0:T(8,128)S(1)}, f32[128,128]{1,0:T(8,128)S(1)}, u32[]{:S(2)}, u32[]{:S(2)}) %collective-permute-start.2) | collective-permute-done | bytes 65568 | tf_op jit(solution)/shard_map/ppermute | solution.py:634
  14.6 0.0 collective-permute-done.3.high_ref.conf_high
  14.6 0.0 copy-start.1
  14.6 1.1 %copy-done.1 = f32[6,2,128,128]{3,2,1,0:T(8,128)S(1)} copy-done((f32[6,2,128,128]{3,2,1,0:T(8,128)S(1)}, f32[6,2,128,128]{3,2,1,0:T(8,128)}, u32[]{:S(2)}) %copy-start.1) | copy-done | bytes 786456
  15.8 0.0 copy-start.3
  15.8 1.7 %copy-done.3 = f32[19,2,128,128]{3,2,1,0:T(8,128)S(1)} copy-done((f32[19,2,128,128]{3,2,1,0:T(8,128)S(1)}, f32[19,2,128,128]{3,2,1,0:T(8,128)}, u32[]{:S(2)}) %copy-start.3) | copy-done | bytes 2490392
  17.5 3.1 %prepare.1.pre_ref = f32[7,2,128,128]{3,2,1,0:T(8,128)S(1)} custom-call(f32[6,2,128,128]{3,2,1,0:T(8,128)S(1)} %copy-done.1, f32[19,2,128,128]{3,2,1,0:T(8,128)S(1)} %copy-done.3, f32[128,128]{1,0:T(8,128)S(1)} %collective-permute-done.2.low_ref.conf_low, f32[128,128]{1,0:T(8,128)S(1)} %collective-permute-done.3.high_ref.conf_high), custom_call_target="tpu_custom_call" | custom-call | tf_op jit(solution)/shard_map/prepare/pallas_call | solution.py:191
  20.6 1.6 %collective-permute-done.halo_ref.halo_e = f32[6,128,128]{2,1,0:T(8,128)S(1)} collective-permute-done((f32[6,128,128]{2,1,0:T(8,128)S(1)}, f32[6,128,128]{2,1,0:T(8,128)S(1)}, u32[]{:S(2)}, u32[]{:S(2)}) %collective-permute-start) | collective-permute-done | bytes 393248 | tf_op jit(solution)/shard_map/ppermute | solution.py:631
  22.2 3.5 %collide_even.1 = (f32[19,2,128,128]{3,2,1,0:T(8,128)S(1)}, f32[8,128,128]{2,1,0:T(8,128)S(1)}, f32[128,128]{1,0:T(8,128)S(1)}, f32[128,128]{1,0:T(8,128)S(1)}) custom-call(s32[1]{0:T(128)} %bitcast.1.plane_ref, f32[19,2,128,128]{3,2,1,0:T(8,128)} %popul_ref.5, f32[7,2,128,128]{3,2,1,0:T(8,128)S(1)} %prepare.1.pre_ref, ...), custom_call_target="tpu_custom_call" | custom-call | tf_op jit(solution)/shard_map/collide_even/pallas_call | solution.py:294
  25.8 1.8 %collective-permute-start.8 = (f32[8,128,128]{2,1,0:T(8,128)S(1)}, f32[8,128,128]{2,1,0:T(8,128)S(1)}, u32[]{:S(2)}, u32[]{:S(2)}) collective-permute-start(f32[8,128,128]{2,1,0:T(8,128)S(1)} %get-tuple-element.28.velo_e.bottom_ref.top_ref), channel_id=1, source_target_pairs={{0,4},{4,0},{8,12},{12,8},{16,20},{20,16},{24,28},{28,24},{1,5},{5... | collective-permute-start | bytes 1572872 | tf_op jit(solution)/shard_map/ppermute | solution.py:638
  27.6 0.0 collective-permute-done.1.halo_ref.halo_o
  27.6 0.0 copy-start.2
  27.6 3.6 %collide_odd.1 = (f32[19,2,128,128]{3,2,1,0:T(8,128)S(1)}, f32[8,128,128]{2,1,0:T(8,128)S(1)}, f32[128,128]{1,0:T(8,128)S(1)}, f32[128,128]{1,0:T(8,128)S(1)}) custom-call(s32[1]{0:T(128)} %bitcast.far_ref.plane_ref, f32[19,2,128,128]{3,2,1,0:T(8,128)} %popul_ref.5, f32[7,2,128,128]{3,2,1,0:T(8,128)S(1)} %prepare.1.pre_ref, ...), custom_call_target="tpu_custom_call", output_to_operand_aliasing={{0}: (4, {})} | custom-call | tf_op jit(solution)/shard_map/collide_odd/pallas_call | solution.py:294
  31.2 3.6 %collective-permute-start.6 = (f32[8,128,128]{2,1,0:T(8,128)S(1)}, f32[8,128,128]{2,1,0:T(8,128)S(1)}, u32[]{:S(2)}, u32[]{:S(2)}) collective-permute-start(f32[8,128,128]{2,1,0:T(8,128)S(1)} %get-tuple-element.29.velo_o.bottom_ref.top_ref), channel_id=1, source_target_pairs={{0,28},{4,8},{8,4},{12,16},{16,12},{20,24},{24,20},{28,0},{1,29},{... | collective-permute-start | bytes 1572872 | tf_op jit(solution)/shard_map/ppermute | solution.py:640
  34.8 0.0 collective-permute-start.4
  34.8 1.7 %collective-permute-start.5 = (f32[128,128]{1,0:T(8,128)S(1)}, f32[128,128]{1,0:T(8,128)S(1)}, u32[]{:S(2)}, u32[]{:S(2)}) collective-permute-start(f32[128,128]{1,0:T(8,128)S(1)} %get-tuple-element.26), channel_id=1, source_target_pairs={{1,0},{2,1},{3,2},{0,3},{5,4},{6,5},{7,6},{4,7},{9,8},{10,9},{11,1... | collective-permute-start | bytes 196616 | tf_op jit(solution)/shard_map/ppermute | solution.py:642
  36.5 1.9 %collective-permute-done.4.low_ref = f32[128,128]{1,0:T(8,128)S(1)} collective-permute-done((f32[128,128]{1,0:T(8,128)S(1)}, f32[128,128]{1,0:T(8,128)S(1)}, u32[]{:S(2)}, u32[]{:S(2)}) %collective-permute-start.4) | collective-permute-done | bytes 65568 | tf_op jit(solution)/shard_map/ppermute | solution.py:641
  38.5 0.0 collective-permute-done.5.high_ref
  38.5 0.1 corners.1
  38.6 0.0 collective-permute-start.9
  38.6 1.9 %collective-permute-start.7 = (f32[16,128]{1,0:T(8,128)S(1)}, f32[16,128]{1,0:T(8,128)S(1)}, u32[]{:S(2)}, u32[]{:S(2)}) collective-permute-start(f32[16,128]{1,0:T(8,128)S(1)} %get-tuple-element.31), channel_id=1, source_target_pairs={{0,28},{4,8},{8,4},{12,16},{16,12},{20,24},{24,20},{28,0},{1,29},{... | collective-permute-start | bytes 24584 | tf_op jit(solution)/shard_map/ppermute | solution.py:645
  40.5 0.1 pad_add_fusion.planes_ref
  40.6 0.0 copy-done.2
  40.6 6.6 %inner.1 = (f32[19,2,128,128]{3,2,1,0:T(8,128)}, f32[6,2,128,128]{3,2,1,0:T(8,128)S(1)}) custom-call(s32[2]{0:T(128)S(1)} %pad_add_fusion.planes_ref, f32[6,2,128,128]{3,2,1,0:T(8,128)S(1)} %copy-done.2, f32[6,128,128]{2,1,0:T(8,128)S(1)} %collective-permute-done.halo_ref.halo_e, f32[6,128,128]{2,1,0:T(8,128)S(1)} %collective-permute-done.1.halo_ref.halo_o, ...), custom_call_target="tpu_custom_call" | custom-call | tf_op jit(solution)/shard_map/inner/pallas_call | solution.py:481
  47.2 4.3 %collective-permute-done.9.corner_ref = f32[16,128]{1,0:T(8,128)S(1)} collective-permute-done((f32[16,128]{1,0:T(8,128)S(1)}, f32[16,128]{1,0:T(8,128)S(1)}, u32[]{:S(2)}, u32[]{:S(2)}) %collective-permute-start.9) | collective-permute-done | bytes 8224 | tf_op jit(solution)/shard_map/ppermute | solution.py:644
  51.6 0.0 collective-permute-done.8.got_ref
  51.6 1.1 %finish_even.1 = (f32[19,2,128,128]{3,2,1,0:T(8,128)}, f32[6,2,128,128]{3,2,1,0:T(8,128)}) custom-call(s32[1]{0:T(128)} %bitcast.1.plane_ref, f32[6,2,128,128]{3,2,1,0:T(8,128)S(1)} %get-tuple-element.30.part_ref, f32[6,2,128,128]{3,2,1,0:T(8,128)S(1)} %copy-done.2, ...), custom_call_target="tpu_custom_call", output_to_operand_aliasing={{0}: (7, {})} | custom-call | tf_op jit(solution)/shard_map/finish_even/pallas_call | solution.py:596
  52.7 0.0 collective-permute-done.7.corner_ref
  52.7 0.0 collective-permute-done.6.got_ref
  52.7 1.1 %finish_odd.1 = (f32[19,2,128,128]{3,2,1,0:T(8,128)}, f32[6,2,128,128]{3,2,1,0:T(8,128)}) custom-call(s32[1]{0:T(128)} %bitcast.far_ref.plane_ref, f32[6,2,128,128]{3,2,1,0:T(8,128)S(1)} %get-tuple-element.30.part_ref, f32[6,2,128,128]{3,2,1,0:T(8,128)S(1)} %copy-done.2, ...), custom_call_target="tpu_custom_call", output_to_operand_aliasing={{0}: (7, {}), {1}: (8, {})} | custom-call | tf_op jit(solution)/shard_map/finish_odd/pallas_call | solution.py:596
Async XLA Ops:
  1.7 20.6 %collective-permute-start = (f32[6,128,128]{2,1,0:T(8,128)S(1)}, f32[6,128,128]{2,1,0:T(8,128)S(1)}, u32[]{:S(2)}, u32[]{:S(2)}) collective-permute-start(f32[6,128,128]{2,1,0:T(8,128)S(1)} %dynamic-slice_bitcast_fusion), channel_id=1, source_target_pairs={{0,4},{4,0},{8,12},{12,8},{16,20},{20,16},{24,28},{28,24},{1,5},{5... | collective-permute-start | bytes 1179656 | tf_op jit(solution)/shard_map/ppermute | solution.py:631
  4.7 1.1 %copy-start = (f32[6,2,128,128]{3,2,1,0:T(8,128)S(1)}, f32[6,2,128,128]{3,2,1,0:T(8,128)}, u32[]{:S(2)}) copy-start(f32[6,2,128,128]{3,2,1,0:T(8,128)} %conf_ref.9) | copy-start | bytes 2359300
  7.3 20.2 %collective-permute-start.1 = (f32[6,128,128]{2,1,0:T(8,128)S(1)}, f32[6,128,128]{2,1,0:T(8,128)S(1)}, u32[]{:S(2)}, u32[]{:S(2)}) collective-permute-start(f32[6,128,128]{2,1,0:T(8,128)S(1)} %get-tuple-element.19), channel_id=1, source_target_pairs={{0,28},{4,8},{8,4},{12,16},{16,12},{20,24},{24,20},{28,0},{1,29},{... | collective-permute-start | bytes 1179656 | tf_op jit(solution)/shard_map/ppermute | solution.py:633
  10.9 3.7 %collective-permute-start.2 = (f32[128,128]{1,0:T(8,128)S(1)}, f32[128,128]{1,0:T(8,128)S(1)}, u32[]{:S(2)}, u32[]{:S(2)}) collective-permute-start(f32[128,128]{1,0:T(8,128)S(1)} %get-tuple-element.20), channel_id=1, source_target_pairs={{0,1},{1,2},{2,3},{3,0},{4,5},{5,6},{6,7},{7,4},{8,9},{9,10},{10,1... | collective-permute-start | bytes 196616 | tf_op jit(solution)/shard_map/ppermute | solution.py:634
  10.9 3.7 %collective-permute-start.3 = (f32[128,128]{1,0:T(8,128)S(1)}, f32[128,128]{1,0:T(8,128)S(1)}, u32[]{:S(2)}, u32[]{:S(2)}) collective-permute-start(f32[128,128]{1,0:T(8,128)S(1)} %get-tuple-element.21), channel_id=1, source_target_pairs={{1,0},{2,1},{3,2},{0,3},{5,4},{6,5},{7,6},{4,7},{9,8},{10,9},{11,1... | collective-permute-start | bytes 196616 | tf_op jit(solution)/shard_map/ppermute | solution.py:635
  14.6 1.1 %copy-start.1 = (f32[6,2,128,128]{3,2,1,0:T(8,128)S(1)}, f32[6,2,128,128]{3,2,1,0:T(8,128)}, u32[]{:S(2)}) copy-start(f32[6,2,128,128]{3,2,1,0:T(8,128)} %conf_ref.9) | copy-start | bytes 2359300
  15.8 1.7 %copy-start.3 = (f32[19,2,128,128]{3,2,1,0:T(8,128)S(1)}, f32[19,2,128,128]{3,2,1,0:T(8,128)}, u32[]{:S(2)}) copy-start(f32[19,2,128,128]{3,2,1,0:T(8,128)} %popul_ref.5) | copy-start | bytes 7471108
  25.8 25.8 %collective-permute-start.8 = (f32[8,128,128]{2,1,0:T(8,128)S(1)}, f32[8,128,128]{2,1,0:T(8,128)S(1)}, u32[]{:S(2)}, u32[]{:S(2)}) collective-permute-start(f32[8,128,128]{2,1,0:T(8,128)S(1)} %get-tuple-element.28.velo_e.bottom_ref.top_ref), channel_id=1, source_target_pairs={{0,4},{4,0},{8,12},{12,8},{16,20},{20,16},{24,28},{28,24},{1,5},{5... | collective-permute-start | bytes 1572872 | tf_op jit(solution)/shard_map/ppermute | solution.py:638
  27.6 13.0 %copy-start.2 = (f32[6,2,128,128]{3,2,1,0:T(8,128)S(1)}, f32[6,2,128,128]{3,2,1,0:T(8,128)}, u32[]{:S(2)}) copy-start(f32[6,2,128,128]{3,2,1,0:T(8,128)} %conf_ref.9) | copy-start | bytes 2359300
  31.2 21.5 %collective-permute-start.6 = (f32[8,128,128]{2,1,0:T(8,128)S(1)}, f32[8,128,128]{2,1,0:T(8,128)S(1)}, u32[]{:S(2)}, u32[]{:S(2)}) collective-permute-start(f32[8,128,128]{2,1,0:T(8,128)S(1)} %get-tuple-element.29.velo_o.bottom_ref.top_ref), channel_id=1, source_target_pairs={{0,28},{4,8},{8,4},{12,16},{16,12},{20,24},{24,20},{28,0},{1,29},{... | collective-permute-start | bytes 1572872 | tf_op jit(solution)/shard_map/ppermute | solution.py:640
  34.8 3.7 %collective-permute-start.4 = (f32[128,128]{1,0:T(8,128)S(1)}, f32[128,128]{1,0:T(8,128)S(1)}, u32[]{:S(2)}, u32[]{:S(2)}) collective-permute-start(f32[128,128]{1,0:T(8,128)S(1)} %get-tuple-element.25), channel_id=1, source_target_pairs={{0,1},{1,2},{2,3},{3,0},{4,5},{5,6},{6,7},{7,4},{8,9},{9,10},{10,1... | collective-permute-start | bytes 196616 | tf_op jit(solution)/shard_map/ppermute | solution.py:641
  34.8 3.7 %collective-permute-start.5 = (f32[128,128]{1,0:T(8,128)S(1)}, f32[128,128]{1,0:T(8,128)S(1)}, u32[]{:S(2)}, u32[]{:S(2)}) collective-permute-start(f32[128,128]{1,0:T(8,128)S(1)} %get-tuple-element.26), channel_id=1, source_target_pairs={{1,0},{2,1},{3,2},{0,3},{5,4},{6,5},{7,6},{4,7},{9,8},{10,9},{11,1... | collective-permute-start | bytes 196616 | tf_op jit(solution)/shard_map/ppermute | solution.py:642
  38.6 13.0 %collective-permute-start.9 = (f32[16,128]{1,0:T(8,128)S(1)}, f32[16,128]{1,0:T(8,128)S(1)}, u32[]{:S(2)}, u32[]{:S(2)}) collective-permute-start(f32[16,128]{1,0:T(8,128)S(1)} %get-tuple-element.32), channel_id=1, source_target_pairs={{0,4},{4,0},{8,12},{12,8},{16,20},{20,16},{24,28},{28,24},{1,5},{5... | collective-permute-start | bytes 24584 | tf_op jit(solution)/shard_map/ppermute | solution.py:644
  38.6 14.1 %collective-permute-start.7 = (f32[16,128]{1,0:T(8,128)S(1)}, f32[16,128]{1,0:T(8,128)S(1)}, u32[]{:S(2)}, u32[]{:S(2)}) collective-permute-start(f32[16,128]{1,0:T(8,128)S(1)} %get-tuple-element.31), channel_id=1, source_target_pairs={{0,28},{4,8},{8,4},{12,16},{16,12},{20,24},{24,20},{28,0},{1,29},{... | collective-permute-start | bytes 24584 | tf_op jit(solution)/shard_map/ppermute | solution.py:645

commit v2 on v1

--- a/solution.py
+++ b/solution.py
@@ -47,7 +47,7 @@
 Z_DOWN = tuple(
     VELOCITIES.index(v) for v in ((0, 0, -1), (0, 1, -1), (0, -1, -1), (1, 0, -1), (-1, 0, -1))
 )
-ROWS = 8
+ROWS = 32
 F32 = jnp.float32
 VMEM = pltpu.VMEM
 
@@ -61,7 +61,7 @@
 
 
 def params():
-    return pltpu.CompilerParams(vmem_limit_bytes=48 << 20)
+    return pltpu.CompilerParams(vmem_limit_bytes=12 << 20)
 
 
 def lanes_of(like):
@@ -94,35 +94,109 @@
     return (EXTENSION_SQ - 3.0) / (EXTENSION_SQ - (c_xx + c_yy + c_zz))
 
 
-def edge_kernel(far_ref, conf_ref, up_ref, down_ref, far_out):
+def load_kernel(near_plane, conf_hbm, conf_ref, near_ref, sems):
+    near = near_plane[0]
+    copies = [
+        pltpu.make_async_copy(conf_hbm.at[:, near], near_ref, sems.at[0]),
+        pltpu.make_async_copy(conf_hbm, conf_ref, sems.at[1]),
+    ]
+    for copy in copies:
+        copy.start()
+    for copy in copies:
+        copy.wait()
+
+
+def load(near_plane, conform):
+    shape = conform.shape
+    return pl.pallas_call(
+        load_kernel,
+        out_shape=(
+            jax.ShapeDtypeStruct(shape, F32),
+            jax.ShapeDtypeStruct((shape[0],) + shape[2:], F32),
+        ),
+        in_specs=[pl.BlockSpec(memory_space=pltpu.SMEM), any_spec()],
+        out_specs=(vmem_spec(), vmem_spec()),
+        scratch_shapes=[pltpu.SemaphoreType.DMA((2,))],
+        compiler_params=params(),
+        name="load",
+    )(near_plane, conform)
+
+
+def edge_kernel(conf_ref, up_ref, down_ref):
     height, width = conf_ref.shape[2:]
-    far = far_ref[0]
 
     def rows(start):
         at = pl.ds(start, ROWS)
         values = [conf_ref[f, p, at, :] for p in range(2) for f in range(6)]
         up_ref[at, :] = pack_columns(values, width - 1)
         down_ref[at, :] = pack_columns(values, 0)
-        for f in range(6):
-            far_out[f, at, :] = conf_ref[f, far, at, :]
 
     for_rows(height, rows)
 
 
-def edges(far, conform):
+def edges(conform):
     height, width = conform.shape[2:]
     tile = jax.ShapeDtypeStruct((height, width), F32)
     return pl.pallas_call(
         edge_kernel,
-        out_shape=(tile, tile, jax.ShapeDtypeStruct((6, height, width), F32)),
-        in_specs=[pl.BlockSpec(memory_space=pltpu.SMEM), vmem_spec()],
-        out_specs=(vmem_spec(), vmem_spec(), vmem_spec()),
+        out_shape=(tile, tile),
+        in_specs=[vmem_spec()],
+        out_specs=(vmem_spec(), vmem_spec()),
         compiler_params=params(),
         name="edges",
-    )(far, conform)
-
-
-def prepare_kernel(conf_ref, popul_ref, low_ref, high_ref, pre_ref, tall):
+    )(conform)
+
+
+def moments_kernel(far_plane, popul_hbm, conf_ref, _, popul_ref, sums_ref, far_ref, sems):
+    height = conf_ref.shape[2]
+    copies = []
+    for p in range(2):
+        copies.append(pltpu.make_async_copy(popul_hbm.at[:, p], popul_ref.at[:, p], sems.at[p]))
+        copies[-1].start()
+    far = far_plane[0]
+    for f in range(6):
+        far_ref[f] = conf_ref[f, far]
+    for p in range(2):
+        copies[p].wait()
+
+        def rows(start, p=p):
+            at = pl.ds(start, ROWS)
+            values = [popul_ref[i, p, at, :] for i in range(19)]
+            density = values[0]
+            for i in range(1, 19):
+                density = density + values[i]
+            sums_ref[0, p, at, :] = density
+            for axis in range(3):
+                moment = None
+                for i in range(19):
+                    if VELOCITIES[i][axis] == 1:
+                        moment = values[i] if moment is None else moment + values[i]
+                for i in range(19):
+                    if VELOCITIES[i][axis] == -1:
+                        moment = moment - values[i]
+                sums_ref[1 + axis, p, at, :] = moment
+
+        for_rows(height, rows)
+
+
+def moments(far_plane, popul, conform, after):
+    shape = conform.shape
+    return pl.pallas_call(
+        moments_kernel,
+        out_shape=(
+            jax.ShapeDtypeStruct(popul.shape, F32),
+            jax.ShapeDtypeStruct((4,) + shape[1:], F32),
+            jax.ShapeDtypeStruct((shape[0],) + shape[2:], F32),
+        ),
+        in_specs=[pl.BlockSpec(memory_space=pltpu.SMEM), any_spec(), vmem_spec(), any_spec()],
+        out_specs=(vmem_spec(),) * 3,
+        scratch_shapes=[pltpu.SemaphoreType.DMA((2,))],
+        compiler_params=params(),
+        name="moments",
+    )(far_plane, popul, conform, after)
+
+
+def prepare_kernel(conf_ref, low_ref, high_ref, pre_ref, tall):
     height, width = conf_ref.shape[2:]
 
     def stress(fields, at_of):
@@ -156,20 +230,6 @@
                 if number == 0:
                     term = term + DRIVE_FORCE
                 pre_ref[number, p, at, :] = term
-            values = [popul_ref[i, p, at, :] for i in range(19)]
-            density = values[0]
-            for i in range(1, 19):
-                density = density + values[i]
-            pre_ref[3, p, at, :] = density
-            for axis in range(3):
-                moment = None
-                for i in range(19):
-                    if VELOCITIES[i][axis] == 1:
-                        moment = values[i] if moment is None else moment + values[i]
-                for i in range(19):
-                    if VELOCITIES[i][axis] == -1:
-                        moment = moment - values[i]
-                pre_ref[4 + axis, p, at, :] = moment
 
         for_rows(height, first)
         for number in range(3):
@@ -186,20 +246,20 @@
         for_rows(height, second)
 
 
-def prepare(conform, popul, low, high):
+def prepare(conform, low, high):
     height, width = conform.shape[2:]
     return pl.pallas_call(
         prepare_kernel,
-        out_shape=jax.ShapeDtypeStruct((7, 2, height, width), F32),
-        in_specs=[vmem_spec()] * 4,
+        out_shape=jax.ShapeDtypeStruct((3, 2, height, width), F32),
+        in_specs=[vmem_spec()] * 3,
         out_specs=vmem_spec(),
         scratch_shapes=[VMEM((3, 2, height + 16, width), F32)],
         compiler_params=params(),
         name="prepare",
-    )(conform, popul, low, high)
-
-
-def collide_kernel(second, plane_ref, popul_ref, pre_ref, halo_ref, *refs):
+    )(conform, low, high)
+
+
+def collide_kernel(second, plane_ref, popul_ref, sums_ref, pre_ref, halo_ref, *refs):
     if second:
         _, up_in, down_in, post_ref, message_ref, up_ref, down_ref = refs
     else:
@@ -217,10 +277,10 @@
         halo = [halo_ref[f, at, :] for f in range(5)]
         peterlin = STRESS_SCALE * peterlin_of(halo[0], halo[1], halo[2])
         stress = (peterlin * halo[0] - STRESS_SCALE, peterlin * halo[3], peterlin * halo[4])
-        force = [pre_ref[a, 0, at, :] + half_sign * stress[a] for a in range(3)]
-        density = pre_ref[3, 0, at, :]
+        force = [pre_ref[a, plane, at, :] + half_sign * stress[a] for a in range(3)]
+        density = sums_ref[0, plane, at, :]
         inverse = 1.0 / density
-        velocity = [(pre_ref[4 + a, 0, at, :] + 0.5 * force[a]) * inverse for a in range(3)]
+        velocity = [(sums_ref[1 + a, plane, at, :] + 0.5 * force[a]) * inverse for a in range(3)]
         speed_sq = (
             velocity[0] * velocity[0] + velocity[1] * velocity[1] + velocity[2] * velocity[2]
         )
@@ -230,7 +290,7 @@
         flow = [rate * velocity[a] for a in range(3)]
         drag = [factor * force[a] for a in range(3)]
         post = [None] * 19
-        post[0] = keep * popul_ref[0, 0, at, :] + LATTICE_WEIGHTS[0] * common
+        post[0] = keep * popul_ref[0, plane, at, :] + LATTICE_WEIGHTS[0] * common
 
         def along(vec, parts):
             total = None
@@ -250,10 +310,10 @@
             total = c_flow + c_drag
             even = weight * common + (4.5 * weight) * (c_u * (total + c_drag))
             odd = (3.0 * weight) * total
-            post[i] = keep * popul_ref[i, 0, at, :] + (even + odd)
-            post[i + 1] = keep * popul_ref[i + 1, 0, at, :] + (even - odd)
+            post[i] = keep * popul_ref[i, plane, at, :] + (even + odd)
+            post[i + 1] = keep * popul_ref[i + 1, plane, at, :] + (even - odd)
         for i in range(19):
-            post_ref[i, 0, at, :] = post[i]
+            post_ref[i, plane, at, :] = post[i]
         for a in range(3):
             message_ref[a, at, :] = velocity[a]
         for slot in range(5):
@@ -270,47 +330,22 @@
     for_rows(height, rows)
 
 
-def collide(plane, popul, pre, halo, earlier=None):
+def collide(plane, popul, sums, pre, halo, earlier=None):
     height, width = popul.shape[2:]
-    block = min(32, height)
     second = earlier is not None
     tile = jax.ShapeDtypeStruct((height, width), F32)
-    tile_spec = pl.BlockSpec((block, width), lambda g, s: (g, 0))
-
-    def plane_spec(count):
-        return pl.BlockSpec((count, 1, block, width), lambda g, s: (0, s[0], g, 0))
-
-    in_specs = [
-        plane_spec(19),
-        plane_spec(7),
-        pl.BlockSpec((6, block, width), lambda g, s: (0, g, 0)),
-    ]
-    operands = [plane, popul, pre, halo]
-    aliases = {}
-    if second:
-        in_specs += [any_spec(), tile_spec, tile_spec]
-        operands += list(earlier)
-        aliases = {4: 0}
+    operands = [plane, popul, sums, pre, halo] + (list(earlier) if second else [])
     return pl.pallas_call(
         functools.partial(collide_kernel, second),
-        grid_spec=pltpu.PrefetchScalarGridSpec(
-            num_scalar_prefetch=1,
-            grid=(height // block,),
-            in_specs=in_specs,
-            out_specs=(
-                plane_spec(19),
-                pl.BlockSpec((8, block, width), lambda g, s: (0, g, 0)),
-                tile_spec,
-                tile_spec,
-            ),
-        ),
+        in_specs=[pl.BlockSpec(memory_space=pltpu.SMEM)] + [vmem_spec()] * (len(operands) - 1),
+        out_specs=(vmem_spec(),) * 4,
         out_shape=(
             jax.ShapeDtypeStruct(popul.shape, F32),
             jax.ShapeDtypeStruct((8, height, width), F32),
             tile,
             tile,
         ),
-        input_output_aliases=aliases,
+        input_output_aliases={5: 0} if second else {},
         compiler_params=params(),
         name="collide_odd" if second else "collide_even",
     )(*operands)
@@ -355,6 +390,8 @@
     conf_tall,
     velo_tall,
     halo,
+    shifted,
+    sems,
 ):
     height, width = conf_ref.shape[2:]
     planes = (planes_ref[0], planes_ref[1])
@@ -382,6 +419,38 @@
         return jnp.where(
             even_first, rolled(pack, target - when_first), rolled(pack, target - otherwise)
         )
+
+    copies = []
+    full_low = low_ref[...]
+    full_high = high_ref[...]
+    lane = lanes_of(full_low)
+    for i in range(19):
+        step_x, step_y, step_z = VELOCITIES[i]
+        for p in range(2):
+            q = p - step_x
+            if q not in (0, 1):
+                continue
+            tile = post_ref.at[i, q]
+            if step_y or step_z:
+                value = post_ref[i, q]
+                if step_z == 1:
+                    edge = edge_value(full_low, q, 3 + Z_UP.index(i), 0)
+                    value = jnp.where(lane == 0, edge, rolled(value, 1))
+                elif step_z == -1:
+                    edge = edge_value(full_high, q, 3 + Z_DOWN.index(i), width - 1)
+                    value = jnp.where(lane == width - 1, edge, rolled(value, -1))
+                back = OPPOSITE[i]
+                tile = shifted.at[i, p]
+                if step_y == 1:
+                    tile[1:height, :] = value[: height - 1]
+                    tile[0:1, :] = post_ref[back, p, 0:1, :]
+                elif step_y == -1:
+                    tile[0 : height - 1, :] = value[1:]
+                    tile[height - 1 : height, :] = post_ref[back, p, height - 1 : height, :]
+                else:
+                    tile[...] = value
+            copies.append(pltpu.make_async_copy(tile, read_ref.at[i, p], sems.at[len(copies)]))
+            copies[-1].start()
 
     for p in range(2):
         sign = 2 * p - 1
@@ -446,32 +515,8 @@
                 )
 
         for_rows(height, rows)
-
-    full_low = low_ref[...]
-    full_high = high_ref[...]
-    lane = lanes_of(full_low)
-    for i in range(19):
-        step_x, step_y, step_z = VELOCITIES[i]
-        for p in range(2):
-            q = p - step_x
-            if q not in (0, 1):
-                continue
-            value = post_ref[i, q]
-            if step_z == 1:
-                edge = edge_value(full_low, q, 3 + Z_UP.index(i), 0)
-                value = jnp.where(lane == 0, edge, rolled(value, 1))
-            elif step_z == -1:
-                edge = edge_value(full_high, q, 3 + Z_DOWN.index(i), width - 1)
-                value = jnp.where(lane == width - 1, edge, rolled(value, -1))
-            back = OPPOSITE[i]
-            if step_y == 1:
-                read_ref[i, p, 1:height, :] = value[: height - 1]
-                read_ref[i, p, 0:1, :] = post_ref[back, p, 0:1, :]
-            elif step_y == -1:
-                read_ref[i, p, 0 : height - 1, :] = value[1:]
-                read_ref[i, p, height - 1 : height, :] = post_ref[back, p, height - 1 : height, :]
-            else:
-                read_ref[i, p] = value
+    for copy in copies:
+        copy.wait()
 
 
 def inner(planes, conform, halo_e, halo_o, conf_low, conf_high, low, high, post, velo_e, velo_o):
@@ -498,11 +543,13 @@
             velo_spec,
             velo_spec,
         ],
-        out_specs=(whole(post.shape), whole(conform.shape)),
+        out_specs=(any_spec(), whole(conform.shape)),
         scratch_shapes=[
             VMEM((6, 2, height + 16, width), F32),
             VMEM((3, 2, height + 16, width), F32),
             VMEM((2, 6, height, width), F32),
+            VMEM(post.shape, F32),
+            pltpu.SemaphoreType.DMA((28,)),
         ],
         compiler_params=params(),
         name="inner",
@@ -627,16 +674,19 @@
     up = [(i, (i + 1) % narrow) for i in range(narrow)]
     down = [(j, i) for i, j in up]
 
-    near = lax.dynamic_index_in_dim(conform, plane_e[0], axis=1, keepdims=False)
+    conform, near = load(plane_e, conform)
     halo_e = lax.ppermute(near, "wide", even_pairs)
-    conf_up, conf_down, far = edges(plane_o, conform)
-    halo_o = lax.ppermute(far, "wide", odd_pairs)
+    conf_up, conf_down = edges(conform)
     conf_low = lax.ppermute(conf_up, "narrow", up)
     conf_high = lax.ppermute(conf_down, "narrow", down)
-    pre = prepare(conform, popul, conf_low, conf_high)
-    post, sent_e, z_up, z_down = collide(plane_e, popul, pre, halo_e)
+    popul, sums, far = moments(plane_o, popul, conform, conf_up)
+    halo_o = lax.ppermute(far, "wide", odd_pairs)
+    pre = prepare(conform, conf_low, conf_high)
+    post, sent_e, z_up, z_down = collide(plane_e, popul, sums, pre, halo_e)
     got_e = lax.ppermute(sent_e, "wide", even_pairs)
-    post, sent_o, z_up, z_down = collide(plane_o, popul, pre, halo_o, (post, z_up, z_down))
+    post, sent_o, z_up, z_down = collide(
+        plane_o, popul, sums, pre, halo_o, (post, z_up, z_down)
+    )
     got_o = lax.ppermute(sent_o, "wide", odd_pairs)
     low = lax.ppermute(z_up, "narrow", up)
     high = lax.ppermute(z_down, "narrow", down)

time: 54.2 us -> 50.4 us (0.930)
  Pallas kernels: 20.7 us -> 9.96 us
  waiting for transfers between devices: 9.86 us -> 19.1 us
  local copies, waits for them, and re-layouts: 5 us -> 2.82 us
    pallas_call x4 -> x6, Pallas kernels: 11.7 us -> 4.1 us  [the longest x2 1.7 us: collide(): pl.pallas_call(functools.partial(collide_kernel, second), in_specs=[pl.Bl...]
    ppermute x1, waiting for transfers between devices: 4.32 us -> 8.99 us  [body(): corner_e = lax.ppermute(corner_e, 'wide', even_pairs)]
    ppermute x1, waiting for transfers between devices: 1.63 us -> 6.21 us  [body(): halo_e = lax.ppermute(near, 'wide', even_pairs)]
    pallas_call x1, Pallas kernels: 6.64 us -> 3.68 us  [inner(): pl.pallas_call(inner_kernel, grid=(1,), out_shape=(jax.ShapeDtypeStruct(p...]
    unnamed x8 -> x4, local copies, waits for them, and re-layouts: 3.97 us -> 2.82 us
    squeeze x1 -> x0, local copies, waits for them, and re-layouts: 1.03 us -> none  [body(): near = lax.dynamic_index_in_dim(conform, plane_e[0], axis=1, keepdims=False)]
  transfers between devices with their start and end apart: 10 -> 10, of which waited for: 4 -> 4; matrix products, arithmetic and copies ran while one was open for 0% -> 0% of each run, Pallas kernels for 36% -> 18%
where the time goes in v2:
time: 50.4 us; the launch traced here: 50.2 us
  waiting for transfers between devices  19.1 us (38%)
  starting transfers between devices  17.5 us (35%)
  Pallas kernels  9.96 us (20%)
  local copies, waits for them, and re-layouts  2.82 us (6%)
  between operations  0.75 us (1%)
    ppermute x1, waiting for transfers between devices, body(): corner_e = lax.ppermute(corner_e, 'wide', even_pairs)  8.99 us
    ppermute x1, waiting for transfers between devices, body(): halo_e = lax.ppermute(near, 'wide', even_pairs)  6.21 us
    pallas_call x1, Pallas kernels, inner(): pl.pallas_call(inner_kernel, grid=(1,), out_shape=(jax.ShapeDtypeStruct(p...  3.68 us
    ppermute x1, starting transfers between devices, body(): got_o = lax.ppermute(sent_o, 'wide', odd_pairs)  3.61 us
    ppermute x1, starting transfers between devices, body(): halo_o = lax.ppermute(far, 'wide', odd_pairs)  3.61 us
    ppermute x1, starting transfers between devices, body(): halo_e = lax.ppermute(near, 'wide', even_pairs)  3.03 us
    unnamed x4, local copies, waits for them, and re-layouts  2.82 us
    pallas_call x2, Pallas kernels, finish(): pl.pallas_call(functools.partial(finish_kernel, second), grid_spec=pltpu....  2.12 us
  transfers between devices with their start and end apart: 10, of which 4 were waited for; matrix products, arithmetic and copies ran while one was open for 0% of the time, Pallas kernels for 18%

profile of v2, /device:TPU:0, one launch (start us, length us, event | category | flops | bytes accessed | tf_op | source)
XLA Modules:
  0.0 50.2 jit_solution(13614609667286011844)
XLA Ops:
  0.6 0.0 copy-start.1
  0.6 1.1 %copy-done.1 = f32[6,2,128,128]{3,2,1,0:T(8,128)S(1)} copy-done((f32[6,2,128,128]{3,2,1,0:T(8,128)S(1)}, f32[6,2,128,128]{3,2,1,0:T(8,128)}, u32[]{:S(2)}) %copy-start.1) | copy-done | bytes 786456
  1.8 0.1 load.1
  1.9 3.0 %collective-permute-start = (f32[6,128,128]{2,1,0:T(8,128)S(1)}, f32[6,128,128]{2,1,0:T(8,128)S(1)}, u32[]{:S(2)}, u32[]{:S(2)}) collective-permute-start(f32[6,128,128]{2,1,0:T(8,128)S(1)} %get-tuple-element.24), channel_id=1, source_target_pairs={{0,4},{4,0},{8,12},{12,8},{16,20},{20,16},{24,28},{28,24},{1,5},{5... | collective-permute-start | bytes 1179656 | tf_op jit(solution)/shard_map/ppermute | solution.py:678
  4.9 0.6 %edges.1 = (f32[128,128]{1,0:T(8,128)S(1)}, f32[128,128]{1,0:T(8,128)S(1)}) custom-call(f32[6,2,128,128]{3,2,1,0:T(8,128)S(1)} %get-tuple-element.23.conf_ref), custom_call_target="tpu_custom_call" | custom-call | tf_op jit(solution)/shard_map/edges/pallas_call | solution.py:140
  5.6 0.0 copy-start
  5.6 1.7 %copy-done = f32[19,2,128,128]{3,2,1,0:T(8,128)S(1)} copy-done((f32[19,2,128,128]{3,2,1,0:T(8,128)S(1)}, f32[19,2,128,128]{3,2,1,0:T(8,128)}, u32[]{:S(2)}) %copy-start) | copy-done | bytes 2490392
  7.3 0.5 moments.1
  7.8 3.6 %collective-permute-start.1 = (f32[6,128,128]{2,1,0:T(8,128)S(1)}, f32[6,128,128]{2,1,0:T(8,128)S(1)}, u32[]{:S(2)}, u32[]{:S(2)}) collective-permute-start(f32[6,128,128]{2,1,0:T(8,128)S(1)} %get-tuple-element.26), channel_id=1, source_target_pairs={{0,28},{4,8},{8,4},{12,16},{16,12},{20,24},{24,20},{28,0},{1,29},{... | collective-permute-start | bytes 1179656 | tf_op jit(solution)/shard_map/ppermute | solution.py:683
  11.4 0.0 collective-permute-start.2
  11.4 1.7 %collective-permute-start.3 = (f32[128,128]{1,0:T(8,128)S(1)}, f32[128,128]{1,0:T(8,128)S(1)}, u32[]{:S(2)}, u32[]{:S(2)}) collective-permute-start(f32[128,128]{1,0:T(8,128)S(1)} %get-tuple-element.27), channel_id=1, source_target_pairs={{1,0},{2,1},{3,2},{0,3},{5,4},{6,5},{7,6},{4,7},{9,8},{10,9},{11,1... | collective-permute-start | bytes 196616 | tf_op jit(solution)/shard_map/ppermute | solution.py:681
  13.1 1.9 %collective-permute-done.2.low_ref.conf_low = f32[128,128]{1,0:T(8,128)S(1)} collective-permute-done((f32[128,128]{1,0:T(8,128)S(1)}, f32[128,128]{1,0:T(8,128)S(1)}, u32[]{:S(2)}, u32[]{:S(2)}) %collective-permute-start.2) | collective-permute-done | bytes 65568 | tf_op jit(solution)/shard_map/ppermute | solution.py:680
  15.1 0.0 collective-permute-done.3.high_ref.conf_high
  15.1 1.2 %prepare.1.pre_ref = f32[3,2,128,128]{3,2,1,0:T(8,128)S(1)} custom-call(f32[6,2,128,128]{3,2,1,0:T(8,128)S(1)} %get-tuple-element.23.conf_ref, f32[128,128]{1,0:T(8,128)S(1)} %collective-permute-done.2.low_ref.conf_low, f32[128,128]{1,0:T(8,128)S(1)} %collective-permute-done.3.high_ref.conf_high), custom_call_target="tpu_custom_call" | custom-call | tf_op jit(solution)/shard_map/prepare/pallas_call | solution.py:251
  16.3 6.2 %collective-permute-done.halo_ref.halo_e = f32[6,128,128]{2,1,0:T(8,128)S(1)} collective-permute-done((f32[6,128,128]{2,1,0:T(8,128)S(1)}, f32[6,128,128]{2,1,0:T(8,128)S(1)}, u32[]{:S(2)}, u32[]{:S(2)}) %collective-permute-start) | collective-permute-done | bytes 393248 | tf_op jit(solution)/shard_map/ppermute | solution.py:678
  22.5 0.8 %collide_even.1 = (f32[19,2,128,128]{3,2,1,0:T(8,128)S(1)}, f32[8,128,128]{2,1,0:T(8,128)S(1)}, f32[128,128]{1,0:T(8,128)S(1)}, f32[128,128]{1,0:T(8,128)S(1)}) custom-call(s32[1]{0:T(128)} %bitcast.1.near_plane.plane_ref, f32[19,2,128,128]{3,2,1,0:T(8,128)S(1)} %get-tuple-element.28.popul_ref, f32[4,2,128,128]{3,2,1,0:T(8,128)S(1)} %get-tuple-element.29.sums_ref, ...), custom_call_target="tpu_custom_call" | custom-call | tf_op jit(solution)/shard_map/collide_even/pallas_call | solution.py:338
  23.3 1.8 %collective-permute-start.8 = (f32[8,128,128]{2,1,0:T(8,128)S(1)}, f32[8,128,128]{2,1,0:T(8,128)S(1)}, u32[]{:S(2)}, u32[]{:S(2)}) collective-permute-start(f32[8,128,128]{2,1,0:T(8,128)S(1)} %get-tuple-element.36.velo_e.bottom_ref.top_ref), channel_id=1, source_target_pairs={{0,4},{4,0},{8,12},{12,8},{16,20},{20,16},{24,28},{28,24},{1,5},{5... | collective-permute-start | bytes 1572872 | tf_op jit(solution)/shard_map/ppermute | solution.py:686
  25.1 0.0 collective-permute-done.1.halo_ref.halo_o
  25.1 0.9 %collide_odd.1 = (f32[19,2,128,128]{3,2,1,0:T(8,128)S(1)}, f32[8,128,128]{2,1,0:T(8,128)S(1)}, f32[128,128]{1,0:T(8,128)S(1)}, f32[128,128]{1,0:T(8,128)S(1)}) custom-call(s32[1]{0:T(128)} %bitcast.far_plane.plane_ref, f32[19,2,128,128]{3,2,1,0:T(8,128)S(1)} %get-tuple-element.28.popul_ref, ...), custom_call_target="tpu_custom_call", output_to_operand_aliasing={{0}: (5, {})} | custom-call | tf_op jit(solution)/shard_map/collide_odd/pallas_call | solution.py:338
  26.0 3.6 %collective-permute-start.6 = (f32[8,128,128]{2,1,0:T(8,128)S(1)}, f32[8,128,128]{2,1,0:T(8,128)S(1)}, u32[]{:S(2)}, u32[]{:S(2)}) collective-permute-start(f32[8,128,128]{2,1,0:T(8,128)S(1)} %get-tuple-element.37.velo_o.bottom_ref.top_ref), channel_id=1, source_target_pairs={{0,28},{4,8},{8,4},{12,16},{16,12},{20,24},{24,20},{28,0},{1,29},{... | collective-permute-start | bytes 1572872 | tf_op jit(solution)/shard_map/ppermute | solution.py:690
  29.6 0.0 collective-permute-start.4
  29.6 1.7 %collective-permute-start.5 = (f32[128,128]{1,0:T(8,128)S(1)}, f32[128,128]{1,0:T(8,128)S(1)}, u32[]{:S(2)}, u32[]{:S(2)}) collective-permute-start(f32[128,128]{1,0:T(8,128)S(1)} %get-tuple-element.34), channel_id=1, source_target_pairs={{1,0},{2,1},{3,2},{0,3},{5,4},{6,5},{7,6},{4,7},{9,8},{10,9},{11,1... | collective-permute-start | bytes 196616 | tf_op jit(solution)/shard_map/ppermute | solution.py:692
  31.3 1.9 %collective-permute-done.4.low_ref = f32[128,128]{1,0:T(8,128)S(1)} collective-permute-done((f32[128,128]{1,0:T(8,128)S(1)}, f32[128,128]{1,0:T(8,128)S(1)}, u32[]{:S(2)}, u32[]{:S(2)}) %collective-permute-start.4) | collective-permute-done | bytes 65568 | tf_op jit(solution)/shard_map/ppermute | solution.py:691
  33.3 0.0 collective-permute-done.5.high_ref
  33.3 0.1 corners.1
  33.3 0.0 collective-permute-start.9
  33.4 1.9 %collective-permute-start.7 = (f32[16,128]{1,0:T(8,128)S(1)}, f32[16,128]{1,0:T(8,128)S(1)}, u32[]{:S(2)}, u32[]{:S(2)}) collective-permute-start(f32[16,128]{1,0:T(8,128)S(1)} %get-tuple-element.39), channel_id=1, source_target_pairs={{0,28},{4,8},{8,4},{12,16},{16,12},{20,24},{24,20},{28,0},{1,29},{... | collective-permute-start | bytes 24584 | tf_op jit(solution)/shard_map/ppermute | solution.py:695
  35.3 0.1 pad_add_fusion.planes_ref
  35.4 3.7 %inner.1 = (f32[19,2,128,128]{3,2,1,0:T(8,128)}, f32[6,2,128,128]{3,2,1,0:T(8,128)S(1)}) custom-call(s32[2]{0:T(128)S(1)} %pad_add_fusion.planes_ref, f32[6,2,128,128]{3,2,1,0:T(8,128)S(1)} %get-tuple-element.23.conf_ref, f32[6,128,128]{2,1,0:T(8,128)S(1)} %collective-permute-done.halo_ref.halo_e, f32[6,128,128]{2,1,0:T(8,128)S(1)} %collective-permute-done.1.halo_ref.halo_o, ...), custom_call_target="tpu_custom_call" | custom-call | tf_op jit(solution)/shard_map/inner/pallas_call | solution.py:526
  39.1 9.0 %collective-permute-done.9.corner_ref = f32[16,128]{1,0:T(8,128)S(1)} collective-permute-done((f32[16,128]{1,0:T(8,128)S(1)}, f32[16,128]{1,0:T(8,128)S(1)}, u32[]{:S(2)}, u32[]{:S(2)}) %collective-permute-start.9) | collective-permute-done | bytes 8224 | tf_op jit(solution)/shard_map/ppermute | solution.py:694
  48.0 0.0 collective-permute-done.8.got_ref
  48.1 1.1 %finish_even.1 = (f32[19,2,128,128]{3,2,1,0:T(8,128)}, f32[6,2,128,128]{3,2,1,0:T(8,128)}) custom-call(s32[1]{0:T(128)} %bitcast.1.near_plane.plane_ref, f32[6,2,128,128]{3,2,1,0:T(8,128)S(1)} %get-tuple-element.38.part_ref, f32[6,2,128,128]{3,2,1,0:T(8,128)S(1)} %get-tuple-element.23.conf_ref, ...), custom_call_target="tpu_custom_call", output_to_operand_aliasing={{0}: (7, {})} | custom-call | tf_op jit(solution)/shard_map/finish_even/pallas_call | solution.py:643
  49.1 0.0 collective-permute-done.7.corner_ref
  49.1 0.0 collective-permute-done.6.got_ref
  49.1 1.1 %finish_odd.1 = (f32[19,2,128,128]{3,2,1,0:T(8,128)}, f32[6,2,128,128]{3,2,1,0:T(8,128)}) custom-call(s32[1]{0:T(128)} %bitcast.far_plane.plane_ref, f32[6,2,128,128]{3,2,1,0:T(8,128)S(1)} %get-tuple-element.38.part_ref, f32[6,2,128,128]{3,2,1,0:T(8,128)S(1)} %get-tuple-element.23.conf_ref, ...), custom_call_target="tpu_custom_call", output_to_operand_aliasing={{0}: (7, {}), {1}: (8, {})} | custom-call | tf_op jit(solution)/shard_map/finish_odd/pallas_call | solution.py:643
Async XLA Ops:
  0.6 1.1 %copy-start.1 = (f32[6,2,128,128]{3,2,1,0:T(8,128)S(1)}, f32[6,2,128,128]{3,2,1,0:T(8,128)}, u32[]{:S(2)}) copy-start(f32[6,2,128,128]{3,2,1,0:T(8,128)} %conf_hbm.1) | copy-start | bytes 2359300
  1.9 20.6 %collective-permute-start = (f32[6,128,128]{2,1,0:T(8,128)S(1)}, f32[6,128,128]{2,1,0:T(8,128)S(1)}, u32[]{:S(2)}, u32[]{:S(2)}) collective-permute-start(f32[6,128,128]{2,1,0:T(8,128)S(1)} %get-tuple-element.24), channel_id=1, source_target_pairs={{0,4},{4,0},{8,12},{12,8},{16,20},{20,16},{24,28},{28,24},{1,5},{5... | collective-permute-start | bytes 1179656 | tf_op jit(solution)/shard_map/ppermute | solution.py:678
  5.6 1.7 %copy-start = (f32[19,2,128,128]{3,2,1,0:T(8,128)S(1)}, f32[19,2,128,128]{3,2,1,0:T(8,128)}, u32[]{:S(2)}) copy-start(f32[19,2,128,128]{3,2,1,0:T(8,128)} %popul_hbm.1) | copy-start | bytes 7471108
  7.8 17.3 %collective-permute-start.1 = (f32[6,128,128]{2,1,0:T(8,128)S(1)}, f32[6,128,128]{2,1,0:T(8,128)S(1)}, u32[]{:S(2)}, u32[]{:S(2)}) collective-permute-start(f32[6,128,128]{2,1,0:T(8,128)S(1)} %get-tuple-element.26), channel_id=1, source_target_pairs={{0,28},{4,8},{8,4},{12,16},{16,12},{20,24},{24,20},{28,0},{1,29},{... | collective-permute-start | bytes 1179656 | tf_op jit(solution)/shard_map/ppermute | solution.py:683
  11.4 3.7 %collective-permute-start.2 = (f32[128,128]{1,0:T(8,128)S(1)}, f32[128,128]{1,0:T(8,128)S(1)}, u32[]{:S(2)}, u32[]{:S(2)}) collective-permute-start(f32[128,128]{1,0:T(8,128)S(1)} %get-tuple-element.25._), channel_id=1, source_target_pairs={{0,1},{1,2},{2,3},{3,0},{4,5},{5,6},{6,7},{7,4},{8,9},{9,10},{10,1... | collective-permute-start | bytes 196616 | tf_op jit(solution)/shard_map/ppermute | solution.py:680
  11.4 3.7 %collective-permute-start.3 = (f32[128,128]{1,0:T(8,128)S(1)}, f32[128,128]{1,0:T(8,128)S(1)}, u32[]{:S(2)}, u32[]{:S(2)}) collective-permute-start(f32[128,128]{1,0:T(8,128)S(1)} %get-tuple-element.27), channel_id=1, source_target_pairs={{1,0},{2,1},{3,2},{0,3},{5,4},{6,5},{7,6},{4,7},{9,8},{10,9},{11,1... | collective-permute-start | bytes 196616 | tf_op jit(solution)/shard_map/ppermute | solution.py:681
  23.3 24.8 %collective-permute-start.8 = (f32[8,128,128]{2,1,0:T(8,128)S(1)}, f32[8,128,128]{2,1,0:T(8,128)S(1)}, u32[]{:S(2)}, u32[]{:S(2)}) collective-permute-start(f32[8,128,128]{2,1,0:T(8,128)S(1)} %get-tuple-element.36.velo_e.bottom_ref.top_ref), channel_id=1, source_target_pairs={{0,4},{4,0},{8,12},{12,8},{16,20},{20,16},{24,28},{28,24},{1,5},{5... | collective-permute-start | bytes 1572872 | tf_op jit(solution)/shard_map/ppermute | solution.py:686
  26.0 23.2 %collective-permute-start.6 = (f32[8,128,128]{2,1,0:T(8,128)S(1)}, f32[8,128,128]{2,1,0:T(8,128)S(1)}, u32[]{:S(2)}, u32[]{:S(2)}) collective-permute-start(f32[8,128,128]{2,1,0:T(8,128)S(1)} %get-tuple-element.37.velo_o.bottom_ref.top_ref), channel_id=1, source_target_pairs={{0,28},{4,8},{8,4},{12,16},{16,12},{20,24},{24,20},{28,0},{1,29},{... | collective-permute-start | bytes 1572872 | tf_op jit(solution)/shard_map/ppermute | solution.py:690
  29.6 3.7 %collective-permute-start.4 = (f32[128,128]{1,0:T(8,128)S(1)}, f32[128,128]{1,0:T(8,128)S(1)}, u32[]{:S(2)}, u32[]{:S(2)}) collective-permute-start(f32[128,128]{1,0:T(8,128)S(1)} %get-tuple-element.33), channel_id=1, source_target_pairs={{0,1},{1,2},{2,3},{3,0},{4,5},{5,6},{6,7},{7,4},{8,9},{9,10},{10,1... | collective-permute-start | bytes 196616 | tf_op jit(solution)/shard_map/ppermute | solution.py:691
  29.6 3.7 %collective-permute-start.5 = (f32[128,128]{1,0:T(8,128)S(1)}, f32[128,128]{1,0:T(8,128)S(1)}, u32[]{:S(2)}, u32[]{:S(2)}) collective-permute-start(f32[128,128]{1,0:T(8,128)S(1)} %get-tuple-element.34), channel_id=1, source_target_pairs={{1,0},{2,1},{3,2},{0,3},{5,4},{6,5},{7,6},{4,7},{9,8},{10,9},{11,1... | collective-permute-start | bytes 196616 | tf_op jit(solution)/shard_map/ppermute | solution.py:692
  33.3 14.7 %collective-permute-start.9 = (f32[16,128]{1,0:T(8,128)S(1)}, f32[16,128]{1,0:T(8,128)S(1)}, u32[]{:S(2)}, u32[]{:S(2)}) collective-permute-start(f32[16,128]{1,0:T(8,128)S(1)} %get-tuple-element.40), channel_id=1, source_target_pairs={{0,4},{4,0},{8,12},{12,8},{16,20},{20,16},{24,28},{28,24},{1,5},{5... | collective-permute-start | bytes 24584 | tf_op jit(solution)/shard_map/ppermute | solution.py:694
  33.4 15.7 %collective-permute-start.7 = (f32[16,128]{1,0:T(8,128)S(1)}, f32[16,128]{1,0:T(8,128)S(1)}, u32[]{:S(2)}, u32[]{:S(2)}) collective-permute-start(f32[16,128]{1,0:T(8,128)S(1)} %get-tuple-element.39), channel_id=1, source_target_pairs={{0,28},{4,8},{8,4},{12,16},{16,12},{20,24},{24,20},{28,0},{1,29},{... | collective-permute-start | bytes 24584 | tf_op jit(solution)/shard_map/ppermute | solution.py:695

commit v3 on v2

--- a/solution.py
+++ b/solution.py
@@ -47,6 +47,7 @@
 Z_DOWN = tuple(
     VELOCITIES.index(v) for v in ((0, 0, -1), (0, 1, -1), (0, -1, -1), (1, 0, -1), (-1, 0, -1))
 )
+COLUMNS = 16
 ROWS = 32
 F32 = jnp.float32
 VMEM = pltpu.VMEM
@@ -82,6 +83,10 @@
     return packed
 
 
+def spread_columns(ref, width):
+    return jnp.concatenate([ref[...]] * (width // COLUMNS), axis=0).T
+
+
 def for_rows(total, body):
     def step(number, carry):
         body(pl.multiple_of(number * ROWS, ROWS))
@@ -94,16 +99,20 @@
     return (EXTENSION_SQ - 3.0) / (EXTENSION_SQ - (c_xx + c_yy + c_zz))
 
 
-def load_kernel(near_plane, conf_hbm, conf_ref, near_ref, sems):
+def divide(conf_ref, plane, early_ref, late_ref):
+    for number, f in enumerate((0, 3, 4)):
+        early_ref[number] = conf_ref[f, plane]
+    early_ref[3] = conf_ref[1, plane] + conf_ref[2, plane]
+    late_ref[0] = conf_ref[1, plane]
+    late_ref[1] = conf_ref[5, plane]
+
+
+def load_kernel(near_plane, conf_hbm, conf_ref, early_ref, late_ref, sems):
     near = near_plane[0]
-    copies = [
-        pltpu.make_async_copy(conf_hbm.at[:, near], near_ref, sems.at[0]),
-        pltpu.make_async_copy(conf_hbm, conf_ref, sems.at[1]),
-    ]
-    for copy in copies:
-        copy.start()
-    for copy in copies:
-        copy.wait()
+    copy = pltpu.make_async_copy(conf_hbm, conf_ref, sems.at[0])
+    copy.start()
+    copy.wait()
+    divide(conf_ref, near, early_ref, late_ref)
 
 
 def load(near_plane, conform):
@@ -112,50 +121,70 @@
         load_kernel,
         out_shape=(
             jax.ShapeDtypeStruct(shape, F32),
-            jax.ShapeDtypeStruct((shape[0],) + shape[2:], F32),
+            jax.ShapeDtypeStruct((4,) + shape[2:], F32),
+            jax.ShapeDtypeStruct((2,) + shape[2:], F32),
         ),
         in_specs=[pl.BlockSpec(memory_space=pltpu.SMEM), any_spec()],
-        out_specs=(vmem_spec(), vmem_spec()),
-        scratch_shapes=[pltpu.SemaphoreType.DMA((2,))],
+        out_specs=(vmem_spec(),) * 3,
+        scratch_shapes=[pltpu.SemaphoreType.DMA((1,))],
         compiler_params=params(),
         name="load",
     )(near_plane, conform)
 
 
-def edge_kernel(conf_ref, up_ref, down_ref):
+def edge_kernel(conf_ref, up_ref, down_ref, up_tile, down_tile):
     height, width = conf_ref.shape[2:]
 
     def rows(start):
         at = pl.ds(start, ROWS)
         values = [conf_ref[f, p, at, :] for p in range(2) for f in range(6)]
-        up_ref[at, :] = pack_columns(values, width - 1)
-        down_ref[at, :] = pack_columns(values, 0)
+        up_tile[at, :] = pack_columns(values, width - 1)
+        down_tile[at, :] = pack_columns(values, 0)
 
     for_rows(height, rows)
+    up_ref[...] = up_tile[...].T[0:COLUMNS]
+    down_ref[...] = down_tile[...].T[0:COLUMNS]
 
 
 def edges(conform):
     height, width = conform.shape[2:]
-    tile = jax.ShapeDtypeStruct((height, width), F32)
+    out = jax.ShapeDtypeStruct((COLUMNS, height), F32)
     return pl.pallas_call(
         edge_kernel,
-        out_shape=(tile, tile),
+        out_shape=(out, out),
         in_specs=[vmem_spec()],
         out_specs=(vmem_spec(), vmem_spec()),
+        scratch_shapes=[VMEM((height, width), F32)] * 2,
         compiler_params=params(),
         name="edges",
     )(conform)
 
 
-def moments_kernel(far_plane, popul_hbm, conf_ref, _, popul_ref, sums_ref, far_ref, sems):
-    height = conf_ref.shape[2]
+def pick_kernel(far_plane, conf_ref, _, early_ref, late_ref):
+    divide(conf_ref, far_plane[0], early_ref, late_ref)
+
+
+def pick(far_plane, conform, after):
+    shape = conform.shape
+    return pl.pallas_call(
+        pick_kernel,
+        out_shape=(
+            jax.ShapeDtypeStruct((4,) + shape[2:], F32),
+            jax.ShapeDtypeStruct((2,) + shape[2:], F32),
+        ),
+        in_specs=[pl.BlockSpec(memory_space=pltpu.SMEM), vmem_spec(), any_spec()],
+        out_specs=(vmem_spec(),) * 2,
+        compiler_params=params(),
+        name="pick",
+    )(far_plane, conform, after)
+
+
+def moments_kernel(popul_hbm, _, popul_ref, sums_ref, sems):
+    height = popul_ref.shape[2]
     copies = []
     for p in range(2):
         copies.append(pltpu.make_async_copy(popul_hbm.at[:, p], popul_ref.at[:, p], sems.at[p]))
         copies[-1].start()
-    far = far_plane[0]
-    for f in range(6):
-        far_ref[f] = conf_ref[f, far]
     for p in range(2):
         copies[p].wait()
 
@@ -179,25 +208,25 @@
         for_rows(height, rows)
 
 
-def moments(far_plane, popul, conform, after):
-    shape = conform.shape
+def moments(popul, after):
     return pl.pallas_call(
         moments_kernel,
         out_shape=(
             jax.ShapeDtypeStruct(popul.shape, F32),
-            jax.ShapeDtypeStruct((4,) + shape[1:], F32),
-            jax.ShapeDtypeStruct((shape[0],) + shape[2:], F32),
+            jax.ShapeDtypeStruct((4,) + popul.shape[1:], F32),
         ),
-        in_specs=[pl.BlockSpec(memory_space=pltpu.SMEM), any_spec(), vmem_spec(), any_spec()],
-        out_specs=(vmem_spec(),) * 3,
+        in_specs=[any_spec(), any_spec()],
+        out_specs=(vmem_spec(),) * 2,
         scratch_shapes=[pltpu.SemaphoreType.DMA((2,))],
         compiler_params=params(),
         name="moments",
-    )(far_plane, popul, conform, after)
-
-
-def prepare_kernel(conf_ref, low_ref, high_ref, pre_ref, tall):
+    )(popul, after)
+
+
+def prepare_kernel(conf_ref, low_cols, high_cols, pre_ref, tall, low_ref, high_ref):
     height, width = conf_ref.shape[2:]
+    low_ref[...] = spread_columns(low_cols, width)
+    high_ref[...] = spread_columns(high_cols, width)
 
     def stress(fields, at_of):
         trace_parts = [at_of(f) for f in range(3)]
@@ -253,7 +282,8 @@
         out_shape=jax.ShapeDtypeStruct((3, 2, height, width), F32),
         in_specs=[vmem_spec()] * 3,
         out_specs=vmem_spec(),
-        scratch_shapes=[VMEM((3, 2, height + 16, width), F32)],
+        scratch_shapes=[VMEM((3, 2, height + 16, width), F32)]
+        + [VMEM((height, width), F32)] * 2,
         compiler_params=params(),
         name="prepare",
     )(conform, low, high)
@@ -261,7 +291,7 @@
 
 def collide_kernel(second, plane_ref, popul_ref, sums_ref, pre_ref, halo_ref, *refs):
     if second:
-        _, up_in, down_in, post_ref, message_ref, up_ref, down_ref = refs
+        _, up_in, down_in, _, post_ref, message_ref, up_out, down_out, up_ref, down_ref = refs
     else:
         post_ref, message_ref, up_ref, down_ref = refs
     height, width = halo_ref.shape[1:]
@@ -274,9 +304,10 @@
 
     def rows(start):
         at = pl.ds(start, ROWS)
-        halo = [halo_ref[f, at, :] for f in range(5)]
-        peterlin = STRESS_SCALE * peterlin_of(halo[0], halo[1], halo[2])
-        stress = (peterlin * halo[0] - STRESS_SCALE, peterlin * halo[3], peterlin * halo[4])
+        halo = [halo_ref[f, at, :] for f in range(4)]
+        trace = halo[0] + halo[3]
+        peterlin = (STRESS_SCALE * (EXTENSION_SQ - 3.0)) / (EXTENSION_SQ - trace)
+        stress = (peterlin * halo[0] - STRESS_SCALE, peterlin * halo[1], peterlin * halo[2])
         force = [pre_ref[a, plane, at, :] + half_sign * stress[a] for a in range(3)]
         density = sums_ref[0, plane, at, :]
         inverse = 1.0 / density
@@ -328,16 +359,23 @@
         down_ref[at, :] = pack_columns(velocity + [post[i] for i in Z_DOWN], 0, down, base)
 
     for_rows(height, rows)
+    if second:
+        up_out[...] = up_ref[...].T[0:COLUMNS]
+        down_out[...] = down_ref[...].T[0:COLUMNS]
 
 
 def collide(plane, popul, sums, pre, halo, earlier=None):
     height, width = popul.shape[2:]
     second = earlier is not None
-    tile = jax.ShapeDtypeStruct((height, width), F32)
+    tile = jax.ShapeDtypeStruct((COLUMNS, height) if second else (height, width), F32)
     operands = [plane, popul, sums, pre, halo] + (list(earlier) if second else [])
     return pl.pallas_call(
         functools.partial(collide_kernel, second),
-        in_specs=[pl.BlockSpec(memory_space=pltpu.SMEM)] + [vmem_spec()] * (len(operands) - 1),
+        in_specs=[pl.BlockSpec(memory_space=pltpu.SMEM)]
+        + [vmem_spec()] * 7
+        + [any_spec()] * (len(operands) - 8)
+        if second
+        else [pl.BlockSpec(memory_space=pltpu.SMEM)] + [vmem_spec()] * 4,
         out_specs=(vmem_spec(),) * 4,
         out_shape=(
             jax.ShapeDtypeStruct(popul.shape, F32),
@@ -345,24 +383,21 @@
             tile,
             tile,
         ),
+        scratch_shapes=[VMEM((height, width), F32)] * 2 if second else [],
         input_output_aliases={5: 0} if second else {},
         compiler_params=params(),
         name="collide_odd" if second else "collide_even",
     )(*operands)
 
 
-def corner_kernel(low_ref, high_ref, even_ref, odd_ref):
-    low = low_ref[...].T
-    high = high_ref[...].T
-    even_ref[0:8, :] = low[0:8]
-    even_ref[8:16, :] = high[0:8]
-    odd_ref[0:8, :] = low[8:16]
-    odd_ref[8:16, :] = high[8:16]
+def corner_kernel(low_ref, high_ref, first_ref, second_ref):
+    for number, out in enumerate((first_ref, second_ref)):
+        out[0:8, :] = low_ref[8 * number : 8 * number + 8, :]
+        out[8:16, :] = high_ref[8 * number : 8 * number + 8, :]
 
 
 def corners(low, high):
-    height = low.shape[0]
-    out = jax.ShapeDtypeStruct((16, height), F32)
+    out = jax.ShapeDtypeStruct(low.shape, F32)
     return pl.pallas_call(
         corner_kernel,
         out_shape=(out, out),
@@ -374,14 +409,17 @@
 
 
 def inner_kernel(
-    planes_ref,
+    plane_e,
+    plane_o,
     conf_ref,
-    halo_e,
-    halo_o,
-    conf_low,
-    conf_high,
-    low_ref,
-    high_ref,
+    early_e,
+    late_e,
+    early_o,
+    late_o,
+    conf_low_cols,
+    conf_high_cols,
+    low_cols,
+    high_cols,
     post_ref,
     velo_e,
     velo_o,
@@ -391,18 +429,30 @@
     velo_tall,
     halo,
     shifted,
+    conf_low,
+    conf_high,
+    low_ref,
+    high_ref,
     sems,
 ):
     height, width = conf_ref.shape[2:]
-    planes = (planes_ref[0], planes_ref[1])
-    for face, (velo, half) in enumerate(((velo_e, halo_e), (velo_o, halo_o))):
+    conf_low[...] = spread_columns(conf_low_cols, width)
+    conf_high[...] = spread_columns(conf_high_cols, width)
+    low_ref[...] = spread_columns(low_cols, width)
+    high_ref[...] = spread_columns(high_cols, width)
+    planes = (plane_e[0], plane_o[0])
+    for p, early, late in ((planes[0], early_e, late_e), (planes[1], early_o, late_o)):
+        for number, f in enumerate((0, 3, 4)):
+            halo[p, f] = early[number]
+        halo[p, 1] = late[0]
+        halo[p, 2] = early[3] - late[0]
+        halo[p, 5] = late[1]
+    for face, velo in enumerate((velo_e, velo_o)):
         p = planes[face]
         for a in range(3):
             velo_tall[a, p, 8 : 8 + height, :] = velo[a]
             velo_tall[a, p, 7:8, :] = -velo[a, 0:1, :]
             velo_tall[a, p, height + 8 : height + 9, :] = -velo[a, height - 1 : height, :]
-        for f in range(6):
-            halo[p, f] = half[f]
     for p in range(2):
         for f in range(6):
             conf_tall[f, p, 8 : 8 + height, :] = conf_ref[f, p]
@@ -519,7 +569,7 @@
         copy.wait()
 
 
-def inner(planes, conform, halo_e, halo_o, conf_low, conf_high, low, high, post, velo_e, velo_o):
+def inner(plane_e, plane_o, conform, halos, conf_low, conf_high, low, high, post, velo_e, velo_o):
     height, width = conform.shape[2:]
     velo_spec = pl.BlockSpec((3, height, width), lambda g: (0, 0, 0))
     whole = lambda shape: pl.BlockSpec(shape, lambda g: (0,) * len(shape))
@@ -532,9 +582,9 @@
         ),
         in_specs=[
             pl.BlockSpec(memory_space=pltpu.SMEM),
+            pl.BlockSpec(memory_space=pltpu.SMEM),
             whole(conform.shape),
-            whole(halo_e.shape),
-            whole(halo_o.shape),
+            *[whole(halo.shape) for halo in halos],
             whole(conf_low.shape),
             whole(conf_low.shape),
             whole(conf_low.shape),
@@ -549,117 +599,95 @@
             VMEM((3, 2, height + 16, width), F32),
             VMEM((2, 6, height, width), F32),
             VMEM(post.shape, F32),
+            VMEM((height, width), F32),
+            VMEM((height, width), F32),
+            VMEM((height, width), F32),
+            VMEM((height, width), F32),
             pltpu.SemaphoreType.DMA((28,)),
         ],
         compiler_params=params(),
         name="inner",
-    )(planes, conform, halo_e, halo_o, conf_low, conf_high, low, high, post, velo_e, velo_o)
-
-
-def finish_kernel(
-    second,
-    plane_ref,
-    part_ref,
-    conf_ref,
-    got_ref,
-    bottom_ref,
-    top_ref,
-    corner_ref,
-    *refs,
-):
-    if second:
-        _, _, read_ref, new_ref, read_tile, new_tile, sems = refs
+    )(plane_e, plane_o, conform, *halos, conf_low, conf_high, low, high, post, velo_e, velo_o)
+
+
+def finish_kernel(parted, chained, plane_ref, part_ref, conf_ref, corner, *refs):
+    if parted:
+        velo, cross, sent = refs[:3]
+        refs = refs[3:]
     else:
-        _, read_ref, new_ref, read_tile, new_tile, sems = refs
-    height, width = got_ref.shape[1:]
+        got, sent = refs[:2]
+        velo, cross, sent = got.at[0:3], got.at[3:8], sent.at[3:8]
+        refs = refs[2:]
+    read_ref, new_ref, tile, new_tile, sems = refs[2:] if chained else refs[1:]
+    height, width = conf_ref.shape[2:]
     plane = plane_ref[0]
+    copies = []
+
+    def send(source, target):
+        copies.append(pltpu.make_async_copy(source, target, sems.at[len(copies)]))
+        copies[-1].start()
+
+    lane = lax.broadcasted_iota(jnp.int32, (height, width), 1)
+    targets = [
+        read_ref.at[jnp.where(plane == 1, MINUS[slot], PLUS[slot]), plane] for slot in range(5)
+    ]
+    send(cross.at[0], targets[0])
+    tile[0, 1:height, :] = cross[1, 0 : height - 1, :]
+    tile[0, 0:1, :] = sent[2, 0:1, :]
+    send(tile.at[0], targets[1])
+    tile[1, 0 : height - 1, :] = cross[2, 1:height, :]
+    tile[1, height - 1 : height, :] = sent[1, height - 1 : height, :]
+    send(tile.at[1], targets[2])
+    low = jnp.broadcast_to(corner[pl.ds(6 + plane, 1), :], (width, height)).T
+    tile[2] = jnp.where(lane == 0, low, rolled(cross[3], 1))
+    send(tile.at[2], targets[3])
+    high = jnp.broadcast_to(corner[pl.ds(14 + plane, 1), :], (width, height)).T
+    tile[3] = jnp.where(lane == width - 1, high, rolled(cross[4], -1))
+    send(tile.at[3], targets[4])
     half_sign = jnp.where(plane == 1, 0.5, -0.5).astype(F32)
-    copies = []
-
-    def send(slot):
-        target = jnp.where(plane == 1, MINUS[slot], PLUS[slot])
-        copy = pltpu.make_async_copy(
-            read_tile.at[slot], read_ref.at[target, plane], sems.at[slot]
-        )
-        copy.start()
-        copies.append(copy)
-
-    lane = lax.broadcasted_iota(jnp.int32, (height, width), 1)
-    low = jnp.broadcast_to(corner_ref[pl.ds(6 + plane, 1), :], (width, height)).T
-    high = jnp.broadcast_to(corner_ref[pl.ds(14 + plane, 1), :], (width, height)).T
-    read_tile[0] = got_ref[3]
-    send(0)
-    read_tile[1, 1:height, :] = got_ref[4, 0 : height - 1, :]
-    read_tile[1, 0:1, :] = bottom_ref[0, 0:1, :]
-    send(1)
-    read_tile[2, 0 : height - 1, :] = got_ref[5, 1:height, :]
-    read_tile[2, height - 1 : height, :] = top_ref[0, 7:8, :]
-    send(2)
-    read_tile[3] = jnp.where(lane == 0, low, rolled(got_ref[6], 1))
-    send(3)
-    read_tile[4] = jnp.where(lane == width - 1, high, rolled(got_ref[7], -1))
-    send(4)
 
     def rows(start):
         at = pl.ds(start, ROWS)
-        slope = [half_sign * got_ref[a, at, :] for a in range(3)]
-        row = [conf_ref[f, 0, at, :] for f in (0, 3, 4)]
+        slope = [half_sign * velo[a, at, :] for a in range(3)]
+        row = [conf_ref[f, plane, at, :] for f in (0, 3, 4)]
         for f in range(6):
             i, j = COMPONENT_PAIRS[f]
             if i == j:
                 term = 2.0 * (row[i] * slope[j])
             else:
                 term = row[i] * slope[j] + slope[i] * row[j]
-            new_tile[f, at, :] = part_ref[f, 0, at, :] + term
+            new_tile[f, at, :] = part_ref[f, plane, at, :] + term
 
     for_rows(height, rows)
     for f in range(6):
-        copy = pltpu.make_async_copy(new_tile.at[f], new_ref.at[f, plane], sems.at[5 + f])
-        copy.start()
-        copies.append(copy)
+        send(new_tile.at[f], new_ref.at[f, plane])
     for copy in copies:
         copy.wait()
 
 
-def finish(plane, part, conform, got, sent, corner, read, new=None):
+def finish(plane, part, conform, corner, got, read, new=None):
     height, width = conform.shape[2:]
-    second = new is not None
-    plane_spec = pl.BlockSpec((6, 1, height, width), lambda g, s: (0, s[0], 0, 0))
-    in_specs = [
-        plane_spec,
-        plane_spec,
-        pl.BlockSpec((8, height, width), lambda g, s: (0, 0, 0)),
-        pl.BlockSpec((1, 8, width), lambda g, s: (5, 0, 0)),
-        pl.BlockSpec((1, 8, width), lambda g, s: (4, height // 8 - 1, 0)),
-        pl.BlockSpec((16, height), lambda g, s: (0, 0)),
-        any_spec(),
-    ]
-    operands = [plane, part, conform, got, sent, sent, corner, read]
-    aliases = {7: 0}
-    if second:
-        in_specs.append(any_spec())
-        operands.append(new)
-        aliases[8] = 1
-    return pl.pallas_call(
-        functools.partial(finish_kernel, second),
-        grid_spec=pltpu.PrefetchScalarGridSpec(
-            num_scalar_prefetch=1,
-            grid=(1,),
-            in_specs=in_specs,
-            out_specs=(any_spec(), any_spec()),
-            scratch_shapes=[
-                VMEM((5, height, width), F32),
-                VMEM((6, height, width), F32),
-                pltpu.SemaphoreType.DMA((11,)),
-            ],
-        ),
+    chained = new is not None
+    operands = [plane, part, conform, corner, *got, read] + ([new] if chained else [])
+    first = 4 + len(got)
+    return pl.pallas_call(
+        functools.partial(finish_kernel, len(got) == 3, chained),
         out_shape=(
             jax.ShapeDtypeStruct(read.shape, F32),
             jax.ShapeDtypeStruct(conform.shape, F32),
         ),
-        input_output_aliases=aliases,
-        compiler_params=params(),
-        name="finish_odd" if second else "finish_even",
+        in_specs=[pl.BlockSpec(memory_space=pltpu.SMEM)]
+        + [vmem_spec()] * (first - 1)
+        + [any_spec()] * (2 if chained else 1),
+        out_specs=(any_spec(), any_spec()),
+        scratch_shapes=[
+            VMEM((4, height, width), F32),
+            VMEM((6, height, width), F32),
+            pltpu.SemaphoreType.DMA((11,)),
+        ],
+        input_output_aliases={first: 0, first + 1: 1} if chained else {first: 0},
+        compiler_params=params(),
+        name="finish_last" if chained else "finish_first",
     )(*operands)
 
 
@@ -674,18 +702,21 @@
     up = [(i, (i + 1) % narrow) for i in range(narrow)]
     down = [(j, i) for i, j in up]
 
-    conform, near = load(plane_e, conform)
-    halo_e = lax.ppermute(near, "wide", even_pairs)
+    conform, early, late = load(plane_e, conform)
+    early_e = lax.ppermute(early, "wide", even_pairs)
+    late_e = lax.ppermute(late, "wide", even_pairs)
     conf_up, conf_down = edges(conform)
     conf_low = lax.ppermute(conf_up, "narrow", up)
     conf_high = lax.ppermute(conf_down, "narrow", down)
-    popul, sums, far = moments(plane_o, popul, conform, conf_up)
-    halo_o = lax.ppermute(far, "wide", odd_pairs)
+    early, late = pick(plane_o, conform, conf_up)
+    popul, sums = moments(popul, early)
+    early_o = lax.ppermute(early, "wide", odd_pairs)
+    late_o = lax.ppermute(late, "wide", odd_pairs)
     pre = prepare(conform, conf_low, conf_high)
-    post, sent_e, z_up, z_down = collide(plane_e, popul, sums, pre, halo_e)
+    post, sent_e, z_up, z_down = collide(plane_e, popul, sums, pre, early_e)
     got_e = lax.ppermute(sent_e, "wide", even_pairs)
     post, sent_o, z_up, z_down = collide(
-        plane_o, popul, sums, pre, halo_o, (post, z_up, z_down)
+        plane_o, popul, sums, pre, early_o, (post, z_up, z_down, late_e)
     )
     got_o = lax.ppermute(sent_o, "wide", odd_pairs)
     low = lax.ppermute(z_up, "narrow", up)
@@ -694,10 +725,10 @@
     corner_e = lax.ppermute(corner_e, "wide", even_pairs)
     corner_o = lax.ppermute(corner_o, "wide", odd_pairs)
     read, part = inner(
-        jnp.concatenate([plane_e, plane_o]),
+        plane_e,
+        plane_o,
         conform,
-        halo_e,
-        halo_o,
+        (early_e, late_e, early_o, late_o),
         conf_low,
         conf_high,
         low,
@@ -706,8 +737,8 @@
         sent_e,
         sent_o,
     )
-    read, new = finish(plane_e, part, conform, got_e, sent_e, corner_e, read)
-    return finish(plane_o, part, conform, got_o, sent_o, corner_o, read, new)
+    read, new = finish(plane_e, part, conform, corner_e, (got_e, sent_e), read)
+    return finish(plane_o, part, conform, corner_o, (got_o, sent_o), read, new)
 
 
 def solution(mesh):

time: 50.4 us -> 47.6 us (0.944)
  waiting for transfers between devices: 19.1 us -> 13.8 us
  starting transfers between devices: 17.5 us -> 20.3 us
    ppermute x1, waiting for transfers between devices: 8.99 us -> 2.22 us  [body(): corner_e = lax.ppermute(corner_e, 'wide', even_pairs)]
    ppermute x2 -> x4, waiting for transfers between devices: 6.21 us -> 9.48 us  [the longest x1 6.21 us: body(): late_o = lax.ppermute(late, 'wide', odd_pairs)]
    ppermute x1, starting transfers between devices: 1.9 us -> 4.16 us  [body(): corner_o = lax.ppermute(corner_o, 'wide', odd_pairs)]
    ppermute x1, starting transfers between devices: 1.74 us -> 0.37 us  [body(): conf_high = lax.ppermute(conf_down, 'narrow', down)]
    ppermute x1, waiting for transfers between devices: 1.94 us -> 0.77 us  [body(): conf_low = lax.ppermute(conf_up, 'narrow', up)]
    ppermute x1, starting transfers between devices: 1.81 us -> 2.49 us  [body(): got_e = lax.ppermute(sent_e, 'wide', even_pairs)]
    ppermute x1, waiting for transfers between devices: 1.94 us -> 1.33 us  [body(): low = lax.ppermute(z_up, 'narrow', up)]
    ppermute x2 -> x4, starting transfers between devices: 6.64 us -> 7.25 us  [the longest x1 3.61 us: body(): early_o = lax.ppermute(early, 'wide', odd_pairs)]
  transfers between devices with their start and end apart: 10 -> 12, of which waited for: 4 -> 5; matrix products, arithmetic and copies ran while one was open for 0% -> 0% of each run, Pallas kernels for 18% -> 18%
where the time goes in v3:
time: 47.6 us; the launch traced here: 47.4 us
  starting transfers between devices  20.3 us (43%)
  waiting for transfers between devices  13.8 us (29%)
  Pallas kernels  9.68 us (20%)
  local copies, waits for them, and re-layouts  2.83 us (6%)
  between operations  0.74 us (2%)
    ppermute x1, waiting for transfers between devices, body(): late_o = lax.ppermute(late, 'wide', odd_pairs)  6.21 us
    ppermute x1, starting transfers between devices, body(): got_o = lax.ppermute(sent_o, 'wide', odd_pairs)  4.16 us
    ppermute x1, starting transfers between devices, body(): corner_o = lax.ppermute(corner_o, 'wide', odd_pairs)  4.16 us
    ppermute x1, starting transfers between devices, body(): early_o = lax.ppermute(early, 'wide', odd_pairs)  3.61 us
    ppermute x1, waiting for transfers between devices, body(): early_e = lax.ppermute(early, 'wide', even_pairs)  3.27 us
    pallas_call x1, Pallas kernels, inner(): pl.pallas_call(inner_kernel, grid=(1,), out_shape=(jax.ShapeDtypeStruct(p...  3.27 us
    ppermute x1, starting transfers between devices, body(): early_e = lax.ppermute(early, 'wide', even_pairs)  3.03 us
    unnamed x4, local copies, waits for them, and re-layouts  2.83 us
  transfers between devices with their start and end apart: 12, of which 5 were waited for; matrix products, arithmetic and copies ran while one was open for 0% of the time, Pallas kernels for 18%

profile of v3, /device:TPU:0, one launch (start us, length us, event | category | flops | bytes accessed | tf_op | source)
XLA Modules:
  0.0 47.4 jit_solution(5267254959045339528)
XLA Ops:
  0.6 0.0 copy-start.1
  0.6 1.1 %copy-done.1 = f32[6,2,128,128]{3,2,1,0:T(8,128)S(1)} copy-done((f32[6,2,128,128]{3,2,1,0:T(8,128)S(1)}, f32[6,2,128,128]{3,2,1,0:T(8,128)}, u32[]{:S(2)}) %copy-start.1) | copy-done | bytes 786456
  1.8 0.1 load.1
  1.9 3.0 %collective-permute-start = (f32[4,128,128]{2,1,0:T(8,128)S(1)}, f32[4,128,128]{2,1,0:T(8,128)S(1)}, u32[]{:S(2)}, u32[]{:S(2)}) collective-permute-start(f32[4,128,128]{2,1,0:T(8,128)S(1)} %get-tuple-element.26), channel_id=1, source_target_pairs={{0,4},{4,0},{8,12},{12,8},{16,20},{20,16},{24,28},{28,24},{1,5},{5... | collective-permute-start | bytes 786440 | tf_op jit(solution)/shard_map/ppermute | solution.py:706
  4.9 0.7 %edges.1 = (f32[16,128]{1,0:T(8,128)S(1)}, f32[16,128]{1,0:T(8,128)S(1)}) custom-call(f32[6,2,128,128]{3,2,1,0:T(8,128)S(1)} %get-tuple-element.25.conf_ref), custom_call_target="tpu_custom_call" | custom-call | tf_op jit(solution)/shard_map/edges/pallas_call | solution.py:152
  5.7 3.6 %collective-permute-start.2 = (f32[4,128,128]{2,1,0:T(8,128)S(1)}, f32[4,128,128]{2,1,0:T(8,128)S(1)}, u32[]{:S(2)}, u32[]{:S(2)}) collective-permute-start(f32[4,128,128]{2,1,0:T(8,128)S(1)} %get-tuple-element.29._), channel_id=1, source_target_pairs={{0,28},{4,8},{8,4},{12,16},{16,12},{20,24},{24,20},{28,0},{1,29},{... | collective-permute-start | bytes 786440 | tf_op jit(solution)/shard_map/ppermute | solution.py:713
  9.3 0.0 collective-permute-start.1
  9.3 0.4 collective-permute-start.5
  9.6 0.1 collective-permute-start.4
  9.8 0.0 copy-start
  9.8 1.7 %copy-done = f32[19,2,128,128]{3,2,1,0:T(8,128)S(1)} copy-done((f32[19,2,128,128]{3,2,1,0:T(8,128)S(1)}, f32[19,2,128,128]{3,2,1,0:T(8,128)}, u32[]{:S(2)}) %copy-start) | copy-done | bytes 2490392
  11.5 0.4 moments.1
  11.9 0.0 collective-permute-done.5.high_cols.conf_high_cols
  12.0 0.8 %collective-permute-done.4.low_cols.conf_low_cols = f32[16,128]{1,0:T(8,128)S(1)} collective-permute-done((f32[16,128]{1,0:T(8,128)S(1)}, f32[16,128]{1,0:T(8,128)S(1)}, u32[]{:S(2)}, u32[]{:S(2)}) %collective-permute-start.4) | collective-permute-done | bytes 8224 | tf_op jit(solution)/shard_map/ppermute | solution.py:709
  12.7 1.3 %prepare.1.pre_ref = f32[3,2,128,128]{3,2,1,0:T(8,128)S(1)} custom-call(f32[6,2,128,128]{3,2,1,0:T(8,128)S(1)} %get-tuple-element.25.conf_ref, f32[16,128]{1,0:T(8,128)S(1)} %collective-permute-done.4.low_cols.conf_low_cols, f32[16,128]{1,0:T(8,128)S(1)} %collective-permute-done.5.high_cols.conf_high_cols), custom_call_target="tpu_custom_call" | custom-call | tf_op jit(solution)/shard_map/prepare/pallas_call | solution.py:280
  14.0 3.3 %collective-permute-done.halo_ref.early_e = f32[4,128,128]{2,1,0:T(8,128)S(1)} collective-permute-done((f32[4,128,128]{2,1,0:T(8,128)S(1)}, f32[4,128,128]{2,1,0:T(8,128)S(1)}, u32[]{:S(2)}, u32[]{:S(2)}) %collective-permute-start) | collective-permute-done | bytes 262176 | tf_op jit(solution)/shard_map/ppermute | solution.py:706
  17.3 0.8 %collide_even.1 = (f32[19,2,128,128]{3,2,1,0:T(8,128)S(1)}, f32[8,128,128]{2,1,0:T(8,128)S(1)}, f32[128,128]{1,0:T(8,128)S(1)}, f32[128,128]{1,0:T(8,128)S(1)}) custom-call(s32[1]{0:T(128)} %bitcast.1.near_plane.plane_ref.plane_e, f32[19,2,128,128]{3,2,1,0:T(8,128)S(1)} %get-tuple-element.32.popul_ref, f32[4,2,128,128]{3,2,1,0:T(8,128)S(1)} %get-tuple-element.33.sums_ref, ...), custom_call_target="tpu_custom_call" | custom-call | tf_op jit(solution)/shard_map/collide_even/pallas_call | solution.py:372
  18.1 2.5 %collective-permute-start.11 = (f32[8,128,128]{2,1,0:T(8,128)S(1)}, f32[8,128,128]{2,1,0:T(8,128)S(1)}, u32[]{:S(2)}, u32[]{:S(2)}) collective-permute-start(f32[8,128,128]{2,1,0:T(8,128)S(1)} %get-tuple-element.40.velo_e.refs_1_), channel_id=1, source_target_pairs={{0,4},{4,0},{8,12},{12,8},{16,20},{20,16},{24,28},{28,24},{1,5},{5... | collective-permute-start | bytes 1572872 | tf_op jit(solution)/shard_map/ppermute | solution.py:717
  20.6 0.0 collective-permute-done.1.refs_3_.late_e
  20.6 0.0 collective-permute-done.2.halo_ref.early_o
  20.6 0.9 %collide_odd.1 = (f32[19,2,128,128]{3,2,1,0:T(8,128)S(1)}, f32[8,128,128]{2,1,0:T(8,128)S(1)}, f32[16,128]{1,0:T(8,128)S(1)}, f32[16,128]{1,0:T(8,128)S(1)}) custom-call(s32[1]{0:T(128)} %bitcast.far_plane.plane_ref.plane_o, f32[19,2,128,128]{3,2,1,0:T(8,128)S(1)} %get-tuple-element.32.popul_ref, ...), custom_call_target="tpu_custom_call", output_to_operand_aliasing={{0}: (5, {})} | custom-call | tf_op jit(solution)/shard_map/collide_odd/pallas_call | solution.py:372
  21.5 4.2 %collective-permute-start.9 = (f32[8,128,128]{2,1,0:T(8,128)S(1)}, f32[8,128,128]{2,1,0:T(8,128)S(1)}, u32[]{:S(2)}, u32[]{:S(2)}) collective-permute-start(f32[8,128,128]{2,1,0:T(8,128)S(1)} %get-tuple-element.41.velo_o.refs_1_), channel_id=1, source_target_pairs={{0,28},{4,8},{8,4},{12,16},{16,12},{20,24},{24,20},{28,0},{1,29},{... | collective-permute-start | bytes 1572872 | tf_op jit(solution)/shard_map/ppermute | solution.py:721
  25.7 0.6 %collective-permute-start.3 = (f32[2,128,128]{2,1,0:T(8,128)S(1)}, f32[2,128,128]{2,1,0:T(8,128)S(1)}, u32[]{:S(2)}, u32[]{:S(2)}) collective-permute-start(f32[2,128,128]{2,1,0:T(8,128)S(1)} %get-tuple-element.30), channel_id=1, source_target_pairs={{0,28},{4,8},{8,4},{12,16},{16,12},{20,24},{24,20},{28,0},{1,29},{... | collective-permute-start | bytes 393224 | tf_op jit(solution)/shard_map/ppermute | solution.py:714
  26.3 0.0 collective-permute-start.6
  26.3 1.7 %collective-permute-start.7 = (f32[16,128]{1,0:T(8,128)S(1)}, f32[16,128]{1,0:T(8,128)S(1)}, u32[]{:S(2)}, u32[]{:S(2)}) collective-permute-start(f32[16,128]{1,0:T(8,128)S(1)} %get-tuple-element.38), channel_id=1, source_target_pairs={{1,0},{2,1},{3,2},{0,3},{5,4},{6,5},{7,6},{4,7},{9,8},{10,9},{11,1... | collective-permute-start | bytes 24584 | tf_op jit(solution)/shard_map/ppermute | solution.py:723
  28.0 1.3 %collective-permute-done.6.low_cols.low_ref = f32[16,128]{1,0:T(8,128)S(1)} collective-permute-done((f32[16,128]{1,0:T(8,128)S(1)}, f32[16,128]{1,0:T(8,128)S(1)}, u32[]{:S(2)}, u32[]{:S(2)}) %collective-permute-start.6) | collective-permute-done | bytes 8224 | tf_op jit(solution)/shard_map/ppermute | solution.py:722
  29.4 0.0 collective-permute-done.7.high_cols.high_ref
  29.4 0.0 collective-permute-start.10
  29.4 4.2 %collective-permute-start.8 = (f32[16,128]{1,0:T(8,128)S(1)}, f32[16,128]{1,0:T(8,128)S(1)}, u32[]{:S(2)}, u32[]{:S(2)}) collective-permute-start(f32[16,128]{1,0:T(8,128)S(1)} %get-tuple-element.43), channel_id=1, source_target_pairs={{0,28},{4,8},{8,4},{12,16},{16,12},{20,24},{24,20},{28,0},{1,29},{... | collective-permute-start | bytes 24584 | tf_op jit(solution)/shard_map/ppermute | solution.py:726
  33.6 6.2 %collective-permute-done.3.late_o = f32[2,128,128]{2,1,0:T(8,128)S(1)} collective-permute-done((f32[2,128,128]{2,1,0:T(8,128)S(1)}, f32[2,128,128]{2,1,0:T(8,128)S(1)}, u32[]{:S(2)}, u32[]{:S(2)}) %collective-permute-start.3) | collective-permute-done | bytes 131104 | tf_op jit(solution)/shard_map/ppermute | solution.py:714
  39.8 3.3 %inner.1 = (f32[19,2,128,128]{3,2,1,0:T(8,128)}, f32[6,2,128,128]{3,2,1,0:T(8,128)S(1)}) custom-call(s32[1]{0:T(128)} %bitcast.1.near_plane.plane_ref.plane_e, s32[1]{0:T(128)} %bitcast.far_plane.plane_ref.plane_o, f32[6,2,128,128]{3,2,1,0:T(8,128)S(1)} %get-tuple-element.25.conf_ref, f32[4,128,128]{2,1,0:T(8,128)S(1)} %collective-permute-done.halo_ref.early_e, ...), custom_call_target="tpu_custom_call" | custom-call | tf_op jit(solution)/shard_map/inner/pallas_call | solution.py:576
  43.0 2.2 %collective-permute-done.10.corner = f32[16,128]{1,0:T(8,128)S(1)} collective-permute-done((f32[16,128]{1,0:T(8,128)S(1)}, f32[16,128]{1,0:T(8,128)S(1)}, u32[]{:S(2)}, u32[]{:S(2)}) %collective-permute-start.10) | collective-permute-done | bytes 8224 | tf_op jit(solution)/shard_map/ppermute | solution.py:725
  45.3 0.0 collective-permute-done.11.refs_0_
  45.3 1.0 %finish_first.1 = (f32[19,2,128,128]{3,2,1,0:T(8,128)}, f32[6,2,128,128]{3,2,1,0:T(8,128)}) custom-call(s32[1]{0:T(128)} %bitcast.1.near_plane.plane_ref.plane_e, f32[6,2,128,128]{3,2,1,0:T(8,128)S(1)} %get-tuple-element.42.part_ref, f32[6,2,128,128]{3,2,1,0:T(8,128)S(1)} %get-tuple-element.25.conf_ref, ...), custom_call_target="tpu_custom_call", output_to_operand_aliasing={{0}: (6, {})} | custom-call | tf_op jit(solution)/shard_map/finish_first/pallas_call | solution.py:673
  46.3 0.0 collective-permute-done.8.corner
  46.3 0.0 collective-permute-done.9.refs_0_
  46.3 1.1 %finish_last.1 = (f32[19,2,128,128]{3,2,1,0:T(8,128)}, f32[6,2,128,128]{3,2,1,0:T(8,128)}) custom-call(s32[1]{0:T(128)} %bitcast.far_plane.plane_ref.plane_o, f32[6,2,128,128]{3,2,1,0:T(8,128)S(1)} %get-tuple-element.42.part_ref, f32[6,2,128,128]{3,2,1,0:T(8,128)S(1)} %get-tuple-element.25.conf_ref, ...), custom_call_target="tpu_custom_call", output_to_operand_aliasing={{0}: (6, {}), {1}: (7, {})} | custom-call | tf_op jit(solution)/shard_map/finish_last/pallas_call | solution.py:673
  (2 shorter events, 0.1 us)
Async XLA Ops:
  0.6 1.1 %copy-start.1 = (f32[6,2,128,128]{3,2,1,0:T(8,128)S(1)}, f32[6,2,128,128]{3,2,1,0:T(8,128)}, u32[]{:S(2)}) copy-start(f32[6,2,128,128]{3,2,1,0:T(8,128)} %conf_hbm.1) | copy-start | bytes 2359300
  1.9 15.4 %collective-permute-start = (f32[4,128,128]{2,1,0:T(8,128)S(1)}, f32[4,128,128]{2,1,0:T(8,128)S(1)}, u32[]{:S(2)}, u32[]{:S(2)}) collective-permute-start(f32[4,128,128]{2,1,0:T(8,128)S(1)} %get-tuple-element.26), channel_id=1, source_target_pairs={{0,4},{4,0},{8,12},{12,8},{16,20},{20,16},{24,28},{28,24},{1,5},{5... | collective-permute-start | bytes 786440 | tf_op jit(solution)/shard_map/ppermute | solution.py:706
  5.7 14.9 %collective-permute-start.2 = (f32[4,128,128]{2,1,0:T(8,128)S(1)}, f32[4,128,128]{2,1,0:T(8,128)S(1)}, u32[]{:S(2)}, u32[]{:S(2)}) collective-permute-start(f32[4,128,128]{2,1,0:T(8,128)S(1)} %get-tuple-element.29._), channel_id=1, source_target_pairs={{0,28},{4,8},{8,4},{12,16},{16,12},{20,24},{24,20},{28,0},{1,29},{... | collective-permute-start | bytes 786440 | tf_op jit(solution)/shard_map/ppermute | solution.py:713
  9.3 11.3 %collective-permute-start.1 = (f32[2,128,128]{2,1,0:T(8,128)S(1)}, f32[2,128,128]{2,1,0:T(8,128)S(1)}, u32[]{:S(2)}, u32[]{:S(2)}) collective-permute-start(f32[2,128,128]{2,1,0:T(8,128)S(1)} %get-tuple-element.27), channel_id=1, source_target_pairs={{0,4},{4,0},{8,12},{12,8},{16,20},{20,16},{24,28},{28,24},{1,5},{5... | collective-permute-start | bytes 393224 | tf_op jit(solution)/shard_map/ppermute | solution.py:707
  9.3 2.7 %collective-permute-start.5 = (f32[16,128]{1,0:T(8,128)S(1)}, f32[16,128]{1,0:T(8,128)S(1)}, u32[]{:S(2)}, u32[]{:S(2)}) collective-permute-start(f32[16,128]{1,0:T(8,128)S(1)} %get-tuple-element.31), channel_id=1, source_target_pairs={{1,0},{2,1},{3,2},{0,3},{5,4},{6,5},{7,6},{4,7},{9,8},{10,9},{11,1... | collective-permute-start | bytes 24584 | tf_op jit(solution)/shard_map/ppermute | solution.py:710
  9.6 3.1 %collective-permute-start.4 = (f32[16,128]{1,0:T(8,128)S(1)}, f32[16,128]{1,0:T(8,128)S(1)}, u32[]{:S(2)}, u32[]{:S(2)}) collective-permute-start(f32[16,128]{1,0:T(8,128)S(1)} %get-tuple-element.28._), channel_id=1, source_target_pairs={{0,1},{1,2},{2,3},{3,0},{4,5},{5,6},{6,7},{7,4},{8,9},{9,10},{10,1... | collective-permute-start | bytes 24584 | tf_op jit(solution)/shard_map/ppermute | solution.py:709
  9.8 1.7 %copy-start = (f32[19,2,128,128]{3,2,1,0:T(8,128)S(1)}, f32[19,2,128,128]{3,2,1,0:T(8,128)}, u32[]{:S(2)}) copy-start(f32[19,2,128,128]{3,2,1,0:T(8,128)} %popul_hbm.1) | copy-start | bytes 7471108
  18.1 27.2 %collective-permute-start.11 = (f32[8,128,128]{2,1,0:T(8,128)S(1)}, f32[8,128,128]{2,1,0:T(8,128)S(1)}, u32[]{:S(2)}, u32[]{:S(2)}) collective-permute-start(f32[8,128,128]{2,1,0:T(8,128)S(1)} %get-tuple-element.40.velo_e.refs_1_), channel_id=1, source_target_pairs={{0,4},{4,0},{8,12},{12,8},{16,20},{20,16},{24,28},{28,24},{1,5},{5... | collective-permute-start | bytes 1572872 | tf_op jit(solution)/shard_map/ppermute | solution.py:717
  21.5 24.8 %collective-permute-start.9 = (f32[8,128,128]{2,1,0:T(8,128)S(1)}, f32[8,128,128]{2,1,0:T(8,128)S(1)}, u32[]{:S(2)}, u32[]{:S(2)}) collective-permute-start(f32[8,128,128]{2,1,0:T(8,128)S(1)} %get-tuple-element.41.velo_o.refs_1_), channel_id=1, source_target_pairs={{0,28},{4,8},{8,4},{12,16},{16,12},{20,24},{24,20},{28,0},{1,29},{... | collective-permute-start | bytes 1572872 | tf_op jit(solution)/shard_map/ppermute | solution.py:721
  25.7 14.1 %collective-permute-start.3 = (f32[2,128,128]{2,1,0:T(8,128)S(1)}, f32[2,128,128]{2,1,0:T(8,128)S(1)}, u32[]{:S(2)}, u32[]{:S(2)}) collective-permute-start(f32[2,128,128]{2,1,0:T(8,128)S(1)} %get-tuple-element.30), channel_id=1, source_target_pairs={{0,28},{4,8},{8,4},{12,16},{16,12},{20,24},{24,20},{28,0},{1,29},{... | collective-permute-start | bytes 393224 | tf_op jit(solution)/shard_map/ppermute | solution.py:714
  26.3 3.1 %collective-permute-start.6 = (f32[16,128]{1,0:T(8,128)S(1)}, f32[16,128]{1,0:T(8,128)S(1)}, u32[]{:S(2)}, u32[]{:S(2)}) collective-permute-start(f32[16,128]{1,0:T(8,128)S(1)} %get-tuple-element.37), channel_id=1, source_target_pairs={{0,1},{1,2},{2,3},{3,0},{4,5},{5,6},{6,7},{7,4},{8,9},{9,10},{10,1... | collective-permute-start | bytes 24584 | tf_op jit(solution)/shard_map/ppermute | solution.py:722
  26.3 3.1 %collective-permute-start.7 = (f32[16,128]{1,0:T(8,128)S(1)}, f32[16,128]{1,0:T(8,128)S(1)}, u32[]{:S(2)}, u32[]{:S(2)}) collective-permute-start(f32[16,128]{1,0:T(8,128)S(1)} %get-tuple-element.38), channel_id=1, source_target_pairs={{1,0},{2,1},{3,2},{0,3},{5,4},{6,5},{7,6},{4,7},{9,8},{10,9},{11,1... | collective-permute-start | bytes 24584 | tf_op jit(solution)/shard_map/ppermute | solution.py:723
  29.4 15.9 %collective-permute-start.10 = (f32[16,128]{1,0:T(8,128)S(1)}, f32[16,128]{1,0:T(8,128)S(1)}, u32[]{:S(2)}, u32[]{:S(2)}) collective-permute-start(f32[16,128]{1,0:T(8,128)S(1)} %get-tuple-element.44), channel_id=1, source_target_pairs={{0,4},{4,0},{8,12},{12,8},{16,20},{20,16},{24,28},{28,24},{1,5},{5... | collective-permute-start | bytes 24584 | tf_op jit(solution)/shard_map/ppermute | solution.py:725
  29.4 16.9 %collective-permute-start.8 = (f32[16,128]{1,0:T(8,128)S(1)}, f32[16,128]{1,0:T(8,128)S(1)}, u32[]{:S(2)}, u32[]{:S(2)}) collective-permute-start(f32[16,128]{1,0:T(8,128)S(1)} %get-tuple-element.43), channel_id=1, source_target_pairs={{0,28},{4,8},{8,4},{12,16},{16,12},{20,24},{24,20},{28,0},{1,29},{... | collective-permute-start | bytes 24584 | tf_op jit(solution)/shard_map/ppermute | solution.py:726

commit v4 on v3

--- a/solution.py
+++ b/solution.py
@@ -610,85 +610,107 @@
     )(plane_e, plane_o, conform, *halos, conf_low, conf_high, low, high, post, velo_e, velo_o)
 
 
-def finish_kernel(parted, chained, plane_ref, part_ref, conf_ref, corner, *refs):
-    if parted:
-        velo, cross, sent = refs[:3]
-        refs = refs[3:]
-    else:
-        got, sent = refs[:2]
-        velo, cross, sent = got.at[0:3], got.at[3:8], sent.at[3:8]
-        refs = refs[2:]
-    read_ref, new_ref, tile, new_tile, sems = refs[2:] if chained else refs[1:]
+def touch_kernel(_, out_ref):
+    out_ref[...] = jnp.zeros_like(out_ref)
+
+
+def touch(value):
+    return pl.pallas_call(
+        touch_kernel,
+        out_shape=jax.ShapeDtypeStruct((8, 128), F32),
+        in_specs=[any_spec()],
+        out_specs=vmem_spec(),
+        compiler_params=params(),
+        name="touch",
+    )(value)
+
+
+def finish_kernel(
+    plane_e,
+    plane_o,
+    part_ref,
+    conf_ref,
+    got_e,
+    sent_e,
+    corner_e,
+    got_o,
+    sent_o,
+    corner_o,
+    _,
+    __,
+    read_ref,
+    new_ref,
+    read_tile,
+    new_tile,
+    sems,
+):
     height, width = conf_ref.shape[2:]
-    plane = plane_ref[0]
+    faces = ((plane_o[0], got_o, sent_o, corner_o), (plane_e[0], got_e, sent_e, corner_e))
+    lane = lax.broadcasted_iota(jnp.int32, (height, width), 1)
     copies = []
 
     def send(source, target):
         copies.append(pltpu.make_async_copy(source, target, sems.at[len(copies)]))
         copies[-1].start()
 
-    lane = lax.broadcasted_iota(jnp.int32, (height, width), 1)
-    targets = [
-        read_ref.at[jnp.where(plane == 1, MINUS[slot], PLUS[slot]), plane] for slot in range(5)
-    ]
-    send(cross.at[0], targets[0])
-    tile[0, 1:height, :] = cross[1, 0 : height - 1, :]
-    tile[0, 0:1, :] = sent[2, 0:1, :]
-    send(tile.at[0], targets[1])
-    tile[1, 0 : height - 1, :] = cross[2, 1:height, :]
-    tile[1, height - 1 : height, :] = sent[1, height - 1 : height, :]
-    send(tile.at[1], targets[2])
-    low = jnp.broadcast_to(corner[pl.ds(6 + plane, 1), :], (width, height)).T
-    tile[2] = jnp.where(lane == 0, low, rolled(cross[3], 1))
-    send(tile.at[2], targets[3])
-    high = jnp.broadcast_to(corner[pl.ds(14 + plane, 1), :], (width, height)).T
-    tile[3] = jnp.where(lane == width - 1, high, rolled(cross[4], -1))
-    send(tile.at[3], targets[4])
-    half_sign = jnp.where(plane == 1, 0.5, -0.5).astype(F32)
-
-    def rows(start):
-        at = pl.ds(start, ROWS)
-        slope = [half_sign * velo[a, at, :] for a in range(3)]
-        row = [conf_ref[f, plane, at, :] for f in (0, 3, 4)]
-        for f in range(6):
-            i, j = COMPONENT_PAIRS[f]
-            if i == j:
-                term = 2.0 * (row[i] * slope[j])
-            else:
-                term = row[i] * slope[j] + slope[i] * row[j]
-            new_tile[f, at, :] = part_ref[f, plane, at, :] + term
-
-    for_rows(height, rows)
-    for f in range(6):
-        send(new_tile.at[f], new_ref.at[f, plane])
+    for face, (plane, got, sent, corner) in enumerate(faces):
+        half_sign = jnp.where(plane == 1, 0.5, -0.5).astype(F32)
+        tile = read_tile.at[face]
+        targets = [
+            read_ref.at[jnp.where(plane == 1, MINUS[slot], PLUS[slot]), plane] for slot in range(5)
+        ]
+        send(got.at[3], targets[0])
+
+        def rows(start, face=face, plane=plane, half_sign=half_sign, got=got):
+            at = pl.ds(start, ROWS)
+            slope = [half_sign * got[a, at, :] for a in range(3)]
+            row = [conf_ref[f, plane, at, :] for f in (0, 3, 4)]
+            for f in range(6):
+                i, j = COMPONENT_PAIRS[f]
+                if i == j:
+                    term = 2.0 * (row[i] * slope[j])
+                else:
+                    term = row[i] * slope[j] + slope[i] * row[j]
+                new_tile[face, f, at, :] = part_ref[f, plane, at, :] + term
+
+        for_rows(height, rows)
+        send(new_tile.at[face], new_ref.at[:, plane])
+        tile[0, 1:height, :] = got[4, 0 : height - 1, :]
+        tile[0, 0:1, :] = sent[5, 0:1, :]
+        send(tile.at[0], targets[1])
+        tile[1, 0 : height - 1, :] = got[5, 1:height, :]
+        tile[1, height - 1 : height, :] = sent[4, height - 1 : height, :]
+        send(tile.at[1], targets[2])
+        low = jnp.broadcast_to(corner[pl.ds(6 + plane, 1), :], (width, height)).T
+        tile[2] = jnp.where(lane == 0, low, rolled(got[6], 1))
+        send(tile.at[2], targets[3])
+        high = jnp.broadcast_to(corner[pl.ds(14 + plane, 1), :], (width, height)).T
+        tile[3] = jnp.where(lane == width - 1, high, rolled(got[7], -1))
+        send(tile.at[3], targets[4])
     for copy in copies:
         copy.wait()
 
 
-def finish(plane, part, conform, corner, got, read, new=None):
+def finish(plane_e, plane_o, part, conform, even, odd, read):
     height, width = conform.shape[2:]
-    chained = new is not None
-    operands = [plane, part, conform, corner, *got, read] + ([new] if chained else [])
-    first = 4 + len(got)
-    return pl.pallas_call(
-        functools.partial(finish_kernel, len(got) == 3, chained),
+    smem = pl.BlockSpec(memory_space=pltpu.SMEM)
+    return pl.pallas_call(
+        finish_kernel,
         out_shape=(
             jax.ShapeDtypeStruct(read.shape, F32),
             jax.ShapeDtypeStruct(conform.shape, F32),
         ),
-        in_specs=[pl.BlockSpec(memory_space=pltpu.SMEM)]
-        + [vmem_spec()] * (first - 1)
-        + [any_spec()] * (2 if chained else 1),
+        in_specs=[smem] * 2 + [vmem_spec()] * 8 + [any_spec()] * 2,
         out_specs=(any_spec(), any_spec()),
         scratch_shapes=[
-            VMEM((4, height, width), F32),
-            VMEM((6, height, width), F32),
-            pltpu.SemaphoreType.DMA((11,)),
+            VMEM((2, 4, height, width), F32),
+            VMEM((2, 6, height, width), F32),
+            pltpu.SemaphoreType.DMA((12,)),
         ],
-        input_output_aliases={first: 0, first + 1: 1} if chained else {first: 0},
-        compiler_params=params(),
-        name="finish_last" if chained else "finish_first",
-    )(*operands)
+        input_output_aliases={10: 0},
+        compiler_params=params(),
+        name="finish",
+    )(plane_e, plane_o, part, conform, *even, *odd, read, touch(even[0]))
 
 
 def body(popul, conform):
@@ -737,8 +759,9 @@
         sent_e,
         sent_o,
     )
-    read, new = finish(plane_e, part, conform, corner_e, (got_e, sent_e), read)
-    return finish(plane_o, part, conform, corner_o, (got_o, sent_o), read, new)
+    even = (got_e, sent_e, corner_e)
+    odd = (got_o, sent_o, corner_o)
+    return finish(plane_e, plane_o, part, conform, even, odd, read)
 
 
 def solution(mesh):

time: 47.6 us -> 46.7 us (0.981)
  Pallas kernels: 9.68 us -> 8.84 us
    ppermute x1, waiting for transfers between devices: 2.22 us -> 0.09 us  [body(): corner_e = lax.ppermute(corner_e, 'wide', even_pairs)]
    ppermute x1, waiting for transfers between devices: 0.01 us -> 2.13 us  [body(): got_e = lax.ppermute(sent_e, 'wide', even_pairs)]
    pallas_call x2, Pallas kernels: 2.1 us -> 1.26 us  [the longest x1 1.26 us: finish(): pl.pallas_call(finish_kernel, out_shape=(jax.ShapeDtypeStruct(read.shape,...]
  transfers between devices with their start and end apart: 12 -> 12, of which waited for: 5 -> 6; matrix products, arithmetic and copies ran while one was open for 0% -> 0% of each run, Pallas kernels for 18% -> 16%
where the time goes in v4:
time: 46.7 us; the launch traced here: 46.5 us
  starting transfers between devices  20.3 us (43%)
  waiting for transfers between devices  13.8 us (30%)
  Pallas kernels  8.84 us (19%)
  local copies, waits for them, and re-layouts  2.83 us (6%)
  between operations  0.71 us (2%)
    ppermute x1, waiting for transfers between devices, body(): late_o = lax.ppermute(late, 'wide', odd_pairs)  6.21 us
    ppermute x1, starting transfers between devices, body(): got_o = lax.ppermute(sent_o, 'wide', odd_pairs)  4.15 us
    ppermute x1, starting transfers between devices, body(): corner_o = lax.ppermute(corner_o, 'wide', odd_pairs)  4.14 us
    ppermute x1, starting transfers between devices, body(): early_o = lax.ppermute(early, 'wide', odd_pairs)  3.61 us
    ppermute x1, waiting for transfers between devices, body(): early_e = lax.ppermute(early, 'wide', even_pairs)  3.27 us
    pallas_call x1, Pallas kernels, inner(): pl.pallas_call(inner_kernel, grid=(1,), out_shape=(jax.ShapeDtypeStruct(p...  3.27 us
    ppermute x1, starting transfers between devices, body(): early_e = lax.ppermute(early, 'wide', even_pairs)  3.03 us
    unnamed x4, local copies, waits for them, and re-layouts  2.83 us
  transfers between devices with their start and end apart: 12, of which 6 were waited for; matrix products, arithmetic and copies ran while one was open for 0% of the time, Pallas kernels for 16%

profile of v4, /device:TPU:0, one launch (start us, length us, event | category | flops | bytes accessed | tf_op | source)
XLA Modules:
  0.0 46.5 jit_solution(13758980608149912419)
XLA Ops:
  0.6 0.0 copy-start.1
  0.6 1.1 %copy-done.1 = f32[6,2,128,128]{3,2,1,0:T(8,128)S(1)} copy-done((f32[6,2,128,128]{3,2,1,0:T(8,128)S(1)}, f32[6,2,128,128]{3,2,1,0:T(8,128)}, u32[]{:S(2)}) %copy-start.1) | copy-done | bytes 786456
  1.8 0.1 load.1
  1.9 3.0 %collective-permute-start = (f32[4,128,128]{2,1,0:T(8,128)S(1)}, f32[4,128,128]{2,1,0:T(8,128)S(1)}, u32[]{:S(2)}, u32[]{:S(2)}) collective-permute-start(f32[4,128,128]{2,1,0:T(8,128)S(1)} %get-tuple-element.24), channel_id=1, source_target_pairs={{0,4},{4,0},{8,12},{12,8},{16,20},{20,16},{24,28},{28,24},{1,5},{5... | collective-permute-start | bytes 786440 | tf_op jit(solution)/shard_map/ppermute | solution.py:728
  4.9 0.7 %edges.1 = (f32[16,128]{1,0:T(8,128)S(1)}, f32[16,128]{1,0:T(8,128)S(1)}) custom-call(f32[6,2,128,128]{3,2,1,0:T(8,128)S(1)} %get-tuple-element.23.conf_ref), custom_call_target="tpu_custom_call" | custom-call | tf_op jit(solution)/shard_map/edges/pallas_call | solution.py:152
  5.7 3.6 %collective-permute-start.2 = (f32[4,128,128]{2,1,0:T(8,128)S(1)}, f32[4,128,128]{2,1,0:T(8,128)S(1)}, u32[]{:S(2)}, u32[]{:S(2)}) collective-permute-start(f32[4,128,128]{2,1,0:T(8,128)S(1)} %get-tuple-element.27._), channel_id=1, source_target_pairs={{0,28},{4,8},{8,4},{12,16},{16,12},{20,24},{24,20},{28,0},{1,29},{... | collective-permute-start | bytes 786440 | tf_op jit(solution)/shard_map/ppermute | solution.py:735
  9.3 0.0 collective-permute-start.1
  9.3 0.4 collective-permute-start.5
  9.6 0.1 collective-permute-start.4
  9.8 0.0 copy-start
  9.8 1.7 %copy-done = f32[19,2,128,128]{3,2,1,0:T(8,128)S(1)} copy-done((f32[19,2,128,128]{3,2,1,0:T(8,128)S(1)}, f32[19,2,128,128]{3,2,1,0:T(8,128)}, u32[]{:S(2)}) %copy-start) | copy-done | bytes 2490392
  11.5 0.4 moments.1
  11.9 0.0 collective-permute-done.5.high_cols.conf_high_cols
  12.0 0.8 %collective-permute-done.4.low_cols.conf_low_cols = f32[16,128]{1,0:T(8,128)S(1)} collective-permute-done((f32[16,128]{1,0:T(8,128)S(1)}, f32[16,128]{1,0:T(8,128)S(1)}, u32[]{:S(2)}, u32[]{:S(2)}) %collective-permute-start.4) | collective-permute-done | bytes 8224 | tf_op jit(solution)/shard_map/ppermute | solution.py:731
  12.7 1.3 %prepare.1.pre_ref = f32[3,2,128,128]{3,2,1,0:T(8,128)S(1)} custom-call(f32[6,2,128,128]{3,2,1,0:T(8,128)S(1)} %get-tuple-element.23.conf_ref, f32[16,128]{1,0:T(8,128)S(1)} %collective-permute-done.4.low_cols.conf_low_cols, f32[16,128]{1,0:T(8,128)S(1)} %collective-permute-done.5.high_cols.conf_high_cols), custom_call_target="tpu_custom_call" | custom-call | tf_op jit(solution)/shard_map/prepare/pallas_call | solution.py:280
  14.0 3.3 %collective-permute-done.halo_ref.early_e = f32[4,128,128]{2,1,0:T(8,128)S(1)} collective-permute-done((f32[4,128,128]{2,1,0:T(8,128)S(1)}, f32[4,128,128]{2,1,0:T(8,128)S(1)}, u32[]{:S(2)}, u32[]{:S(2)}) %collective-permute-start) | collective-permute-done | bytes 262176 | tf_op jit(solution)/shard_map/ppermute | solution.py:728
  17.3 0.8 %collide_even.1 = (f32[19,2,128,128]{3,2,1,0:T(8,128)S(1)}, f32[8,128,128]{2,1,0:T(8,128)S(1)}, f32[128,128]{1,0:T(8,128)S(1)}, f32[128,128]{1,0:T(8,128)S(1)}) custom-call(s32[1]{0:T(128)} %bitcast.near_plane.plane_ref.plane_e, f32[19,2,128,128]{3,2,1,0:T(8,128)S(1)} %get-tuple-element.30.popul_ref, f32[4,2,128,128]{3,2,1,0:T(8,128)S(1)} %get-tuple-element.31.sums_ref, ...), custom_call_target="tpu_custom_call" | custom-call | tf_op jit(solution)/shard_map/collide_even/pallas_call | solution.py:372
  18.1 2.5 %collective-permute-start.8 = (f32[8,128,128]{2,1,0:T(8,128)S(1)}, f32[8,128,128]{2,1,0:T(8,128)S(1)}, u32[]{:S(2)}, u32[]{:S(2)}) collective-permute-start(f32[8,128,128]{2,1,0:T(8,128)S(1)} %get-tuple-element.38.velo_e.sent_e), channel_id=1, source_target_pairs={{0,4},{4,0},{8,12},{12,8},{16,20},{20,16},{24,28},{28,24},{1,5},{5... | collective-permute-start | bytes 1572872 | tf_op jit(solution)/shard_map/ppermute | solution.py:739
  20.6 0.0 collective-permute-done.1.refs_3_.late_e
  20.6 0.0 collective-permute-done.2.halo_ref.early_o
  20.6 0.9 %collide_odd.1 = (f32[19,2,128,128]{3,2,1,0:T(8,128)S(1)}, f32[8,128,128]{2,1,0:T(8,128)S(1)}, f32[16,128]{1,0:T(8,128)S(1)}, f32[16,128]{1,0:T(8,128)S(1)}) custom-call(s32[1]{0:T(128)} %bitcast.1.far_plane.plane_ref.plane_o, f32[19,2,128,128]{3,2,1,0:T(8,128)S(1)} %get-tuple-element.30.popul_ref, ...), custom_call_target="tpu_custom_call", output_to_operand_aliasing={{0}: (5, {})} | custom-call | tf_op jit(solution)/shard_map/collide_odd/pallas_call | solution.py:372
  21.5 4.2 %collective-permute-start.10 = (f32[8,128,128]{2,1,0:T(8,128)S(1)}, f32[8,128,128]{2,1,0:T(8,128)S(1)}, u32[]{:S(2)}, u32[]{:S(2)}) collective-permute-start(f32[8,128,128]{2,1,0:T(8,128)S(1)} %get-tuple-element.39.velo_o.sent_o), channel_id=1, source_target_pairs={{0,28},{4,8},{8,4},{12,16},{16,12},{20,24},{24,20},{28,0},{1,29},{... | collective-permute-start | bytes 1572872 | tf_op jit(solution)/shard_map/ppermute | solution.py:743
  25.7 0.6 %collective-permute-start.3 = (f32[2,128,128]{2,1,0:T(8,128)S(1)}, f32[2,128,128]{2,1,0:T(8,128)S(1)}, u32[]{:S(2)}, u32[]{:S(2)}) collective-permute-start(f32[2,128,128]{2,1,0:T(8,128)S(1)} %get-tuple-element.28), channel_id=1, source_target_pairs={{0,28},{4,8},{8,4},{12,16},{16,12},{20,24},{24,20},{28,0},{1,29},{... | collective-permute-start | bytes 393224 | tf_op jit(solution)/shard_map/ppermute | solution.py:736
  26.3 0.0 collective-permute-start.6
  26.3 1.7 %collective-permute-start.7 = (f32[16,128]{1,0:T(8,128)S(1)}, f32[16,128]{1,0:T(8,128)S(1)}, u32[]{:S(2)}, u32[]{:S(2)}) collective-permute-start(f32[16,128]{1,0:T(8,128)S(1)} %get-tuple-element.36), channel_id=1, source_target_pairs={{1,0},{2,1},{3,2},{0,3},{5,4},{6,5},{7,6},{4,7},{9,8},{10,9},{11,1... | collective-permute-start | bytes 24584 | tf_op jit(solution)/shard_map/ppermute | solution.py:745
  28.0 1.3 %collective-permute-done.6.low_cols.low_ref = f32[16,128]{1,0:T(8,128)S(1)} collective-permute-done((f32[16,128]{1,0:T(8,128)S(1)}, f32[16,128]{1,0:T(8,128)S(1)}, u32[]{:S(2)}, u32[]{:S(2)}) %collective-permute-start.6) | collective-permute-done | bytes 8224 | tf_op jit(solution)/shard_map/ppermute | solution.py:744
  29.4 0.0 collective-permute-done.7.high_cols.high_ref
  29.4 0.0 collective-permute-start.9
  29.4 4.1 %collective-permute-start.11 = (f32[16,128]{1,0:T(8,128)S(1)}, f32[16,128]{1,0:T(8,128)S(1)}, u32[]{:S(2)}, u32[]{:S(2)}) collective-permute-start(f32[16,128]{1,0:T(8,128)S(1)} %get-tuple-element.42), channel_id=1, source_target_pairs={{0,28},{4,8},{8,4},{12,16},{16,12},{20,24},{24,20},{28,0},{1,29},{... | collective-permute-start | bytes 24584 | tf_op jit(solution)/shard_map/ppermute | solution.py:748
  33.6 6.2 %collective-permute-done.3.late_o = f32[2,128,128]{2,1,0:T(8,128)S(1)} collective-permute-done((f32[2,128,128]{2,1,0:T(8,128)S(1)}, f32[2,128,128]{2,1,0:T(8,128)S(1)}, u32[]{:S(2)}, u32[]{:S(2)}) %collective-permute-start.3) | collective-permute-done | bytes 131104 | tf_op jit(solution)/shard_map/ppermute | solution.py:736
  39.8 3.3 %inner.1 = (f32[19,2,128,128]{3,2,1,0:T(8,128)}, f32[6,2,128,128]{3,2,1,0:T(8,128)S(1)}) custom-call(s32[1]{0:T(128)} %bitcast.near_plane.plane_ref.plane_e, s32[1]{0:T(128)} %bitcast.1.far_plane.plane_ref.plane_o, f32[6,2,128,128]{3,2,1,0:T(8,128)S(1)} %get-tuple-element.23.conf_ref, f32[4,128,128]{2,1,0:T(8,128)S(1)} %collective-permute-done.halo_ref.early_e, ...), custom_call_target="tpu_custom_call" | custom-call | tf_op jit(solution)/shard_map/inner/pallas_call | solution.py:576
  43.0 2.1 %collective-permute-done.8._.got_e = f32[8,128,128]{2,1,0:T(8,128)S(1)} collective-permute-done((f32[8,128,128]{2,1,0:T(8,128)S(1)}, f32[8,128,128]{2,1,0:T(8,128)S(1)}, u32[]{:S(2)}, u32[]{:S(2)}) %collective-permute-start.8) | collective-permute-done | bytes 524320 | tf_op jit(solution)/shard_map/ppermute | solution.py:739
  45.2 0.1 collective-permute-done.9.corner_e
  45.3 0.0 collective-permute-done.11.corner_o
  45.3 0.0 collective-permute-done.10.got_o
  45.3 1.3 %finish.1 = (f32[19,2,128,128]{3,2,1,0:T(8,128)}, f32[6,2,128,128]{3,2,1,0:T(8,128)}) custom-call(s32[1]{0:T(128)} %bitcast.near_plane.plane_ref.plane_e, s32[1]{0:T(128)} %bitcast.1.far_plane.plane_ref.plane_o, f32[6,2,128,128]{3,2,1,0:T(8,128)S(1)} %get-tuple-element.40.part_ref, ...), custom_call_target="tpu_custom_call", output_to_operand_aliasing={{0}: (10, {})} | custom-call | tf_op jit(solution)/shard_map/finish/pallas_call | solution.py:697
  (3 shorter events, 0.1 us)
Async XLA Ops:
  0.6 1.1 %copy-start.1 = (f32[6,2,128,128]{3,2,1,0:T(8,128)S(1)}, f32[6,2,128,128]{3,2,1,0:T(8,128)}, u32[]{:S(2)}) copy-start(f32[6,2,128,128]{3,2,1,0:T(8,128)} %conf_hbm.1) | copy-start | bytes 2359300
  1.9 15.4 %collective-permute-start = (f32[4,128,128]{2,1,0:T(8,128)S(1)}, f32[4,128,128]{2,1,0:T(8,128)S(1)}, u32[]{:S(2)}, u32[]{:S(2)}) collective-permute-start(f32[4,128,128]{2,1,0:T(8,128)S(1)} %get-tuple-element.24), channel_id=1, source_target_pairs={{0,4},{4,0},{8,12},{12,8},{16,20},{20,16},{24,28},{28,24},{1,5},{5... | collective-permute-start | bytes 786440 | tf_op jit(solution)/shard_map/ppermute | solution.py:728
  5.7 14.9 %collective-permute-start.2 = (f32[4,128,128]{2,1,0:T(8,128)S(1)}, f32[4,128,128]{2,1,0:T(8,128)S(1)}, u32[]{:S(2)}, u32[]{:S(2)}) collective-permute-start(f32[4,128,128]{2,1,0:T(8,128)S(1)} %get-tuple-element.27._), channel_id=1, source_target_pairs={{0,28},{4,8},{8,4},{12,16},{16,12},{20,24},{24,20},{28,0},{1,29},{... | collective-permute-start | bytes 786440 | tf_op jit(solution)/shard_map/ppermute | solution.py:735
  9.3 11.3 %collective-permute-start.1 = (f32[2,128,128]{2,1,0:T(8,128)S(1)}, f32[2,128,128]{2,1,0:T(8,128)S(1)}, u32[]{:S(2)}, u32[]{:S(2)}) collective-permute-start(f32[2,128,128]{2,1,0:T(8,128)S(1)} %get-tuple-element.25), channel_id=1, source_target_pairs={{0,4},{4,0},{8,12},{12,8},{16,20},{20,16},{24,28},{28,24},{1,5},{5... | collective-permute-start | bytes 393224 | tf_op jit(solution)/shard_map/ppermute | solution.py:729
  9.3 2.7 %collective-permute-start.5 = (f32[16,128]{1,0:T(8,128)S(1)}, f32[16,128]{1,0:T(8,128)S(1)}, u32[]{:S(2)}, u32[]{:S(2)}) collective-permute-start(f32[16,128]{1,0:T(8,128)S(1)} %get-tuple-element.29), channel_id=1, source_target_pairs={{1,0},{2,1},{3,2},{0,3},{5,4},{6,5},{7,6},{4,7},{9,8},{10,9},{11,1... | collective-permute-start | bytes 24584 | tf_op jit(solution)/shard_map/ppermute | solution.py:732
  9.6 3.1 %collective-permute-start.4 = (f32[16,128]{1,0:T(8,128)S(1)}, f32[16,128]{1,0:T(8,128)S(1)}, u32[]{:S(2)}, u32[]{:S(2)}) collective-permute-start(f32[16,128]{1,0:T(8,128)S(1)} %get-tuple-element.26._), channel_id=1, source_target_pairs={{0,1},{1,2},{2,3},{3,0},{4,5},{5,6},{6,7},{7,4},{8,9},{9,10},{10,1... | collective-permute-start | bytes 24584 | tf_op jit(solution)/shard_map/ppermute | solution.py:731
  9.8 1.7 %copy-start = (f32[19,2,128,128]{3,2,1,0:T(8,128)S(1)}, f32[19,2,128,128]{3,2,1,0:T(8,128)}, u32[]{:S(2)}) copy-start(f32[19,2,128,128]{3,2,1,0:T(8,128)} %popul_hbm.1) | copy-start | bytes 7471108
  18.1 27.1 %collective-permute-start.8 = (f32[8,128,128]{2,1,0:T(8,128)S(1)}, f32[8,128,128]{2,1,0:T(8,128)S(1)}, u32[]{:S(2)}, u32[]{:S(2)}) collective-permute-start(f32[8,128,128]{2,1,0:T(8,128)S(1)} %get-tuple-element.38.velo_e.sent_e), channel_id=1, source_target_pairs={{0,4},{4,0},{8,12},{12,8},{16,20},{20,16},{24,28},{28,24},{1,5},{5... | collective-permute-start | bytes 1572872 | tf_op jit(solution)/shard_map/ppermute | solution.py:739
  21.5 23.7 %collective-permute-start.10 = (f32[8,128,128]{2,1,0:T(8,128)S(1)}, f32[8,128,128]{2,1,0:T(8,128)S(1)}, u32[]{:S(2)}, u32[]{:S(2)}) collective-permute-start(f32[8,128,128]{2,1,0:T(8,128)S(1)} %get-tuple-element.39.velo_o.sent_o), channel_id=1, source_target_pairs={{0,28},{4,8},{8,4},{12,16},{16,12},{20,24},{24,20},{28,0},{1,29},{... | collective-permute-start | bytes 1572872 | tf_op jit(solution)/shard_map/ppermute | solution.py:743
  25.7 14.1 %collective-permute-start.3 = (f32[2,128,128]{2,1,0:T(8,128)S(1)}, f32[2,128,128]{2,1,0:T(8,128)S(1)}, u32[]{:S(2)}, u32[]{:S(2)}) collective-permute-start(f32[2,128,128]{2,1,0:T(8,128)S(1)} %get-tuple-element.28), channel_id=1, source_target_pairs={{0,28},{4,8},{8,4},{12,16},{16,12},{20,24},{24,20},{28,0},{1,29},{... | collective-permute-start | bytes 393224 | tf_op jit(solution)/shard_map/ppermute | solution.py:736
  26.3 3.1 %collective-permute-start.6 = (f32[16,128]{1,0:T(8,128)S(1)}, f32[16,128]{1,0:T(8,128)S(1)}, u32[]{:S(2)}, u32[]{:S(2)}) collective-permute-start(f32[16,128]{1,0:T(8,128)S(1)} %get-tuple-element.35), channel_id=1, source_target_pairs={{0,1},{1,2},{2,3},{3,0},{4,5},{5,6},{6,7},{7,4},{8,9},{9,10},{10,1... | collective-permute-start | bytes 24584 | tf_op jit(solution)/shard_map/ppermute | solution.py:744
  26.3 3.1 %collective-permute-start.7 = (f32[16,128]{1,0:T(8,128)S(1)}, f32[16,128]{1,0:T(8,128)S(1)}, u32[]{:S(2)}, u32[]{:S(2)}) collective-permute-start(f32[16,128]{1,0:T(8,128)S(1)} %get-tuple-element.36), channel_id=1, source_target_pairs={{1,0},{2,1},{3,2},{0,3},{5,4},{6,5},{7,6},{4,7},{9,8},{10,9},{11,1... | collective-permute-start | bytes 24584 | tf_op jit(solution)/shard_map/ppermute | solution.py:745
  29.4 15.9 %collective-permute-start.9 = (f32[16,128]{1,0:T(8,128)S(1)}, f32[16,128]{1,0:T(8,128)S(1)}, u32[]{:S(2)}, u32[]{:S(2)}) collective-permute-start(f32[16,128]{1,0:T(8,128)S(1)} %get-tuple-element.41), channel_id=1, source_target_pairs={{0,4},{4,0},{8,12},{12,8},{16,20},{20,16},{24,28},{28,24},{1,5},{5... | collective-permute-start | bytes 24584 | tf_op jit(solution)/shard_map/ppermute | solution.py:747
  29.4 15.9 %collective-permute-start.11 = (f32[16,128]{1,0:T(8,128)S(1)}, f32[16,128]{1,0:T(8,128)S(1)}, u32[]{:S(2)}, u32[]{:S(2)}) collective-permute-start(f32[16,128]{1,0:T(8,128)S(1)} %get-tuple-element.42), channel_id=1, source_target_pairs={{0,28},{4,8},{8,4},{12,16},{16,12},{20,24},{24,20},{28,0},{1,29},{... | collective-permute-start | bytes 24584 | tf_op jit(solution)/shard_map/ppermute | solution.py:748

commit v5 on v4

--- a/solution.py
+++ b/solution.py
@@ -390,22 +390,24 @@
     )(*operands)
 
 
-def corner_kernel(low_ref, high_ref, first_ref, second_ref):
-    for number, out in enumerate((first_ref, second_ref)):
-        out[0:8, :] = low_ref[8 * number : 8 * number + 8, :]
-        out[8:16, :] = high_ref[8 * number : 8 * number + 8, :]
-
-
-def corners(low, high):
-    out = jax.ShapeDtypeStruct(low.shape, F32)
+def corner_kernel(plane_1, plane_2, low_ref, high_ref, first_ref, second_ref):
+    for base, plane, out in ((0, plane_1[0], first_ref), (8, plane_2[0], second_ref)):
+        row = base + 7 - plane
+        out[0:1, :] = low_ref[pl.ds(row, 1), :]
+        out[1:2, :] = high_ref[pl.ds(row, 1), :]
+
+
+def corners(plane_1, plane_2, low, high):
+    out = jax.ShapeDtypeStruct((2, low.shape[1]), F32)
+    smem = pl.BlockSpec(memory_space=pltpu.SMEM)
     return pl.pallas_call(
         corner_kernel,
         out_shape=(out, out),
-        in_specs=[vmem_spec()] * 2,
+        in_specs=[smem, smem, vmem_spec(), vmem_spec()],
         out_specs=(vmem_spec(), vmem_spec()),
         compiler_params=params(),
         name="corners",
-    )(low, high)
+    )(plane_1, plane_2, low, high)
 
 
 def inner_kernel(
@@ -681,10 +683,10 @@
         tile[1, 0 : height - 1, :] = got[5, 1:height, :]
         tile[1, height - 1 : height, :] = sent[4, height - 1 : height, :]
         send(tile.at[1], targets[2])
-        low = jnp.broadcast_to(corner[pl.ds(6 + plane, 1), :], (width, height)).T
+        low = jnp.broadcast_to(corner[0:1, :], (width, height)).T
         tile[2] = jnp.where(lane == 0, low, rolled(got[6], 1))
         send(tile.at[2], targets[3])
-        high = jnp.broadcast_to(corner[pl.ds(14 + plane, 1), :], (width, height)).T
+        high = jnp.broadcast_to(corner[1:2, :], (width, height)).T
         tile[3] = jnp.where(lane == width - 1, high, rolled(got[7], -1))
         send(tile.at[3], targets[4])
     for copy in copies:
@@ -743,7 +745,7 @@
     got_o = lax.ppermute(sent_o, "wide", odd_pairs)
     low = lax.ppermute(z_up, "narrow", up)
     high = lax.ppermute(z_down, "narrow", down)
-    corner_e, corner_o = corners(low, high)
+    corner_e, corner_o = corners(plane_e, plane_o, low, high)
     corner_e = lax.ppermute(corner_e, "wide", even_pairs)
     corner_o = lax.ppermute(corner_o, "wide", odd_pairs)
     read, part = inner(

time: 46.7 us -> 46.4 us (level)
  transfers between devices with their start and end apart: 12 -> 12, of which waited for: 6 -> 5; matrix products, arithmetic and copies ran while one was open for 0% -> 0% of each run, Pallas kernels for 16% -> 16%
where the time goes in v5:
time: 46.4 us; the launch traced here: 46.2 us
  starting transfers between devices  20.3 us (44%)
  waiting for transfers between devices  13.6 us (29%)
  Pallas kernels  8.83 us (19%)
  local copies, waits for them, and re-layouts  2.83 us (6%)
  between operations  0.71 us (2%)
    ppermute x1, waiting for transfers between devices, body(): late_o = lax.ppermute(late, 'wide', odd_pairs)  6.13 us
    ppermute x1, starting transfers between devices, body(): got_o = lax.ppermute(sent_o, 'wide', odd_pairs)  4.15 us
    ppermute x1, starting transfers between devices, body(): corner_o = lax.ppermute(corner_o, 'wide', odd_pairs)  4.15 us
    ppermute x1, starting transfers between devices, body(): early_o = lax.ppermute(early, 'wide', odd_pairs)  3.61 us
    ppermute x1, waiting for transfers between devices, body(): early_e = lax.ppermute(early, 'wide', even_pairs)  3.27 us
    pallas_call x1, Pallas kernels, inner(): pl.pallas_call(inner_kernel, grid=(1,), out_shape=(jax.ShapeDtypeStruct(p...  3.27 us
    ppermute x1, starting transfers between devices, body(): early_e = lax.ppermute(early, 'wide', even_pairs)  3.03 us
    unnamed x4, local copies, waits for them, and re-layouts  2.83 us
  transfers between devices with their start and end apart: 12, of which 5 were waited for; matrix products, arithmetic and copies ran while one was open for 0% of the time, Pallas kernels for 16%

profile of v5, /device:TPU:0, one launch (start us, length us, event | category | flops | bytes accessed | tf_op | source)
XLA Modules:
  0.0 46.2 jit_solution(13200960108127465708)
XLA Ops:
  0.6 0.0 copy-start.1
  0.6 1.1 %copy-done.1 = f32[6,2,128,128]{3,2,1,0:T(8,128)S(1)} copy-done((f32[6,2,128,128]{3,2,1,0:T(8,128)S(1)}, f32[6,2,128,128]{3,2,1,0:T(8,128)}, u32[]{:S(2)}) %copy-start.1) | copy-done | bytes 786456
  1.8 0.1 load.1
  1.9 3.0 %collective-permute-start = (f32[4,128,128]{2,1,0:T(8,128)S(1)}, f32[4,128,128]{2,1,0:T(8,128)S(1)}, u32[]{:S(2)}, u32[]{:S(2)}) collective-permute-start(f32[4,128,128]{2,1,0:T(8,128)S(1)} %get-tuple-element.24), channel_id=1, source_target_pairs={{0,4},{4,0},{8,12},{12,8},{16,20},{20,16},{24,28},{28,24},{1,5},{5... | collective-permute-start | bytes 786440 | tf_op jit(solution)/shard_map/ppermute | solution.py:730
  4.9 0.7 %edges.1 = (f32[16,128]{1,0:T(8,128)S(1)}, f32[16,128]{1,0:T(8,128)S(1)}) custom-call(f32[6,2,128,128]{3,2,1,0:T(8,128)S(1)} %get-tuple-element.23.conf_ref), custom_call_target="tpu_custom_call" | custom-call | tf_op jit(solution)/shard_map/edges/pallas_call | solution.py:152
  5.7 3.6 %collective-permute-start.2 = (f32[4,128,128]{2,1,0:T(8,128)S(1)}, f32[4,128,128]{2,1,0:T(8,128)S(1)}, u32[]{:S(2)}, u32[]{:S(2)}) collective-permute-start(f32[4,128,128]{2,1,0:T(8,128)S(1)} %get-tuple-element.27._), channel_id=1, source_target_pairs={{0,28},{4,8},{8,4},{12,16},{16,12},{20,24},{24,20},{28,0},{1,29},{... | collective-permute-start | bytes 786440 | tf_op jit(solution)/shard_map/ppermute | solution.py:737
  9.3 0.0 collective-permute-start.1
  9.3 0.4 collective-permute-start.5
  9.6 0.1 collective-permute-start.4
  9.8 0.0 copy-start
  9.8 1.7 %copy-done = f32[19,2,128,128]{3,2,1,0:T(8,128)S(1)} copy-done((f32[19,2,128,128]{3,2,1,0:T(8,128)S(1)}, f32[19,2,128,128]{3,2,1,0:T(8,128)}, u32[]{:S(2)}) %copy-start) | copy-done | bytes 2490392
  11.5 0.4 moments.1
  11.9 0.0 collective-permute-done.5.high_cols.conf_high_cols
  12.0 0.8 %collective-permute-done.4.low_cols.conf_low_cols = f32[16,128]{1,0:T(8,128)S(1)} collective-permute-done((f32[16,128]{1,0:T(8,128)S(1)}, f32[16,128]{1,0:T(8,128)S(1)}, u32[]{:S(2)}, u32[]{:S(2)}) %collective-permute-start.4) | collective-permute-done | bytes 8224 | tf_op jit(solution)/shard_map/ppermute | solution.py:733
  12.7 1.3 %prepare.1.pre_ref = f32[3,2,128,128]{3,2,1,0:T(8,128)S(1)} custom-call(f32[6,2,128,128]{3,2,1,0:T(8,128)S(1)} %get-tuple-element.23.conf_ref, f32[16,128]{1,0:T(8,128)S(1)} %collective-permute-done.4.low_cols.conf_low_cols, f32[16,128]{1,0:T(8,128)S(1)} %collective-permute-done.5.high_cols.conf_high_cols), custom_call_target="tpu_custom_call" | custom-call | tf_op jit(solution)/shard_map/prepare/pallas_call | solution.py:280
  14.0 3.3 %collective-permute-done.halo_ref.early_e = f32[4,128,128]{2,1,0:T(8,128)S(1)} collective-permute-done((f32[4,128,128]{2,1,0:T(8,128)S(1)}, f32[4,128,128]{2,1,0:T(8,128)S(1)}, u32[]{:S(2)}, u32[]{:S(2)}) %collective-permute-start) | collective-permute-done | bytes 262176 | tf_op jit(solution)/shard_map/ppermute | solution.py:730
  17.3 0.8 %collide_even.1 = (f32[19,2,128,128]{3,2,1,0:T(8,128)S(1)}, f32[8,128,128]{2,1,0:T(8,128)S(1)}, f32[128,128]{1,0:T(8,128)S(1)}, f32[128,128]{1,0:T(8,128)S(1)}) custom-call(s32[1]{0:T(128)} %bitcast.near_plane.plane_ref.plane_e.plane_1, f32[19,2,128,128]{3,2,1,0:T(8,128)S(1)} %get-tuple-element.30.popul_ref, ...), custom_call_target="tpu_custom_call" | custom-call | tf_op jit(solution)/shard_map/collide_even/pallas_call | solution.py:372
  18.1 2.5 %collective-permute-start.8 = (f32[8,128,128]{2,1,0:T(8,128)S(1)}, f32[8,128,128]{2,1,0:T(8,128)S(1)}, u32[]{:S(2)}, u32[]{:S(2)}) collective-permute-start(f32[8,128,128]{2,1,0:T(8,128)S(1)} %get-tuple-element.38.velo_e.sent_e), channel_id=1, source_target_pairs={{0,4},{4,0},{8,12},{12,8},{16,20},{20,16},{24,28},{28,24},{1,5},{5... | collective-permute-start | bytes 1572872 | tf_op jit(solution)/shard_map/ppermute | solution.py:741
  20.6 0.0 collective-permute-done.1.refs_3_.late_e
  20.6 0.0 collective-permute-done.2.halo_ref.early_o
  20.6 0.9 %collide_odd.1 = (f32[19,2,128,128]{3,2,1,0:T(8,128)S(1)}, f32[8,128,128]{2,1,0:T(8,128)S(1)}, f32[16,128]{1,0:T(8,128)S(1)}, f32[16,128]{1,0:T(8,128)S(1)}) custom-call(s32[1]{0:T(128)} %bitcast.1.far_plane.plane_ref.plane_o.plane_2, f32[19,2,128,128]{3,2,1,0:T(8,128)S(1)} %get-tuple-element.30.popul_ref, ...), custom_call_target="tpu_custom_call", output_to_operand_aliasing={{0}: (5, {})} | custom-call | tf_op jit(solution)/shard_map/collide_odd/pallas_call | solution.py:372
  21.5 4.2 %collective-permute-start.10 = (f32[8,128,128]{2,1,0:T(8,128)S(1)}, f32[8,128,128]{2,1,0:T(8,128)S(1)}, u32[]{:S(2)}, u32[]{:S(2)}) collective-permute-start(f32[8,128,128]{2,1,0:T(8,128)S(1)} %get-tuple-element.39.velo_o.sent_o), channel_id=1, source_target_pairs={{0,28},{4,8},{8,4},{12,16},{16,12},{20,24},{24,20},{28,0},{1,29},{... | collective-permute-start | bytes 1572872 | tf_op jit(solution)/shard_map/ppermute | solution.py:745
  25.7 0.6 %collective-permute-start.3 = (f32[2,128,128]{2,1,0:T(8,128)S(1)}, f32[2,128,128]{2,1,0:T(8,128)S(1)}, u32[]{:S(2)}, u32[]{:S(2)}) collective-permute-start(f32[2,128,128]{2,1,0:T(8,128)S(1)} %get-tuple-element.28), channel_id=1, source_target_pairs={{0,28},{4,8},{8,4},{12,16},{16,12},{20,24},{24,20},{28,0},{1,29},{... | collective-permute-start | bytes 393224 | tf_op jit(solution)/shard_map/ppermute | solution.py:738
  26.3 0.0 collective-permute-start.6
  26.3 1.7 %collective-permute-start.7 = (f32[16,128]{1,0:T(8,128)S(1)}, f32[16,128]{1,0:T(8,128)S(1)}, u32[]{:S(2)}, u32[]{:S(2)}) collective-permute-start(f32[16,128]{1,0:T(8,128)S(1)} %get-tuple-element.36), channel_id=1, source_target_pairs={{1,0},{2,1},{3,2},{0,3},{5,4},{6,5},{7,6},{4,7},{9,8},{10,9},{11,1... | collective-permute-start | bytes 24584 | tf_op jit(solution)/shard_map/ppermute | solution.py:747
  28.0 1.3 %collective-permute-done.6.low_cols.low_ref = f32[16,128]{1,0:T(8,128)S(1)} collective-permute-done((f32[16,128]{1,0:T(8,128)S(1)}, f32[16,128]{1,0:T(8,128)S(1)}, u32[]{:S(2)}, u32[]{:S(2)}) %collective-permute-start.6) | collective-permute-done | bytes 8224 | tf_op jit(solution)/shard_map/ppermute | solution.py:746
  29.4 0.0 collective-permute-done.7.high_cols.high_ref
  29.4 0.0 collective-permute-start.9
  29.4 4.1 %collective-permute-start.11 = (f32[2,128]{1,0:T(2,128)S(1)}, f32[2,128]{1,0:T(2,128)S(1)}, u32[]{:S(2)}, u32[]{:S(2)}) collective-permute-start(f32[2,128]{1,0:T(2,128)S(1)} %get-tuple-element.42), channel_id=1, source_target_pairs={{0,28},{4,8},{8,4},{12,16},{16,12},{20,24},{24,20},{28,0},{1,29},{... | collective-permute-start | bytes 3080 | tf_op jit(solution)/shard_map/ppermute | solution.py:750
  33.6 6.1 %collective-permute-done.3.late_o = f32[2,128,128]{2,1,0:T(8,128)S(1)} collective-permute-done((f32[2,128,128]{2,1,0:T(8,128)S(1)}, f32[2,128,128]{2,1,0:T(8,128)S(1)}, u32[]{:S(2)}, u32[]{:S(2)}) %collective-permute-start.3) | collective-permute-done | bytes 131104 | tf_op jit(solution)/shard_map/ppermute | solution.py:738
  39.7 3.3 %inner.1 = (f32[19,2,128,128]{3,2,1,0:T(8,128)}, f32[6,2,128,128]{3,2,1,0:T(8,128)S(1)}) custom-call(s32[1]{0:T(128)} %bitcast.near_plane.plane_ref.plane_e.plane_1, s32[1]{0:T(128)} %bitcast.1.far_plane.plane_ref.plane_o.plane_2, f32[6,2,128,128]{3,2,1,0:T(8,128)S(1)} %get-tuple-element.23.conf_ref, ...), custom_call_target="tpu_custom_call" | custom-call | tf_op jit(solution)/shard_map/inner/pallas_call | solution.py:578
  43.0 2.0 %collective-permute-done.8._.got_e = f32[8,128,128]{2,1,0:T(8,128)S(1)} collective-permute-done((f32[8,128,128]{2,1,0:T(8,128)S(1)}, f32[8,128,128]{2,1,0:T(8,128)S(1)}, u32[]{:S(2)}, u32[]{:S(2)}) %collective-permute-start.8) | collective-permute-done | bytes 524320 | tf_op jit(solution)/shard_map/ppermute | solution.py:741
  44.9 0.0 collective-permute-done.9.corner_e
  45.0 0.0 collective-permute-done.11.corner_o
  45.0 0.0 collective-permute-done.10.got_o
  45.0 1.2 %finish.1 = (f32[19,2,128,128]{3,2,1,0:T(8,128)}, f32[6,2,128,128]{3,2,1,0:T(8,128)}) custom-call(s32[1]{0:T(128)} %bitcast.near_plane.plane_ref.plane_e.plane_1, s32[1]{0:T(128)} %bitcast.1.far_plane.plane_ref.plane_o.plane_2, f32[6,2,128,128]{3,2,1,0:T(8,128)S(1)} %get-tuple-element.40.part_ref, ...), custom_call_target="tpu_custom_call", output_to_operand_aliasing={{0}: (10, {})} | custom-call | tf_op jit(solution)/shard_map/finish/pallas_call | solution.py:699
  (3 shorter events, 0.1 us)
Async XLA Ops:
  0.6 1.1 %copy-start.1 = (f32[6,2,128,128]{3,2,1,0:T(8,128)S(1)}, f32[6,2,128,128]{3,2,1,0:T(8,128)}, u32[]{:S(2)}) copy-start(f32[6,2,128,128]{3,2,1,0:T(8,128)} %conf_hbm.1) | copy-start | bytes 2359300
  1.9 15.4 %collective-permute-start = (f32[4,128,128]{2,1,0:T(8,128)S(1)}, f32[4,128,128]{2,1,0:T(8,128)S(1)}, u32[]{:S(2)}, u32[]{:S(2)}) collective-permute-start(f32[4,128,128]{2,1,0:T(8,128)S(1)} %get-tuple-element.24), channel_id=1, source_target_pairs={{0,4},{4,0},{8,12},{12,8},{16,20},{20,16},{24,28},{28,24},{1,5},{5... | collective-permute-start | bytes 786440 | tf_op jit(solution)/shard_map/ppermute | solution.py:730
  5.7 14.9 %collective-permute-start.2 = (f32[4,128,128]{2,1,0:T(8,128)S(1)}, f32[4,128,128]{2,1,0:T(8,128)S(1)}, u32[]{:S(2)}, u32[]{:S(2)}) collective-permute-start(f32[4,128,128]{2,1,0:T(8,128)S(1)} %get-tuple-element.27._), channel_id=1, source_target_pairs={{0,28},{4,8},{8,4},{12,16},{16,12},{20,24},{24,20},{28,0},{1,29},{... | collective-permute-start | bytes 786440 | tf_op jit(solution)/shard_map/ppermute | solution.py:737
  9.3 11.3 %collective-permute-start.1 = (f32[2,128,128]{2,1,0:T(8,128)S(1)}, f32[2,128,128]{2,1,0:T(8,128)S(1)}, u32[]{:S(2)}, u32[]{:S(2)}) collective-permute-start(f32[2,128,128]{2,1,0:T(8,128)S(1)} %get-tuple-element.25), channel_id=1, source_target_pairs={{0,4},{4,0},{8,12},{12,8},{16,20},{20,16},{24,28},{28,24},{1,5},{5... | collective-permute-start | bytes 393224 | tf_op jit(solution)/shard_map/ppermute | solution.py:731
  9.3 2.7 %collective-permute-start.5 = (f32[16,128]{1,0:T(8,128)S(1)}, f32[16,128]{1,0:T(8,128)S(1)}, u32[]{:S(2)}, u32[]{:S(2)}) collective-permute-start(f32[16,128]{1,0:T(8,128)S(1)} %get-tuple-element.29), channel_id=1, source_target_pairs={{1,0},{2,1},{3,2},{0,3},{5,4},{6,5},{7,6},{4,7},{9,8},{10,9},{11,1... | collective-permute-start | bytes 24584 | tf_op jit(solution)/shard_map/ppermute | solution.py:734
  9.6 3.1 %collective-permute-start.4 = (f32[16,128]{1,0:T(8,128)S(1)}, f32[16,128]{1,0:T(8,128)S(1)}, u32[]{:S(2)}, u32[]{:S(2)}) collective-permute-start(f32[16,128]{1,0:T(8,128)S(1)} %get-tuple-element.26._), channel_id=1, source_target_pairs={{0,1},{1,2},{2,3},{3,0},{4,5},{5,6},{6,7},{7,4},{8,9},{9,10},{10,1... | collective-permute-start | bytes 24584 | tf_op jit(solution)/shard_map/ppermute | solution.py:733
  9.8 1.7 %copy-start = (f32[19,2,128,128]{3,2,1,0:T(8,128)S(1)}, f32[19,2,128,128]{3,2,1,0:T(8,128)}, u32[]{:S(2)}) copy-start(f32[19,2,128,128]{3,2,1,0:T(8,128)} %popul_hbm.1) | copy-start | bytes 7471108
  18.1 26.8 %collective-permute-start.8 = (f32[8,128,128]{2,1,0:T(8,128)S(1)}, f32[8,128,128]{2,1,0:T(8,128)S(1)}, u32[]{:S(2)}, u32[]{:S(2)}) collective-permute-start(f32[8,128,128]{2,1,0:T(8,128)S(1)} %get-tuple-element.38.velo_e.sent_e), channel_id=1, source_target_pairs={{0,4},{4,0},{8,12},{12,8},{16,20},{20,16},{24,28},{28,24},{1,5},{5... | collective-permute-start | bytes 1572872 | tf_op jit(solution)/shard_map/ppermute | solution.py:741
  21.5 23.5 %collective-permute-start.10 = (f32[8,128,128]{2,1,0:T(8,128)S(1)}, f32[8,128,128]{2,1,0:T(8,128)S(1)}, u32[]{:S(2)}, u32[]{:S(2)}) collective-permute-start(f32[8,128,128]{2,1,0:T(8,128)S(1)} %get-tuple-element.39.velo_o.sent_o), channel_id=1, source_target_pairs={{0,28},{4,8},{8,4},{12,16},{16,12},{20,24},{24,20},{28,0},{1,29},{... | collective-permute-start | bytes 1572872 | tf_op jit(solution)/shard_map/ppermute | solution.py:745
  25.7 14.0 %collective-permute-start.3 = (f32[2,128,128]{2,1,0:T(8,128)S(1)}, f32[2,128,128]{2,1,0:T(8,128)S(1)}, u32[]{:S(2)}, u32[]{:S(2)}) collective-permute-start(f32[2,128,128]{2,1,0:T(8,128)S(1)} %get-tuple-element.28), channel_id=1, source_target_pairs={{0,28},{4,8},{8,4},{12,16},{16,12},{20,24},{24,20},{28,0},{1,29},{... | collective-permute-start | bytes 393224 | tf_op jit(solution)/shard_map/ppermute | solution.py:738
  26.3 3.1 %collective-permute-start.6 = (f32[16,128]{1,0:T(8,128)S(1)}, f32[16,128]{1,0:T(8,128)S(1)}, u32[]{:S(2)}, u32[]{:S(2)}) collective-permute-start(f32[16,128]{1,0:T(8,128)S(1)} %get-tuple-element.35), channel_id=1, source_target_pairs={{0,1},{1,2},{2,3},{3,0},{4,5},{5,6},{6,7},{7,4},{8,9},{9,10},{10,1... | collective-permute-start | bytes 24584 | tf_op jit(solution)/shard_map/ppermute | solution.py:746
  26.3 3.1 %collective-permute-start.7 = (f32[16,128]{1,0:T(8,128)S(1)}, f32[16,128]{1,0:T(8,128)S(1)}, u32[]{:S(2)}, u32[]{:S(2)}) collective-permute-start(f32[16,128]{1,0:T(8,128)S(1)} %get-tuple-element.36), channel_id=1, source_target_pairs={{1,0},{2,1},{3,2},{0,3},{5,4},{6,5},{7,6},{4,7},{9,8},{10,9},{11,1... | collective-permute-start | bytes 24584 | tf_op jit(solution)/shard_map/ppermute | solution.py:747
  29.4 15.6 %collective-permute-start.9 = (f32[2,128]{1,0:T(2,128)S(1)}, f32[2,128]{1,0:T(2,128)S(1)}, u32[]{:S(2)}, u32[]{:S(2)}) collective-permute-start(f32[2,128]{1,0:T(2,128)S(1)} %get-tuple-element.41), channel_id=1, source_target_pairs={{0,4},{4,0},{8,12},{12,8},{16,20},{20,16},{24,28},{28,24},{1,5},{5... | collective-permute-start | bytes 3080 | tf_op jit(solution)/shard_map/ppermute | solution.py:749
  29.4 15.6 %collective-permute-start.11 = (f32[2,128]{1,0:T(2,128)S(1)}, f32[2,128]{1,0:T(2,128)S(1)}, u32[]{:S(2)}, u32[]{:S(2)}) collective-permute-start(f32[2,128]{1,0:T(2,128)S(1)} %get-tuple-element.42), channel_id=1, source_target_pairs={{0,28},{4,8},{8,4},{12,16},{16,12},{20,24},{24,20},{28,0},{1,29},{... | collective-permute-start | bytes 3080 | tf_op jit(solution)/shard_map/ppermute | solution.py:750

commit v6 on v5

--- a/solution.py
+++ b/solution.py
@@ -291,9 +291,9 @@
 
 def collide_kernel(second, plane_ref, popul_ref, sums_ref, pre_ref, halo_ref, *refs):
     if second:
-        _, up_in, down_in, _, post_ref, message_ref, up_out, down_out, up_ref, down_ref = refs
+        _, up_in, down_in, _, post_ref, message_ref, slant_ref, up_out, down_out, up_ref, down_ref = refs
     else:
-        post_ref, message_ref, up_ref, down_ref = refs
+        post_ref, message_ref, slant_ref, up_ref, down_ref = refs
     height, width = halo_ref.shape[1:]
     plane = plane_ref[0]
     outward_plus = plane == 1
@@ -348,9 +348,8 @@
         for a in range(3):
             message_ref[a, at, :] = velocity[a]
         for slot in range(5):
-            message_ref[3 + slot, at, :] = jnp.where(
-                outward_plus, post[PLUS[slot]], post[MINUS[slot]]
-            )
+            out = message_ref.at[3 + slot] if slot < 3 else slant_ref.at[slot - 3]
+            out[at, :] = jnp.where(outward_plus, post[PLUS[slot]], post[MINUS[slot]])
         up = up_in[at, :] if second else None
         down = down_in[at, :] if second else None
         up_ref[at, :] = pack_columns(
@@ -376,10 +375,11 @@
         + [any_spec()] * (len(operands) - 8)
         if second
         else [pl.BlockSpec(memory_space=pltpu.SMEM)] + [vmem_spec()] * 4,
-        out_specs=(vmem_spec(),) * 4,
+        out_specs=(vmem_spec(),) * 5,
         out_shape=(
             jax.ShapeDtypeStruct(popul.shape, F32),
-            jax.ShapeDtypeStruct((8, height, width), F32),
+            jax.ShapeDtypeStruct((6, height, width), F32),
+            jax.ShapeDtypeStruct((2, height, width), F32),
             tile,
             tile,
         ),
@@ -390,24 +390,29 @@
     )(*operands)
 
 
-def corner_kernel(plane_1, plane_2, low_ref, high_ref, first_ref, second_ref):
-    for base, plane, out in ((0, plane_1[0], first_ref), (8, plane_2[0], second_ref)):
-        row = base + 7 - plane
-        out[0:1, :] = low_ref[pl.ds(row, 1), :]
-        out[1:2, :] = high_ref[pl.ds(row, 1), :]
-
-
-def corners(plane_1, plane_2, low, high):
-    out = jax.ShapeDtypeStruct((2, low.shape[1]), F32)
+def slant_kernel(plane_e, plane_o, low_ref, high_ref, slant_e, slant_o, even_ref, odd_ref):
+    height, width = slant_e.shape[1:]
+    lane = lax.broadcasted_iota(jnp.int32, (height, width), 1)
+    faces = ((0, plane_e[0], slant_e, even_ref), (8, plane_o[0], slant_o, odd_ref))
+    for base, plane, slant, out in faces:
+        row = pl.ds(base + 7 - plane, 1)
+        low = jnp.broadcast_to(low_ref[row, :], (width, height)).T
+        high = jnp.broadcast_to(high_ref[row, :], (width, height)).T
+        out[0] = jnp.where(lane == 0, low, rolled(slant[0], 1))
+        out[1] = jnp.where(lane == width - 1, high, rolled(slant[1], -1))
+
+
+def slants(plane_e, plane_o, low, high, slant_e, slant_o):
+    out = jax.ShapeDtypeStruct(slant_e.shape, F32)
     smem = pl.BlockSpec(memory_space=pltpu.SMEM)
     return pl.pallas_call(
-        corner_kernel,
+        slant_kernel,
         out_shape=(out, out),
-        in_specs=[smem, smem, vmem_spec(), vmem_spec()],
+        in_specs=[smem] * 2 + [vmem_spec()] * 4,
         out_specs=(vmem_spec(), vmem_spec()),
         compiler_params=params(),
-        name="corners",
-    )(plane_1, plane_2, low, high)
+        name="slants",
+    )(plane_e, plane_o, low, high, slant_e, slant_o)
 
 
 def inner_kernel(
@@ -627,6 +632,12 @@
     )(value)
 
 
+def targets_of(read_ref, plane):
+    return [
+        read_ref.at[jnp.where(plane == 1, MINUS[slot], PLUS[slot]), plane] for slot in range(5)
+    ]
+
+
 def finish_kernel(
     plane_e,
     plane_o,
@@ -634,10 +645,8 @@
     conf_ref,
     got_e,
     sent_e,
-    corner_e,
     got_o,
     sent_o,
-    corner_o,
     _,
     __,
     read_ref,
@@ -646,21 +655,18 @@
     new_tile,
     sems,
 ):
-    height, width = conf_ref.shape[2:]
-    faces = ((plane_o[0], got_o, sent_o, corner_o), (plane_e[0], got_e, sent_e, corner_e))
-    lane = lax.broadcasted_iota(jnp.int32, (height, width), 1)
+    height = conf_ref.shape[2]
+    faces = ((plane_o[0], got_o, sent_o), (plane_e[0], got_e, sent_e))
     copies = []
 
     def send(source, target):
         copies.append(pltpu.make_async_copy(source, target, sems.at[len(copies)]))
         copies[-1].start()
 
-    for face, (plane, got, sent, corner) in enumerate(faces):
+    for face, (plane, got, sent) in enumerate(faces):
         half_sign = jnp.where(plane == 1, 0.5, -0.5).astype(F32)
         tile = read_tile.at[face]
-        targets = [
-            read_ref.at[jnp.where(plane == 1, MINUS[slot], PLUS[slot]), plane] for slot in range(5)
-        ]
+        targets = targets_of(read_ref, plane)
         send(got.at[3], targets[0])
 
         def rows(start, face=face, plane=plane, half_sign=half_sign, got=got):
@@ -683,36 +689,52 @@
         tile[1, 0 : height - 1, :] = got[5, 1:height, :]
         tile[1, height - 1 : height, :] = sent[4, height - 1 : height, :]
         send(tile.at[1], targets[2])
-        low = jnp.broadcast_to(corner[0:1, :], (width, height)).T
-        tile[2] = jnp.where(lane == 0, low, rolled(got[6], 1))
-        send(tile.at[2], targets[3])
-        high = jnp.broadcast_to(corner[1:2, :], (width, height)).T
-        tile[3] = jnp.where(lane == width - 1, high, rolled(got[7], -1))
-        send(tile.at[3], targets[4])
     for copy in copies:
         copy.wait()
 
 
-def finish(plane_e, plane_o, part, conform, even, odd, read):
+def last_kernel(plane_e, plane_o, slant_e, slant_o, _, read_ref, sems):
+    copies = []
+    for plane, slant in ((plane_o[0], slant_o), (plane_e[0], slant_e)):
+        targets = targets_of(read_ref, plane)
+        for slot in (3, 4):
+            copies.append(
+                pltpu.make_async_copy(slant.at[slot - 3], targets[slot], sems.at[len(copies)])
+            )
+            copies[-1].start()
+    for copy in copies:
+        copy.wait()
+
+
+def finish(plane_e, plane_o, part, conform, even, odd, slant_e, slant_o, read):
     height, width = conform.shape[2:]
     smem = pl.BlockSpec(memory_space=pltpu.SMEM)
-    return pl.pallas_call(
+    read_shape = jax.ShapeDtypeStruct(read.shape, F32)
+    read, new = pl.pallas_call(
         finish_kernel,
-        out_shape=(
-            jax.ShapeDtypeStruct(read.shape, F32),
-            jax.ShapeDtypeStruct(conform.shape, F32),
-        ),
-        in_specs=[smem] * 2 + [vmem_spec()] * 8 + [any_spec()] * 2,
+        out_shape=(read_shape, jax.ShapeDtypeStruct(conform.shape, F32)),
+        in_specs=[smem] * 2 + [vmem_spec()] * 6 + [any_spec()] * 2,
         out_specs=(any_spec(), any_spec()),
         scratch_shapes=[
-            VMEM((2, 4, height, width), F32),
+            VMEM((2, 2, height, width), F32),
             VMEM((2, 6, height, width), F32),
-            pltpu.SemaphoreType.DMA((12,)),
+            pltpu.SemaphoreType.DMA((8,)),
         ],
-        input_output_aliases={10: 0},
+        input_output_aliases={8: 0},
         compiler_params=params(),
         name="finish",
     )(plane_e, plane_o, part, conform, *even, *odd, read, touch(even[0]))
+    read = pl.pallas_call(
+        last_kernel,
+        out_shape=read_shape,
+        in_specs=[smem] * 2 + [vmem_spec()] * 2 + [any_spec()],
+        out_specs=any_spec(),
+        scratch_shapes=[pltpu.SemaphoreType.DMA((4,))],
+        input_output_aliases={4: 0},
+        compiler_params=params(),
+        name="last",
+    )(plane_e, plane_o, slant_e, slant_o, read)
+    return read, new
 
 
 def body(popul, conform):
@@ -737,17 +759,17 @@
     early_o = lax.ppermute(early, "wide", odd_pairs)
     late_o = lax.ppermute(late, "wide", odd_pairs)
     pre = prepare(conform, conf_low, conf_high)
-    post, sent_e, z_up, z_down = collide(plane_e, popul, sums, pre, early_e)
+    post, sent_e, slant_e, z_up, z_down = collide(plane_e, popul, sums, pre, early_e)
     got_e = lax.ppermute(sent_e, "wide", even_pairs)
-    post, sent_o, z_up, z_down = collide(
+    post, sent_o, slant_o, z_up, z_down = collide(
         plane_o, popul, sums, pre, early_o, (post, z_up, z_down, late_e)
     )
     got_o = lax.ppermute(sent_o, "wide", odd_pairs)
     low = lax.ppermute(z_up, "narrow", up)
     high = lax.ppermute(z_down, "narrow", down)
-    corner_e, corner_o = corners(plane_e, plane_o, low, high)
-    corner_e = lax.ppermute(corner_e, "wide", even_pairs)
-    corner_o = lax.ppermute(corner_o, "wide", odd_pairs)
+    slant_e, slant_o = slants(plane_e, plane_o, low, high, slant_e, slant_o)
+    slant_e = lax.ppermute(slant_e, "wide", even_pairs)
+    slant_o = lax.ppermute(slant_o, "wide", odd_pairs)
     read, part = inner(
         plane_e,
         plane_o,
@@ -761,9 +783,9 @@
         sent_e,
         sent_o,
     )
-    even = (got_e, sent_e, corner_e)
-    odd = (got_o, sent_o, corner_o)
-    return finish(plane_e, plane_o, part, conform, even, odd, read)
+    even = (got_e, sent_e)
+    odd = (got_o, sent_o)
+    return finish(plane_e, plane_o, part, conform, even, odd, slant_e, slant_o, read)
 
 
 def solution(mesh):

time: 46.4 us -> 45.8 us (0.987)
  Pallas kernels: 8.83 us -> 9.65 us
  waiting for transfers between devices: 13.6 us -> 12.8 us
  starting transfers between devices: 20.3 us -> 19.7 us
    ppermute x1, waiting for transfers between devices: 6.13 us -> 4.73 us  [body(): late_o = lax.ppermute(late, 'wide', odd_pairs)]
    ppermute x1, waiting for transfers between devices: 1.98 us -> 2.97 us  [body(): got_e = lax.ppermute(sent_e, 'wide', even_pairs)]
    pallas_call x2 -> x3, Pallas kernels: 1.25 us -> 2.07 us  [the longest x1 1.13 us: finish(): pl.pallas_call(finish_kernel, out_shape=(read_shape, jax.ShapeDtypeStruct...]
    ppermute x2, starting transfers between devices: 4.15 us -> 3.5 us  [the longest x1 3.43 us: body(): slant_o = lax.ppermute(slant_o, 'wide', odd_pairs)]
    ppermute x1, waiting for transfers between devices: 1.33 us -> 0.73 us  [body(): low = lax.ppermute(z_up, 'narrow', up)]
  transfers between devices with their start and end apart: 12 -> 12, of which waited for: 5 -> 6; matrix products, arithmetic and copies ran while one was open for 0% -> 0% of each run, Pallas kernels for 16% -> 19%
where the time goes in v6:
time: 45.8 us; the launch traced here: 45.6 us
  starting transfers between devices  19.7 us (43%)
  waiting for transfers between devices  12.8 us (28%)
  Pallas kernels  9.65 us (21%)
  local copies, waits for them, and re-layouts  2.83 us (6%)
  between operations  0.74 us (2%)
    ppermute x1, waiting for transfers between devices, body(): late_o = lax.ppermute(late, 'wide', odd_pairs)  4.73 us
    ppermute x1, starting transfers between devices, body(): got_o = lax.ppermute(sent_o, 'wide', odd_pairs)  4.16 us
    ppermute x1, starting transfers between devices, body(): early_o = lax.ppermute(early, 'wide', odd_pairs)  3.61 us
    ppermute x1, starting transfers between devices, body(): slant_o = lax.ppermute(slant_o, 'wide', odd_pairs)  3.43 us
    ppermute x1, waiting for transfers between devices, body(): early_e = lax.ppermute(early, 'wide', even_pairs)  3.27 us
    pallas_call x1, Pallas kernels, inner(): pl.pallas_call(inner_kernel, grid=(1,), out_shape=(jax.ShapeDtypeStruct(p...  3.27 us
    ppermute x1, starting transfers between devices, body(): early_e = lax.ppermute(early, 'wide', even_pairs)  3.03 us
    ppermute x1, waiting for transfers between devices, body(): got_e = lax.ppermute(sent_e, 'wide', even_pairs)  2.97 us
  transfers between devices with their start and end apart: 12, of which 6 were waited for; matrix products, arithmetic and copies ran while one was open for 0% of the time, Pallas kernels for 19%

profile of v6, /device:TPU:0, one launch (start us, length us, event | category | flops | bytes accessed | tf_op | source)
XLA Modules:
  0.0 45.6 jit_solution(15509399496075400613)
XLA Ops:
  0.6 0.0 copy-start.1
  0.6 1.1 %copy-done.1 = f32[6,2,128,128]{3,2,1,0:T(8,128)S(1)} copy-done((f32[6,2,128,128]{3,2,1,0:T(8,128)S(1)}, f32[6,2,128,128]{3,2,1,0:T(8,128)}, u32[]{:S(2)}) %copy-start.1) | copy-done | bytes 786456
  1.8 0.1 load.1
  1.9 3.0 %collective-permute-start.3 = (f32[4,128,128]{2,1,0:T(8,128)S(1)}, f32[4,128,128]{2,1,0:T(8,128)S(1)}, u32[]{:S(2)}, u32[]{:S(2)}) collective-permute-start(f32[4,128,128]{2,1,0:T(8,128)S(1)} %get-tuple-element.33), channel_id=1, source_target_pairs={{0,4},{4,0},{8,12},{12,8},{16,20},{20,16},{24,28},{28,24},{1,5},{5... | collective-permute-start | bytes 786440 | tf_op jit(solution)/shard_map/ppermute | solution.py:752
  4.9 0.7 %edges.1 = (f32[16,128]{1,0:T(8,128)S(1)}, f32[16,128]{1,0:T(8,128)S(1)}) custom-call(f32[6,2,128,128]{3,2,1,0:T(8,128)S(1)} %get-tuple-element.27.conf_ref), custom_call_target="tpu_custom_call" | custom-call | tf_op jit(solution)/shard_map/edges/pallas_call | solution.py:152
  5.7 3.6 %collective-permute-start.2 = (f32[4,128,128]{2,1,0:T(8,128)S(1)}, f32[4,128,128]{2,1,0:T(8,128)S(1)}, u32[]{:S(2)}, u32[]{:S(2)}) collective-permute-start(f32[4,128,128]{2,1,0:T(8,128)S(1)} %get-tuple-element.29._), channel_id=1, source_target_pairs={{0,28},{4,8},{8,4},{12,16},{16,12},{20,24},{24,20},{28,0},{1,29},{... | collective-permute-start | bytes 786440 | tf_op jit(solution)/shard_map/ppermute | solution.py:759
  9.3 0.0 collective-permute-start.4
  9.3 0.4 collective-permute-start.1
  9.6 0.1 collective-permute-start
  9.8 0.0 copy-start
  9.8 1.7 %copy-done = f32[19,2,128,128]{3,2,1,0:T(8,128)S(1)} copy-done((f32[19,2,128,128]{3,2,1,0:T(8,128)S(1)}, f32[19,2,128,128]{3,2,1,0:T(8,128)}, u32[]{:S(2)}) %copy-start) | copy-done | bytes 2490392
  11.5 0.4 moments.1
  11.9 0.0 collective-permute-done.1.high_cols.conf_high_cols
  12.0 0.8 %collective-permute-done.low_cols.conf_low_cols = f32[16,128]{1,0:T(8,128)S(1)} collective-permute-done((f32[16,128]{1,0:T(8,128)S(1)}, f32[16,128]{1,0:T(8,128)S(1)}, u32[]{:S(2)}, u32[]{:S(2)}) %collective-permute-start) | collective-permute-done | bytes 8224 | tf_op jit(solution)/shard_map/ppermute | solution.py:755
  12.7 1.3 %prepare.1.pre_ref = f32[3,2,128,128]{3,2,1,0:T(8,128)S(1)} custom-call(f32[6,2,128,128]{3,2,1,0:T(8,128)S(1)} %get-tuple-element.27.conf_ref, f32[16,128]{1,0:T(8,128)S(1)} %collective-permute-done.low_cols.conf_low_cols, f32[16,128]{1,0:T(8,128)S(1)} %collective-permute-done.1.high_cols.conf_high_cols), custom_call_target="tpu_custom_call" | custom-call | tf_op jit(solution)/shard_map/prepare/pallas_call | solution.py:280
  14.0 3.3 %collective-permute-done.3.halo_ref.early_e = f32[4,128,128]{2,1,0:T(8,128)S(1)} collective-permute-done((f32[4,128,128]{2,1,0:T(8,128)S(1)}, f32[4,128,128]{2,1,0:T(8,128)S(1)}, u32[]{:S(2)}, u32[]{:S(2)}) %collective-permute-start.3) | collective-permute-done | bytes 262176 | tf_op jit(solution)/shard_map/ppermute | solution.py:752
  17.3 0.8 %collide_even.1 = (f32[19,2,128,128]{3,2,1,0:T(8,128)S(1)}, f32[6,128,128]{2,1,0:T(8,128)S(1)}, f32[2,128,128]{2,1,0:T(8,128)S(1)}, f32[128,128]{1,0:T(8,128)S(1)}, f32[128,128]{1,0:T(8,128)S(1)}) custom-call(s32[1]{0:T(128)} %bitcast.near_plane.plane_ref.plane_e, f32[19,2,128,128]{3,2,1,0:T(8,128)S(1)} %get-tuple-element.30.popul_ref, ...), custom_call_target="tpu_custom_call" | custom-call | tf_op jit(solution)/shard_map/collide_even/pallas_call | solution.py:371
  18.1 2.5 %collective-permute-start.10 = (f32[6,128,128]{2,1,0:T(8,128)S(1)}, f32[6,128,128]{2,1,0:T(8,128)S(1)}, u32[]{:S(2)}, u32[]{:S(2)}) collective-permute-start(f32[6,128,128]{2,1,0:T(8,128)S(1)} %get-tuple-element.46.velo_e.sent_e), channel_id=1, source_target_pairs={{0,4},{4,0},{8,12},{12,8},{16,20},{20,16},{24,28},{28,24},{1,5},{5... | collective-permute-start | bytes 1179656 | tf_op jit(solution)/shard_map/ppermute | solution.py:763
  20.6 0.0 collective-permute-done.4.refs_3_.late_e
  20.6 0.0 collective-permute-done.2.halo_ref.early_o
  20.6 0.9 %collide_odd.1 = (f32[19,2,128,128]{3,2,1,0:T(8,128)S(1)}, f32[6,128,128]{2,1,0:T(8,128)S(1)}, f32[2,128,128]{2,1,0:T(8,128)S(1)}, f32[16,128]{1,0:T(8,128)S(1)}, f32[16,128]{1,0:T(8,128)S(1)}) custom-call(s32[1]{0:T(128)} %bitcast.1.far_plane.plane_ref.plane_o, ...), custom_call_target="tpu_custom_call", output_to_operand_aliasing={{0}: (5, {})} | custom-call | tf_op jit(solution)/shard_map/collide_odd/pallas_call | solution.py:371
  21.5 4.2 %collective-permute-start.11 = (f32[6,128,128]{2,1,0:T(8,128)S(1)}, f32[6,128,128]{2,1,0:T(8,128)S(1)}, u32[]{:S(2)}, u32[]{:S(2)}) collective-permute-start(f32[6,128,128]{2,1,0:T(8,128)S(1)} %get-tuple-element.47.velo_o.sent_o), channel_id=1, source_target_pairs={{0,28},{4,8},{8,4},{12,16},{16,12},{20,24},{24,20},{28,0},{1,29},{... | collective-permute-start | bytes 1179656 | tf_op jit(solution)/shard_map/ppermute | solution.py:767
  25.7 0.0 collective-permute-start.5
  25.7 1.7 %collective-permute-start.6 = (f32[16,128]{1,0:T(8,128)S(1)}, f32[16,128]{1,0:T(8,128)S(1)}, u32[]{:S(2)}, u32[]{:S(2)}) collective-permute-start(f32[16,128]{1,0:T(8,128)S(1)} %get-tuple-element.39), channel_id=1, source_target_pairs={{1,0},{2,1},{3,2},{0,3},{5,4},{6,5},{7,6},{4,7},{9,8},{10,9},{11,1... | collective-permute-start | bytes 24584 | tf_op jit(solution)/shard_map/ppermute | solution.py:769
  27.4 0.6 %collective-permute-start.9 = (f32[2,128,128]{2,1,0:T(8,128)S(1)}, f32[2,128,128]{2,1,0:T(8,128)S(1)}, u32[]{:S(2)}, u32[]{:S(2)}) collective-permute-start(f32[2,128,128]{2,1,0:T(8,128)S(1)} %get-tuple-element.44), channel_id=1, source_target_pairs={{0,28},{4,8},{8,4},{12,16},{16,12},{20,24},{24,20},{28,0},{1,29},{... | collective-permute-start | bytes 393224 | tf_op jit(solution)/shard_map/ppermute | solution.py:760
  28.0 0.7 %collective-permute-done.5.low_ref.low_cols = f32[16,128]{1,0:T(8,128)S(1)} collective-permute-done((f32[16,128]{1,0:T(8,128)S(1)}, f32[16,128]{1,0:T(8,128)S(1)}, u32[]{:S(2)}, u32[]{:S(2)}) %collective-permute-start.5) | collective-permute-done | bytes 8224 | tf_op jit(solution)/shard_map/ppermute | solution.py:768
  28.8 0.0 collective-permute-done.6.high_ref.high_cols
  28.8 0.2 slants.1
  29.0 0.1 collective-permute-start.7
  29.1 3.4 %collective-permute-start.8 = (f32[2,128,128]{2,1,0:T(8,128)S(1)}, f32[2,128,128]{2,1,0:T(8,128)S(1)}, u32[]{:S(2)}, u32[]{:S(2)}) collective-permute-start(f32[2,128,128]{2,1,0:T(8,128)S(1)} %get-tuple-element.43), channel_id=1, source_target_pairs={{0,28},{4,8},{8,4},{12,16},{16,12},{20,24},{24,20},{28,0},{1,29},{... | collective-permute-start | bytes 393224 | tf_op jit(solution)/shard_map/ppermute | solution.py:772
  32.5 4.7 %collective-permute-done.9.late_o = f32[2,128,128]{2,1,0:T(8,128)S(1)} collective-permute-done((f32[2,128,128]{2,1,0:T(8,128)S(1)}, f32[2,128,128]{2,1,0:T(8,128)S(1)}, u32[]{:S(2)}, u32[]{:S(2)}) %collective-permute-start.9) | collective-permute-done | bytes 131104 | tf_op jit(solution)/shard_map/ppermute | solution.py:760
  37.3 3.3 %inner.1 = (f32[19,2,128,128]{3,2,1,0:T(8,128)}, f32[6,2,128,128]{3,2,1,0:T(8,128)S(1)}) custom-call(s32[1]{0:T(128)} %bitcast.near_plane.plane_ref.plane_e, s32[1]{0:T(128)} %bitcast.1.far_plane.plane_ref.plane_o, f32[6,2,128,128]{3,2,1,0:T(8,128)S(1)} %get-tuple-element.27.conf_ref, f32[4,128,128]{2,1,0:T(8,128)S(1)} %collective-permute-done.3.halo_ref.early_e, ...), custom_call_target="tpu_custom_call" | custom-call | tf_op jit(solution)/shard_map/inner/pallas_call | solution.py:583
  40.5 3.0 %collective-permute-done.10._.got_e = f32[6,128,128]{2,1,0:T(8,128)S(1)} collective-permute-done((f32[6,128,128]{2,1,0:T(8,128)S(1)}, f32[6,128,128]{2,1,0:T(8,128)S(1)}, u32[]{:S(2)}, u32[]{:S(2)}) %collective-permute-start.10) | collective-permute-done | bytes 393248 | tf_op jit(solution)/shard_map/ppermute | solution.py:763
  43.5 0.0 collective-permute-done.11.got_o
  43.5 1.1 %finish.1 = (f32[19,2,128,128]{3,2,1,0:T(8,128)}, f32[6,2,128,128]{3,2,1,0:T(8,128)}) custom-call(s32[1]{0:T(128)} %bitcast.near_plane.plane_ref.plane_e, s32[1]{0:T(128)} %bitcast.1.far_plane.plane_ref.plane_o, f32[6,2,128,128]{3,2,1,0:T(8,128)S(1)} %get-tuple-element.48.part_ref, ...), custom_call_target="tpu_custom_call", output_to_operand_aliasing={{0}: (8, {})} | custom-call | tf_op jit(solution)/shard_map/finish/pallas_call | solution.py:713
  44.6 0.3 collective-permute-done.7.slant_e
  44.9 0.0 collective-permute-done.8.slant_o
  44.9 0.7 %last.1 = f32[19,2,128,128]{3,2,1,0:T(8,128)} custom-call(s32[1]{0:T(128)} %bitcast.near_plane.plane_ref.plane_e, s32[1]{0:T(128)} %bitcast.1.far_plane.plane_ref.plane_o, f32[2,128,128]{2,1,0:T(8,128)S(1)} %collective-permute-done.7.slant_e, f32[2,128,128]{2,1,0:T(8,128)S(1)} %collective-permute-done.8.slant_o, ...), custom_call_target="tpu_custom_call", output_to_operand_aliasing={{}: (4, {})} | custom-call | tf_op jit(solution)/shard_map/last/pallas_call | solution.py:727
  (2 shorter events, 0.1 us)
Async XLA Ops:
  0.6 1.1 %copy-start.1 = (f32[6,2,128,128]{3,2,1,0:T(8,128)S(1)}, f32[6,2,128,128]{3,2,1,0:T(8,128)}, u32[]{:S(2)}) copy-start(f32[6,2,128,128]{3,2,1,0:T(8,128)} %conf_hbm.1) | copy-start | bytes 2359300
  1.9 15.4 %collective-permute-start.3 = (f32[4,128,128]{2,1,0:T(8,128)S(1)}, f32[4,128,128]{2,1,0:T(8,128)S(1)}, u32[]{:S(2)}, u32[]{:S(2)}) collective-permute-start(f32[4,128,128]{2,1,0:T(8,128)S(1)} %get-tuple-element.33), channel_id=1, source_target_pairs={{0,4},{4,0},{8,12},{12,8},{16,20},{20,16},{24,28},{28,24},{1,5},{5... | collective-permute-start | bytes 786440 | tf_op jit(solution)/shard_map/ppermute | solution.py:752
  5.7 14.9 %collective-permute-start.2 = (f32[4,128,128]{2,1,0:T(8,128)S(1)}, f32[4,128,128]{2,1,0:T(8,128)S(1)}, u32[]{:S(2)}, u32[]{:S(2)}) collective-permute-start(f32[4,128,128]{2,1,0:T(8,128)S(1)} %get-tuple-element.29._), channel_id=1, source_target_pairs={{0,28},{4,8},{8,4},{12,16},{16,12},{20,24},{24,20},{28,0},{1,29},{... | collective-permute-start | bytes 786440 | tf_op jit(solution)/shard_map/ppermute | solution.py:759
  9.3 11.3 %collective-permute-start.4 = (f32[2,128,128]{2,1,0:T(8,128)S(1)}, f32[2,128,128]{2,1,0:T(8,128)S(1)}, u32[]{:S(2)}, u32[]{:S(2)}) collective-permute-start(f32[2,128,128]{2,1,0:T(8,128)S(1)} %get-tuple-element.37), channel_id=1, source_target_pairs={{0,4},{4,0},{8,12},{12,8},{16,20},{20,16},{24,28},{28,24},{1,5},{5... | collective-permute-start | bytes 393224 | tf_op jit(solution)/shard_map/ppermute | solution.py:753
  9.3 2.7 %collective-permute-start.1 = (f32[16,128]{1,0:T(8,128)S(1)}, f32[16,128]{1,0:T(8,128)S(1)}, u32[]{:S(2)}, u32[]{:S(2)}) collective-permute-start(f32[16,128]{1,0:T(8,128)S(1)} %get-tuple-element.32), channel_id=1, source_target_pairs={{1,0},{2,1},{3,2},{0,3},{5,4},{6,5},{7,6},{4,7},{9,8},{10,9},{11,1... | collective-permute-start | bytes 24584 | tf_op jit(solution)/shard_map/ppermute | solution.py:756
  9.6 3.1 %collective-permute-start = (f32[16,128]{1,0:T(8,128)S(1)}, f32[16,128]{1,0:T(8,128)S(1)}, u32[]{:S(2)}, u32[]{:S(2)}) collective-permute-start(f32[16,128]{1,0:T(8,128)S(1)} %get-tuple-element.28._), channel_id=1, source_target_pairs={{0,1},{1,2},{2,3},{3,0},{4,5},{5,6},{6,7},{7,4},{8,9},{9,10},{10,1... | collective-permute-start | bytes 24584 | tf_op jit(solution)/shard_map/ppermute | solution.py:755
  9.8 1.7 %copy-start = (f32[19,2,128,128]{3,2,1,0:T(8,128)S(1)}, f32[19,2,128,128]{3,2,1,0:T(8,128)}, u32[]{:S(2)}) copy-start(f32[19,2,128,128]{3,2,1,0:T(8,128)} %popul_hbm.1) | copy-start | bytes 7471108
  18.1 25.4 %collective-permute-start.10 = (f32[6,128,128]{2,1,0:T(8,128)S(1)}, f32[6,128,128]{2,1,0:T(8,128)S(1)}, u32[]{:S(2)}, u32[]{:S(2)}) collective-permute-start(f32[6,128,128]{2,1,0:T(8,128)S(1)} %get-tuple-element.46.velo_e.sent_e), channel_id=1, source_target_pairs={{0,4},{4,0},{8,12},{12,8},{16,20},{20,16},{24,28},{28,24},{1,5},{5... | collective-permute-start | bytes 1179656 | tf_op jit(solution)/shard_map/ppermute | solution.py:763
  21.5 22.0 %collective-permute-start.11 = (f32[6,128,128]{2,1,0:T(8,128)S(1)}, f32[6,128,128]{2,1,0:T(8,128)S(1)}, u32[]{:S(2)}, u32[]{:S(2)}) collective-permute-start(f32[6,128,128]{2,1,0:T(8,128)S(1)} %get-tuple-element.47.velo_o.sent_o), channel_id=1, source_target_pairs={{0,28},{4,8},{8,4},{12,16},{16,12},{20,24},{24,20},{28,0},{1,29},{... | collective-permute-start | bytes 1179656 | tf_op jit(solution)/shard_map/ppermute | solution.py:767
  25.7 3.1 %collective-permute-start.5 = (f32[16,128]{1,0:T(8,128)S(1)}, f32[16,128]{1,0:T(8,128)S(1)}, u32[]{:S(2)}, u32[]{:S(2)}) collective-permute-start(f32[16,128]{1,0:T(8,128)S(1)} %get-tuple-element.38), channel_id=1, source_target_pairs={{0,1},{1,2},{2,3},{3,0},{4,5},{5,6},{6,7},{7,4},{8,9},{9,10},{10,1... | collective-permute-start | bytes 24584 | tf_op jit(solution)/shard_map/ppermute | solution.py:768
  25.7 3.1 %collective-permute-start.6 = (f32[16,128]{1,0:T(8,128)S(1)}, f32[16,128]{1,0:T(8,128)S(1)}, u32[]{:S(2)}, u32[]{:S(2)}) collective-permute-start(f32[16,128]{1,0:T(8,128)S(1)} %get-tuple-element.39), channel_id=1, source_target_pairs={{1,0},{2,1},{3,2},{0,3},{5,4},{6,5},{7,6},{4,7},{9,8},{10,9},{11,1... | collective-permute-start | bytes 24584 | tf_op jit(solution)/shard_map/ppermute | solution.py:769
  27.4 9.8 %collective-permute-start.9 = (f32[2,128,128]{2,1,0:T(8,128)S(1)}, f32[2,128,128]{2,1,0:T(8,128)S(1)}, u32[]{:S(2)}, u32[]{:S(2)}) collective-permute-start(f32[2,128,128]{2,1,0:T(8,128)S(1)} %get-tuple-element.44), channel_id=1, source_target_pairs={{0,28},{4,8},{8,4},{12,16},{16,12},{20,24},{24,20},{28,0},{1,29},{... | collective-permute-start | bytes 393224 | tf_op jit(solution)/shard_map/ppermute | solution.py:760
  29.0 15.9 %collective-permute-start.7 = (f32[2,128,128]{2,1,0:T(8,128)S(1)}, f32[2,128,128]{2,1,0:T(8,128)S(1)}, u32[]{:S(2)}, u32[]{:S(2)}) collective-permute-start(f32[2,128,128]{2,1,0:T(8,128)S(1)} %get-tuple-element.42), channel_id=1, source_target_pairs={{0,4},{4,0},{8,12},{12,8},{16,20},{20,16},{24,28},{28,24},{1,5},{5... | collective-permute-start | bytes 393224 | tf_op jit(solution)/shard_map/ppermute | solution.py:771
  29.1 15.8 %collective-permute-start.8 = (f32[2,128,128]{2,1,0:T(8,128)S(1)}, f32[2,128,128]{2,1,0:T(8,128)S(1)}, u32[]{:S(2)}, u32[]{:S(2)}) collective-permute-start(f32[2,128,128]{2,1,0:T(8,128)S(1)} %get-tuple-element.43), channel_id=1, source_target_pairs={{0,28},{4,8},{8,4},{12,16},{16,12},{20,24},{24,20},{28,0},{1,29},{... | collective-permute-start | bytes 393224 | tf_op jit(solution)/shard_map/ppermute | solution.py:772

commit v7 on v6

--- a/solution.py
+++ b/solution.py
@@ -48,7 +48,7 @@
     VELOCITIES.index(v) for v in ((0, 0, -1), (0, 1, -1), (0, -1, -1), (1, 0, -1), (-1, 0, -1))
 )
 COLUMNS = 16
-ROWS = 32
+ROWS = 64
 F32 = jnp.float32
 VMEM = pltpu.VMEM
 

time: 45.8 us -> 45.8 us (level)
  waiting for transfers between devices: 12.8 us -> 13.7 us
  Pallas kernels: 9.65 us -> 8.83 us
    ppermute x1, waiting for transfers between devices: 3.27 us -> 3.83 us  [body(): early_e = lax.ppermute(early, 'wide', even_pairs)]
  transfers between devices with their start and end apart: 12 -> 12, of which waited for: 6 -> 6; matrix products, arithmetic and copies ran while one was open for 0% -> 0% of each run, Pallas kernels for 19% -> 18%
where the time goes in v7:
time: 45.8 us; the launch traced here: 45.6 us
  starting transfers between devices  19.5 us (43%)
  waiting for transfers between devices  13.7 us (30%)
  Pallas kernels  8.83 us (19%)
  local copies, waits for them, and re-layouts  2.83 us (6%)
  between operations  0.74 us (2%)
    ppermute x1, waiting for transfers between devices, body(): late_o = lax.ppermute(late, 'wide', odd_pairs)  4.47 us
    ppermute x1, starting transfers between devices, body(): got_o = lax.ppermute(sent_o, 'wide', odd_pairs)  4.36 us
    ppermute x1, waiting for transfers between devices, body(): early_e = lax.ppermute(early, 'wide', even_pairs)  3.83 us
    ppermute x1, starting transfers between devices, body(): early_o = lax.ppermute(early, 'wide', odd_pairs)  3.61 us
    ppermute x1, starting transfers between devices, body(): slant_o = lax.ppermute(slant_o, 'wide', odd_pairs)  3.43 us
    ppermute x1, waiting for transfers between devices, body(): got_e = lax.ppermute(sent_e, 'wide', even_pairs)  3.4 us
    pallas_call x1, Pallas kernels, inner(): pl.pallas_call(inner_kernel, grid=(1,), out_shape=(jax.ShapeDtypeStruct(p...  3.15 us
    ppermute x1, starting transfers between devices, body(): early_e = lax.ppermute(early, 'wide', even_pairs)  3.03 us
  transfers between devices with their start and end apart: 12, of which 6 were waited for; matrix products, arithmetic and copies ran while one was open for 0% of the time, Pallas kernels for 18%

profile of v7, /device:TPU:0, one launch (start us, length us, event | category | flops | bytes accessed | tf_op | source)
XLA Modules:
  0.0 45.6 jit_solution(413744779149236872)
XLA Ops:
  0.6 0.0 copy-start.1
  0.6 1.1 %copy-done.1 = f32[6,2,128,128]{3,2,1,0:T(8,128)S(1)} copy-done((f32[6,2,128,128]{3,2,1,0:T(8,128)S(1)}, f32[6,2,128,128]{3,2,1,0:T(8,128)}, u32[]{:S(2)}) %copy-start.1) | copy-done | bytes 786456
  1.8 0.1 load.1
  1.9 3.0 %collective-permute-start.3 = (f32[4,128,128]{2,1,0:T(8,128)S(1)}, f32[4,128,128]{2,1,0:T(8,128)S(1)}, u32[]{:S(2)}, u32[]{:S(2)}) collective-permute-start(f32[4,128,128]{2,1,0:T(8,128)S(1)} %get-tuple-element.33), channel_id=1, source_target_pairs={{0,4},{4,0},{8,12},{12,8},{16,20},{20,16},{24,28},{28,24},{1,5},{5... | collective-permute-start | bytes 786440 | tf_op jit(solution)/shard_map/ppermute | solution.py:752
  4.9 0.6 %edges.1 = (f32[16,128]{1,0:T(8,128)S(1)}, f32[16,128]{1,0:T(8,128)S(1)}) custom-call(f32[6,2,128,128]{3,2,1,0:T(8,128)S(1)} %get-tuple-element.27.conf_ref), custom_call_target="tpu_custom_call" | custom-call | tf_op jit(solution)/shard_map/edges/pallas_call | solution.py:152
  5.5 3.6 %collective-permute-start.2 = (f32[4,128,128]{2,1,0:T(8,128)S(1)}, f32[4,128,128]{2,1,0:T(8,128)S(1)}, u32[]{:S(2)}, u32[]{:S(2)}) collective-permute-start(f32[4,128,128]{2,1,0:T(8,128)S(1)} %get-tuple-element.29._), channel_id=1, source_target_pairs={{0,28},{4,8},{8,4},{12,16},{16,12},{20,24},{24,20},{28,0},{1,29},{... | collective-permute-start | bytes 786440 | tf_op jit(solution)/shard_map/ppermute | solution.py:759
  9.1 0.0 collective-permute-start.4
  9.1 0.4 collective-permute-start.1
  9.5 0.1 collective-permute-start
  9.6 0.0 copy-start
  9.7 1.7 %copy-done = f32[19,2,128,128]{3,2,1,0:T(8,128)S(1)} copy-done((f32[19,2,128,128]{3,2,1,0:T(8,128)S(1)}, f32[19,2,128,128]{3,2,1,0:T(8,128)}, u32[]{:S(2)}) %copy-start) | copy-done | bytes 2490392
  11.4 0.4 moments.1
  11.8 0.0 collective-permute-done.1.high_cols.conf_high_cols
  11.8 0.8 %collective-permute-done.low_cols.conf_low_cols = f32[16,128]{1,0:T(8,128)S(1)} collective-permute-done((f32[16,128]{1,0:T(8,128)S(1)}, f32[16,128]{1,0:T(8,128)S(1)}, u32[]{:S(2)}, u32[]{:S(2)}) %collective-permute-start) | collective-permute-done | bytes 8224 | tf_op jit(solution)/shard_map/ppermute | solution.py:755
  12.6 1.0 %prepare.1.pre_ref = f32[3,2,128,128]{3,2,1,0:T(8,128)S(1)} custom-call(f32[6,2,128,128]{3,2,1,0:T(8,128)S(1)} %get-tuple-element.27.conf_ref, f32[16,128]{1,0:T(8,128)S(1)} %collective-permute-done.low_cols.conf_low_cols, f32[16,128]{1,0:T(8,128)S(1)} %collective-permute-done.1.high_cols.conf_high_cols), custom_call_target="tpu_custom_call" | custom-call | tf_op jit(solution)/shard_map/prepare/pallas_call | solution.py:280
  13.6 3.8 %collective-permute-done.3.halo_ref.early_e = f32[4,128,128]{2,1,0:T(8,128)S(1)} collective-permute-done((f32[4,128,128]{2,1,0:T(8,128)S(1)}, f32[4,128,128]{2,1,0:T(8,128)S(1)}, u32[]{:S(2)}, u32[]{:S(2)}) %collective-permute-start.3) | collective-permute-done | bytes 262176 | tf_op jit(solution)/shard_map/ppermute | solution.py:752
  17.4 0.7 %collide_even.1 = (f32[19,2,128,128]{3,2,1,0:T(8,128)S(1)}, f32[6,128,128]{2,1,0:T(8,128)S(1)}, f32[2,128,128]{2,1,0:T(8,128)S(1)}, f32[128,128]{1,0:T(8,128)S(1)}, f32[128,128]{1,0:T(8,128)S(1)}) custom-call(s32[1]{0:T(128)} %bitcast.near_plane.plane_ref.plane_e, f32[19,2,128,128]{3,2,1,0:T(8,128)S(1)} %get-tuple-element.30.popul_ref, ...), custom_call_target="tpu_custom_call" | custom-call | tf_op jit(solution)/shard_map/collide_even/pallas_call | solution.py:371
  18.1 2.3 %collective-permute-start.10 = (f32[6,128,128]{2,1,0:T(8,128)S(1)}, f32[6,128,128]{2,1,0:T(8,128)S(1)}, u32[]{:S(2)}, u32[]{:S(2)}) collective-permute-start(f32[6,128,128]{2,1,0:T(8,128)S(1)} %get-tuple-element.46.velo_e.sent_e), channel_id=1, source_target_pairs={{0,4},{4,0},{8,12},{12,8},{16,20},{20,16},{24,28},{28,24},{1,5},{5... | collective-permute-start | bytes 1179656 | tf_op jit(solution)/shard_map/ppermute | solution.py:763
  20.5 0.0 collective-permute-done.4.refs_3_.late_e
  20.5 0.0 collective-permute-done.2.halo_ref.early_o
  20.5 0.8 %collide_odd.1 = (f32[19,2,128,128]{3,2,1,0:T(8,128)S(1)}, f32[6,128,128]{2,1,0:T(8,128)S(1)}, f32[2,128,128]{2,1,0:T(8,128)S(1)}, f32[16,128]{1,0:T(8,128)S(1)}, f32[16,128]{1,0:T(8,128)S(1)}) custom-call(s32[1]{0:T(128)} %bitcast.1.far_plane.plane_ref.plane_o, ...), custom_call_target="tpu_custom_call", output_to_operand_aliasing={{0}: (5, {})} | custom-call | tf_op jit(solution)/shard_map/collide_odd/pallas_call | solution.py:371
  21.3 4.4 %collective-permute-start.11 = (f32[6,128,128]{2,1,0:T(8,128)S(1)}, f32[6,128,128]{2,1,0:T(8,128)S(1)}, u32[]{:S(2)}, u32[]{:S(2)}) collective-permute-start(f32[6,128,128]{2,1,0:T(8,128)S(1)} %get-tuple-element.47.velo_o.sent_o), channel_id=1, source_target_pairs={{0,28},{4,8},{8,4},{12,16},{16,12},{20,24},{24,20},{28,0},{1,29},{... | collective-permute-start | bytes 1179656 | tf_op jit(solution)/shard_map/ppermute | solution.py:767
  25.6 0.0 collective-permute-start.5
  25.6 1.7 %collective-permute-start.6 = (f32[16,128]{1,0:T(8,128)S(1)}, f32[16,128]{1,0:T(8,128)S(1)}, u32[]{:S(2)}, u32[]{:S(2)}) collective-permute-start(f32[16,128]{1,0:T(8,128)S(1)} %get-tuple-element.39), channel_id=1, source_target_pairs={{1,0},{2,1},{3,2},{0,3},{5,4},{6,5},{7,6},{4,7},{9,8},{10,9},{11,1... | collective-permute-start | bytes 24584 | tf_op jit(solution)/shard_map/ppermute | solution.py:769
  27.4 0.4 collective-permute-start.9
  27.8 0.9 %collective-permute-done.5.low_ref.low_cols = f32[16,128]{1,0:T(8,128)S(1)} collective-permute-done((f32[16,128]{1,0:T(8,128)S(1)}, f32[16,128]{1,0:T(8,128)S(1)}, u32[]{:S(2)}, u32[]{:S(2)}) %collective-permute-start.5) | collective-permute-done | bytes 8224 | tf_op jit(solution)/shard_map/ppermute | solution.py:768
  28.7 0.0 collective-permute-done.6.high_ref.high_cols
  28.7 0.2 slants.1
  29.0 0.1 collective-permute-start.7
  29.1 3.4 %collective-permute-start.8 = (f32[2,128,128]{2,1,0:T(8,128)S(1)}, f32[2,128,128]{2,1,0:T(8,128)S(1)}, u32[]{:S(2)}, u32[]{:S(2)}) collective-permute-start(f32[2,128,128]{2,1,0:T(8,128)S(1)} %get-tuple-element.43), channel_id=1, source_target_pairs={{0,28},{4,8},{8,4},{12,16},{16,12},{20,24},{24,20},{28,0},{1,29},{... | collective-permute-start | bytes 393224 | tf_op jit(solution)/shard_map/ppermute | solution.py:772
  32.5 4.5 %collective-permute-done.9.late_o = f32[2,128,128]{2,1,0:T(8,128)S(1)} collective-permute-done((f32[2,128,128]{2,1,0:T(8,128)S(1)}, f32[2,128,128]{2,1,0:T(8,128)S(1)}, u32[]{:S(2)}, u32[]{:S(2)}) %collective-permute-start.9) | collective-permute-done | bytes 131104 | tf_op jit(solution)/shard_map/ppermute | solution.py:760
  37.0 3.1 %inner.1 = (f32[19,2,128,128]{3,2,1,0:T(8,128)}, f32[6,2,128,128]{3,2,1,0:T(8,128)S(1)}) custom-call(s32[1]{0:T(128)} %bitcast.near_plane.plane_ref.plane_e, s32[1]{0:T(128)} %bitcast.1.far_plane.plane_ref.plane_o, f32[6,2,128,128]{3,2,1,0:T(8,128)S(1)} %get-tuple-element.27.conf_ref, f32[4,128,128]{2,1,0:T(8,128)S(1)} %collective-permute-done.3.halo_ref.early_e, ...), custom_call_target="tpu_custom_call" | custom-call | tf_op jit(solution)/shard_map/inner/pallas_call | solution.py:583
  40.1 3.4 %collective-permute-done.10._.got_e = f32[6,128,128]{2,1,0:T(8,128)S(1)} collective-permute-done((f32[6,128,128]{2,1,0:T(8,128)S(1)}, f32[6,128,128]{2,1,0:T(8,128)S(1)}, u32[]{:S(2)}, u32[]{:S(2)}) %collective-permute-start.10) | collective-permute-done | bytes 393248 | tf_op jit(solution)/shard_map/ppermute | solution.py:763
  43.5 0.0 collective-permute-done.11.got_o
  43.5 1.1 %finish.1 = (f32[19,2,128,128]{3,2,1,0:T(8,128)}, f32[6,2,128,128]{3,2,1,0:T(8,128)}) custom-call(s32[1]{0:T(128)} %bitcast.near_plane.plane_ref.plane_e, s32[1]{0:T(128)} %bitcast.1.far_plane.plane_ref.plane_o, f32[6,2,128,128]{3,2,1,0:T(8,128)S(1)} %get-tuple-element.48.part_ref, ...), custom_call_target="tpu_custom_call", output_to_operand_aliasing={{0}: (8, {})} | custom-call | tf_op jit(solution)/shard_map/finish/pallas_call | solution.py:713
  44.6 0.3 collective-permute-done.7.slant_e
  44.9 0.0 collective-permute-done.8.slant_o
  44.9 0.7 %last.1 = f32[19,2,128,128]{3,2,1,0:T(8,128)} custom-call(s32[1]{0:T(128)} %bitcast.near_plane.plane_ref.plane_e, s32[1]{0:T(128)} %bitcast.1.far_plane.plane_ref.plane_o, f32[2,128,128]{2,1,0:T(8,128)S(1)} %collective-permute-done.7.slant_e, f32[2,128,128]{2,1,0:T(8,128)S(1)} %collective-permute-done.8.slant_o, ...), custom_call_target="tpu_custom_call", output_to_operand_aliasing={{}: (4, {})} | custom-call | tf_op jit(solution)/shard_map/last/pallas_call | solution.py:727
  (2 shorter events, 0.1 us)
Async XLA Ops:
  0.6 1.1 %copy-start.1 = (f32[6,2,128,128]{3,2,1,0:T(8,128)S(1)}, f32[6,2,128,128]{3,2,1,0:T(8,128)}, u32[]{:S(2)}) copy-start(f32[6,2,128,128]{3,2,1,0:T(8,128)} %conf_hbm.1) | copy-start | bytes 2359300
  1.9 15.6 %collective-permute-start.3 = (f32[4,128,128]{2,1,0:T(8,128)S(1)}, f32[4,128,128]{2,1,0:T(8,128)S(1)}, u32[]{:S(2)}, u32[]{:S(2)}) collective-permute-start(f32[4,128,128]{2,1,0:T(8,128)S(1)} %get-tuple-element.33), channel_id=1, source_target_pairs={{0,4},{4,0},{8,12},{12,8},{16,20},{20,16},{24,28},{28,24},{1,5},{5... | collective-permute-start | bytes 786440 | tf_op jit(solution)/shard_map/ppermute | solution.py:752
  5.5 15.0 %collective-permute-start.2 = (f32[4,128,128]{2,1,0:T(8,128)S(1)}, f32[4,128,128]{2,1,0:T(8,128)S(1)}, u32[]{:S(2)}, u32[]{:S(2)}) collective-permute-start(f32[4,128,128]{2,1,0:T(8,128)S(1)} %get-tuple-element.29._), channel_id=1, source_target_pairs={{0,28},{4,8},{8,4},{12,16},{16,12},{20,24},{24,20},{28,0},{1,29},{... | collective-permute-start | bytes 786440 | tf_op jit(solution)/shard_map/ppermute | solution.py:759
  9.1 11.4 %collective-permute-start.4 = (f32[2,128,128]{2,1,0:T(8,128)S(1)}, f32[2,128,128]{2,1,0:T(8,128)S(1)}, u32[]{:S(2)}, u32[]{:S(2)}) collective-permute-start(f32[2,128,128]{2,1,0:T(8,128)S(1)} %get-tuple-element.37), channel_id=1, source_target_pairs={{0,4},{4,0},{8,12},{12,8},{16,20},{20,16},{24,28},{28,24},{1,5},{5... | collective-permute-start | bytes 393224 | tf_op jit(solution)/shard_map/ppermute | solution.py:753
  9.1 2.7 %collective-permute-start.1 = (f32[16,128]{1,0:T(8,128)S(1)}, f32[16,128]{1,0:T(8,128)S(1)}, u32[]{:S(2)}, u32[]{:S(2)}) collective-permute-start(f32[16,128]{1,0:T(8,128)S(1)} %get-tuple-element.32), channel_id=1, source_target_pairs={{1,0},{2,1},{3,2},{0,3},{5,4},{6,5},{7,6},{4,7},{9,8},{10,9},{11,1... | collective-permute-start | bytes 24584 | tf_op jit(solution)/shard_map/ppermute | solution.py:756
  9.5 3.1 %collective-permute-start = (f32[16,128]{1,0:T(8,128)S(1)}, f32[16,128]{1,0:T(8,128)S(1)}, u32[]{:S(2)}, u32[]{:S(2)}) collective-permute-start(f32[16,128]{1,0:T(8,128)S(1)} %get-tuple-element.28._), channel_id=1, source_target_pairs={{0,1},{1,2},{2,3},{3,0},{4,5},{5,6},{6,7},{7,4},{8,9},{9,10},{10,1... | collective-permute-start | bytes 24584 | tf_op jit(solution)/shard_map/ppermute | solution.py:755
  9.6 1.7 %copy-start = (f32[19,2,128,128]{3,2,1,0:T(8,128)S(1)}, f32[19,2,128,128]{3,2,1,0:T(8,128)}, u32[]{:S(2)}) copy-start(f32[19,2,128,128]{3,2,1,0:T(8,128)} %popul_hbm.1) | copy-start | bytes 7471108
  18.1 25.4 %collective-permute-start.10 = (f32[6,128,128]{2,1,0:T(8,128)S(1)}, f32[6,128,128]{2,1,0:T(8,128)S(1)}, u32[]{:S(2)}, u32[]{:S(2)}) collective-permute-start(f32[6,128,128]{2,1,0:T(8,128)S(1)} %get-tuple-element.46.velo_e.sent_e), channel_id=1, source_target_pairs={{0,4},{4,0},{8,12},{12,8},{16,20},{20,16},{24,28},{28,24},{1,5},{5... | collective-permute-start | bytes 1179656 | tf_op jit(solution)/shard_map/ppermute | solution.py:763
  21.3 22.2 %collective-permute-start.11 = (f32[6,128,128]{2,1,0:T(8,128)S(1)}, f32[6,128,128]{2,1,0:T(8,128)S(1)}, u32[]{:S(2)}, u32[]{:S(2)}) collective-permute-start(f32[6,128,128]{2,1,0:T(8,128)S(1)} %get-tuple-element.47.velo_o.sent_o), channel_id=1, source_target_pairs={{0,28},{4,8},{8,4},{12,16},{16,12},{20,24},{24,20},{28,0},{1,29},{... | collective-permute-start | bytes 1179656 | tf_op jit(solution)/shard_map/ppermute | solution.py:767
  25.6 3.1 %collective-permute-start.5 = (f32[16,128]{1,0:T(8,128)S(1)}, f32[16,128]{1,0:T(8,128)S(1)}, u32[]{:S(2)}, u32[]{:S(2)}) collective-permute-start(f32[16,128]{1,0:T(8,128)S(1)} %get-tuple-element.38), channel_id=1, source_target_pairs={{0,1},{1,2},{2,3},{3,0},{4,5},{5,6},{6,7},{7,4},{8,9},{9,10},{10,1... | collective-permute-start | bytes 24584 | tf_op jit(solution)/shard_map/ppermute | solution.py:768
  25.6 3.1 %collective-permute-start.6 = (f32[16,128]{1,0:T(8,128)S(1)}, f32[16,128]{1,0:T(8,128)S(1)}, u32[]{:S(2)}, u32[]{:S(2)}) collective-permute-start(f32[16,128]{1,0:T(8,128)S(1)} %get-tuple-element.39), channel_id=1, source_target_pairs={{1,0},{2,1},{3,2},{0,3},{5,4},{6,5},{7,6},{4,7},{9,8},{10,9},{11,1... | collective-permute-start | bytes 24584 | tf_op jit(solution)/shard_map/ppermute | solution.py:769
  27.4 9.6 %collective-permute-start.9 = (f32[2,128,128]{2,1,0:T(8,128)S(1)}, f32[2,128,128]{2,1,0:T(8,128)S(1)}, u32[]{:S(2)}, u32[]{:S(2)}) collective-permute-start(f32[2,128,128]{2,1,0:T(8,128)S(1)} %get-tuple-element.44), channel_id=1, source_target_pairs={{0,28},{4,8},{8,4},{12,16},{16,12},{20,24},{24,20},{28,0},{1,29},{... | collective-permute-start | bytes 393224 | tf_op jit(solution)/shard_map/ppermute | solution.py:760
  29.0 15.9 %collective-permute-start.7 = (f32[2,128,128]{2,1,0:T(8,128)S(1)}, f32[2,128,128]{2,1,0:T(8,128)S(1)}, u32[]{:S(2)}, u32[]{:S(2)}) collective-permute-start(f32[2,128,128]{2,1,0:T(8,128)S(1)} %get-tuple-element.42), channel_id=1, source_target_pairs={{0,4},{4,0},{8,12},{12,8},{16,20},{20,16},{24,28},{28,24},{1,5},{5... | collective-permute-start | bytes 393224 | tf_op jit(solution)/shard_map/ppermute | solution.py:771
  29.1 15.9 %collective-permute-start.8 = (f32[2,128,128]{2,1,0:T(8,128)S(1)}, f32[2,128,128]{2,1,0:T(8,128)S(1)}, u32[]{:S(2)}, u32[]{:S(2)}) collective-permute-start(f32[2,128,128]{2,1,0:T(8,128)S(1)} %get-tuple-element.43), channel_id=1, source_target_pairs={{0,28},{4,8},{8,4},{12,16},{16,12},{20,24},{24,20},{28,0},{1,29},{... | collective-permute-start | bytes 393224 | tf_op jit(solution)/shard_map/ppermute | solution.py:772

commit v8 on v7

--- a/solution.py
+++ b/solution.py
@@ -48,7 +48,7 @@
     VELOCITIES.index(v) for v in ((0, 0, -1), (0, 1, -1), (0, -1, -1), (1, 0, -1), (-1, 0, -1))
 )
 COLUMNS = 16
-ROWS = 64
+ROWS = 128
 F32 = jnp.float32
 VMEM = pltpu.VMEM
 

time: 45.8 us -> 45.8 us (level)
  waiting for transfers between devices: 13.7 us -> 14.4 us
  Pallas kernels: 8.83 us -> 8.27 us
    ppermute x1, waiting for transfers between devices: 3.83 us -> 4.3 us  [body(): early_e = lax.ppermute(early, 'wide', even_pairs)]
  transfers between devices with their start and end apart: 12 -> 12, of which waited for: 6 -> 6; matrix products, arithmetic and copies ran while one was open for 0% -> 0% of each run, Pallas kernels for 18% -> 16%
where the time goes in v8:
time: 45.8 us; the launch traced here: 45.6 us
  starting transfers between devices  19.4 us (42%)
  waiting for transfers between devices  14.4 us (31%)
  Pallas kernels  8.27 us (18%)
  local copies, waits for them, and re-layouts  2.83 us (6%)
  between operations  0.74 us (2%)
    ppermute x1, starting transfers between devices, body(): got_o = lax.ppermute(sent_o, 'wide', odd_pairs)  4.47 us
    ppermute x1, waiting for transfers between devices, body(): late_o = lax.ppermute(late, 'wide', odd_pairs)  4.41 us
    ppermute x1, waiting for transfers between devices, body(): early_e = lax.ppermute(early, 'wide', even_pairs)  4.3 us
    ppermute x1, starting transfers between devices, body(): early_o = lax.ppermute(early, 'wide', odd_pairs)  3.61 us
    ppermute x1, waiting for transfers between devices, body(): got_e = lax.ppermute(sent_e, 'wide', even_pairs)  3.59 us
    ppermute x1, starting transfers between devices, body(): slant_o = lax.ppermute(slant_o, 'wide', odd_pairs)  3.43 us
    ppermute x1, starting transfers between devices, body(): early_e = lax.ppermute(early, 'wide', even_pairs)  3.03 us
    pallas_call x1, Pallas kernels, inner(): pl.pallas_call(inner_kernel, grid=(1,), out_shape=(jax.ShapeDtypeStruct(p...  3.03 us
  transfers between devices with their start and end apart: 12, of which 6 were waited for; matrix products, arithmetic and copies ran while one was open for 0% of the time, Pallas kernels for 16%

profile of v8, /device:TPU:0, one launch (start us, length us, event | category | flops | bytes accessed | tf_op | source)
XLA Modules:
  0.0 45.6 jit_solution(1698502954700614521)
XLA Ops:
  0.6 0.0 copy-start.1
  0.6 1.1 %copy-done.1 = f32[6,2,128,128]{3,2,1,0:T(8,128)S(1)} copy-done((f32[6,2,128,128]{3,2,1,0:T(8,128)S(1)}, f32[6,2,128,128]{3,2,1,0:T(8,128)}, u32[]{:S(2)}) %copy-start.1) | copy-done | bytes 786456
  1.8 0.1 load.1
  1.9 3.0 %collective-permute-start.3 = (f32[4,128,128]{2,1,0:T(8,128)S(1)}, f32[4,128,128]{2,1,0:T(8,128)S(1)}, u32[]{:S(2)}, u32[]{:S(2)}) collective-permute-start(f32[4,128,128]{2,1,0:T(8,128)S(1)} %get-tuple-element.33), channel_id=1, source_target_pairs={{0,4},{4,0},{8,12},{12,8},{16,20},{20,16},{24,28},{28,24},{1,5},{5... | collective-permute-start | bytes 786440 | tf_op jit(solution)/shard_map/ppermute | solution.py:752
  4.9 0.5 %edges.1 = (f32[16,128]{1,0:T(8,128)S(1)}, f32[16,128]{1,0:T(8,128)S(1)}) custom-call(f32[6,2,128,128]{3,2,1,0:T(8,128)S(1)} %get-tuple-element.27.conf_ref), custom_call_target="tpu_custom_call" | custom-call | tf_op jit(solution)/shard_map/edges/pallas_call | solution.py:152
  5.4 3.6 %collective-permute-start.2 = (f32[4,128,128]{2,1,0:T(8,128)S(1)}, f32[4,128,128]{2,1,0:T(8,128)S(1)}, u32[]{:S(2)}, u32[]{:S(2)}) collective-permute-start(f32[4,128,128]{2,1,0:T(8,128)S(1)} %get-tuple-element.29._), channel_id=1, source_target_pairs={{0,28},{4,8},{8,4},{12,16},{16,12},{20,24},{24,20},{28,0},{1,29},{... | collective-permute-start | bytes 786440 | tf_op jit(solution)/shard_map/ppermute | solution.py:759
  9.0 0.0 collective-permute-start.4
  9.0 0.4 collective-permute-start.1
  9.4 0.1 collective-permute-start
  9.6 0.0 copy-start
  9.6 1.7 %copy-done = f32[19,2,128,128]{3,2,1,0:T(8,128)S(1)} copy-done((f32[19,2,128,128]{3,2,1,0:T(8,128)S(1)}, f32[19,2,128,128]{3,2,1,0:T(8,128)}, u32[]{:S(2)}) %copy-start) | copy-done | bytes 2490392
  11.3 0.4 moments.1
  11.7 0.0 collective-permute-done.1.high_cols.conf_high_cols
  11.7 0.8 %collective-permute-done.low_cols.conf_low_cols = f32[16,128]{1,0:T(8,128)S(1)} collective-permute-done((f32[16,128]{1,0:T(8,128)S(1)}, f32[16,128]{1,0:T(8,128)S(1)}, u32[]{:S(2)}, u32[]{:S(2)}) %collective-permute-start) | collective-permute-done | bytes 8224 | tf_op jit(solution)/shard_map/ppermute | solution.py:755
  12.5 0.7 %prepare.1.pre_ref = f32[3,2,128,128]{3,2,1,0:T(8,128)S(1)} custom-call(f32[6,2,128,128]{3,2,1,0:T(8,128)S(1)} %get-tuple-element.27.conf_ref, f32[16,128]{1,0:T(8,128)S(1)} %collective-permute-done.low_cols.conf_low_cols, f32[16,128]{1,0:T(8,128)S(1)} %collective-permute-done.1.high_cols.conf_high_cols), custom_call_target="tpu_custom_call" | custom-call | tf_op jit(solution)/shard_map/prepare/pallas_call | solution.py:280
  13.2 4.3 %collective-permute-done.3.halo_ref.early_e = f32[4,128,128]{2,1,0:T(8,128)S(1)} collective-permute-done((f32[4,128,128]{2,1,0:T(8,128)S(1)}, f32[4,128,128]{2,1,0:T(8,128)S(1)}, u32[]{:S(2)}, u32[]{:S(2)}) %collective-permute-start.3) | collective-permute-done | bytes 262176 | tf_op jit(solution)/shard_map/ppermute | solution.py:752
  17.5 0.7 %collide_even.1 = (f32[19,2,128,128]{3,2,1,0:T(8,128)S(1)}, f32[6,128,128]{2,1,0:T(8,128)S(1)}, f32[2,128,128]{2,1,0:T(8,128)S(1)}, f32[128,128]{1,0:T(8,128)S(1)}, f32[128,128]{1,0:T(8,128)S(1)}) custom-call(s32[1]{0:T(128)} %bitcast.near_plane.plane_ref.plane_e, f32[19,2,128,128]{3,2,1,0:T(8,128)S(1)} %get-tuple-element.30.popul_ref, ...), custom_call_target="tpu_custom_call" | custom-call | tf_op jit(solution)/shard_map/collide_even/pallas_call | solution.py:371
  18.2 2.3 %collective-permute-start.10 = (f32[6,128,128]{2,1,0:T(8,128)S(1)}, f32[6,128,128]{2,1,0:T(8,128)S(1)}, u32[]{:S(2)}, u32[]{:S(2)}) collective-permute-start(f32[6,128,128]{2,1,0:T(8,128)S(1)} %get-tuple-element.46.velo_e.sent_e), channel_id=1, source_target_pairs={{0,4},{4,0},{8,12},{12,8},{16,20},{20,16},{24,28},{28,24},{1,5},{5... | collective-permute-start | bytes 1179656 | tf_op jit(solution)/shard_map/ppermute | solution.py:763
  20.4 0.0 collective-permute-done.4.refs_3_.late_e
  20.4 0.0 collective-permute-done.2.halo_ref.early_o
  20.4 0.7 %collide_odd.1 = (f32[19,2,128,128]{3,2,1,0:T(8,128)S(1)}, f32[6,128,128]{2,1,0:T(8,128)S(1)}, f32[2,128,128]{2,1,0:T(8,128)S(1)}, f32[16,128]{1,0:T(8,128)S(1)}, f32[16,128]{1,0:T(8,128)S(1)}) custom-call(s32[1]{0:T(128)} %bitcast.1.far_plane.plane_ref.plane_o, ...), custom_call_target="tpu_custom_call", output_to_operand_aliasing={{0}: (5, {})} | custom-call | tf_op jit(solution)/shard_map/collide_odd/pallas_call | solution.py:371
  21.2 4.5 %collective-permute-start.11 = (f32[6,128,128]{2,1,0:T(8,128)S(1)}, f32[6,128,128]{2,1,0:T(8,128)S(1)}, u32[]{:S(2)}, u32[]{:S(2)}) collective-permute-start(f32[6,128,128]{2,1,0:T(8,128)S(1)} %get-tuple-element.47.velo_o.sent_o), channel_id=1, source_target_pairs={{0,28},{4,8},{8,4},{12,16},{16,12},{20,24},{24,20},{28,0},{1,29},{... | collective-permute-start | bytes 1179656 | tf_op jit(solution)/shard_map/ppermute | solution.py:767
  25.6 0.0 collective-permute-start.5
  25.6 1.7 %collective-permute-start.6 = (f32[16,128]{1,0:T(8,128)S(1)}, f32[16,128]{1,0:T(8,128)S(1)}, u32[]{:S(2)}, u32[]{:S(2)}) collective-permute-start(f32[16,128]{1,0:T(8,128)S(1)} %get-tuple-element.39), channel_id=1, source_target_pairs={{1,0},{2,1},{3,2},{0,3},{5,4},{6,5},{7,6},{4,7},{9,8},{10,9},{11,1... | collective-permute-start | bytes 24584 | tf_op jit(solution)/shard_map/ppermute | solution.py:769
  27.4 0.3 collective-permute-start.9
  27.7 1.0 %collective-permute-done.5.low_ref.low_cols = f32[16,128]{1,0:T(8,128)S(1)} collective-permute-done((f32[16,128]{1,0:T(8,128)S(1)}, f32[16,128]{1,0:T(8,128)S(1)}, u32[]{:S(2)}, u32[]{:S(2)}) %collective-permute-start.5) | collective-permute-done | bytes 8224 | tf_op jit(solution)/shard_map/ppermute | solution.py:768
  28.7 0.0 collective-permute-done.6.high_ref.high_cols
  28.7 0.2 slants.1
  29.0 0.1 collective-permute-start.7
  29.0 3.4 %collective-permute-start.8 = (f32[2,128,128]{2,1,0:T(8,128)S(1)}, f32[2,128,128]{2,1,0:T(8,128)S(1)}, u32[]{:S(2)}, u32[]{:S(2)}) collective-permute-start(f32[2,128,128]{2,1,0:T(8,128)S(1)} %get-tuple-element.43), channel_id=1, source_target_pairs={{0,28},{4,8},{8,4},{12,16},{16,12},{20,24},{24,20},{28,0},{1,29},{... | collective-permute-start | bytes 393224 | tf_op jit(solution)/shard_map/ppermute | solution.py:772
  32.5 4.4 %collective-permute-done.9.late_o = f32[2,128,128]{2,1,0:T(8,128)S(1)} collective-permute-done((f32[2,128,128]{2,1,0:T(8,128)S(1)}, f32[2,128,128]{2,1,0:T(8,128)S(1)}, u32[]{:S(2)}, u32[]{:S(2)}) %collective-permute-start.9) | collective-permute-done | bytes 131104 | tf_op jit(solution)/shard_map/ppermute | solution.py:760
  36.9 3.0 %inner.1 = (f32[19,2,128,128]{3,2,1,0:T(8,128)}, f32[6,2,128,128]{3,2,1,0:T(8,128)S(1)}) custom-call(s32[1]{0:T(128)} %bitcast.near_plane.plane_ref.plane_e, s32[1]{0:T(128)} %bitcast.1.far_plane.plane_ref.plane_o, f32[6,2,128,128]{3,2,1,0:T(8,128)S(1)} %get-tuple-element.27.conf_ref, f32[4,128,128]{2,1,0:T(8,128)S(1)} %collective-permute-done.3.halo_ref.early_e, ...), custom_call_target="tpu_custom_call" | custom-call | tf_op jit(solution)/shard_map/inner/pallas_call | solution.py:583
  39.9 3.6 %collective-permute-done.10._.got_e = f32[6,128,128]{2,1,0:T(8,128)S(1)} collective-permute-done((f32[6,128,128]{2,1,0:T(8,128)S(1)}, f32[6,128,128]{2,1,0:T(8,128)S(1)}, u32[]{:S(2)}, u32[]{:S(2)}) %collective-permute-start.10) | collective-permute-done | bytes 393248 | tf_op jit(solution)/shard_map/ppermute | solution.py:763
  43.5 0.0 collective-permute-done.11.got_o
  43.5 1.2 %finish.1 = (f32[19,2,128,128]{3,2,1,0:T(8,128)}, f32[6,2,128,128]{3,2,1,0:T(8,128)}) custom-call(s32[1]{0:T(128)} %bitcast.near_plane.plane_ref.plane_e, s32[1]{0:T(128)} %bitcast.1.far_plane.plane_ref.plane_o, f32[6,2,128,128]{3,2,1,0:T(8,128)S(1)} %get-tuple-element.48.part_ref, ...), custom_call_target="tpu_custom_call", output_to_operand_aliasing={{0}: (8, {})} | custom-call | tf_op jit(solution)/shard_map/finish/pallas_call | solution.py:713
  44.7 0.2 collective-permute-done.7.slant_e
  44.9 0.0 collective-permute-done.8.slant_o
  44.9 0.7 %last.1 = f32[19,2,128,128]{3,2,1,0:T(8,128)} custom-call(s32[1]{0:T(128)} %bitcast.near_plane.plane_ref.plane_e, s32[1]{0:T(128)} %bitcast.1.far_plane.plane_ref.plane_o, f32[2,128,128]{2,1,0:T(8,128)S(1)} %collective-permute-done.7.slant_e, f32[2,128,128]{2,1,0:T(8,128)S(1)} %collective-permute-done.8.slant_o, ...), custom_call_target="tpu_custom_call", output_to_operand_aliasing={{}: (4, {})} | custom-call | tf_op jit(solution)/shard_map/last/pallas_call | solution.py:727
  (2 shorter events, 0.0 us)
Async XLA Ops:
  0.6 1.1 %copy-start.1 = (f32[6,2,128,128]{3,2,1,0:T(8,128)S(1)}, f32[6,2,128,128]{3,2,1,0:T(8,128)}, u32[]{:S(2)}) copy-start(f32[6,2,128,128]{3,2,1,0:T(8,128)} %conf_hbm.1) | copy-start | bytes 2359300
  1.9 15.7 %collective-permute-start.3 = (f32[4,128,128]{2,1,0:T(8,128)S(1)}, f32[4,128,128]{2,1,0:T(8,128)S(1)}, u32[]{:S(2)}, u32[]{:S(2)}) collective-permute-start(f32[4,128,128]{2,1,0:T(8,128)S(1)} %get-tuple-element.33), channel_id=1, source_target_pairs={{0,4},{4,0},{8,12},{12,8},{16,20},{20,16},{24,28},{28,24},{1,5},{5... | collective-permute-start | bytes 786440 | tf_op jit(solution)/shard_map/ppermute | solution.py:752
  5.4 15.0 %collective-permute-start.2 = (f32[4,128,128]{2,1,0:T(8,128)S(1)}, f32[4,128,128]{2,1,0:T(8,128)S(1)}, u32[]{:S(2)}, u32[]{:S(2)}) collective-permute-start(f32[4,128,128]{2,1,0:T(8,128)S(1)} %get-tuple-element.29._), channel_id=1, source_target_pairs={{0,28},{4,8},{8,4},{12,16},{16,12},{20,24},{24,20},{28,0},{1,29},{... | collective-permute-start | bytes 786440 | tf_op jit(solution)/shard_map/ppermute | solution.py:759
  9.0 11.4 %collective-permute-start.4 = (f32[2,128,128]{2,1,0:T(8,128)S(1)}, f32[2,128,128]{2,1,0:T(8,128)S(1)}, u32[]{:S(2)}, u32[]{:S(2)}) collective-permute-start(f32[2,128,128]{2,1,0:T(8,128)S(1)} %get-tuple-element.37), channel_id=1, source_target_pairs={{0,4},{4,0},{8,12},{12,8},{16,20},{20,16},{24,28},{28,24},{1,5},{5... | collective-permute-start | bytes 393224 | tf_op jit(solution)/shard_map/ppermute | solution.py:753
  9.0 2.7 %collective-permute-start.1 = (f32[16,128]{1,0:T(8,128)S(1)}, f32[16,128]{1,0:T(8,128)S(1)}, u32[]{:S(2)}, u32[]{:S(2)}) collective-permute-start(f32[16,128]{1,0:T(8,128)S(1)} %get-tuple-element.32), channel_id=1, source_target_pairs={{1,0},{2,1},{3,2},{0,3},{5,4},{6,5},{7,6},{4,7},{9,8},{10,9},{11,1... | collective-permute-start | bytes 24584 | tf_op jit(solution)/shard_map/ppermute | solution.py:756
  9.4 3.1 %collective-permute-start = (f32[16,128]{1,0:T(8,128)S(1)}, f32[16,128]{1,0:T(8,128)S(1)}, u32[]{:S(2)}, u32[]{:S(2)}) collective-permute-start(f32[16,128]{1,0:T(8,128)S(1)} %get-tuple-element.28._), channel_id=1, source_target_pairs={{0,1},{1,2},{2,3},{3,0},{4,5},{5,6},{6,7},{7,4},{8,9},{9,10},{10,1... | collective-permute-start | bytes 24584 | tf_op jit(solution)/shard_map/ppermute | solution.py:755
  9.6 1.7 %copy-start = (f32[19,2,128,128]{3,2,1,0:T(8,128)S(1)}, f32[19,2,128,128]{3,2,1,0:T(8,128)}, u32[]{:S(2)}) copy-start(f32[19,2,128,128]{3,2,1,0:T(8,128)} %popul_hbm.1) | copy-start | bytes 7471108
  18.2 25.3 %collective-permute-start.10 = (f32[6,128,128]{2,1,0:T(8,128)S(1)}, f32[6,128,128]{2,1,0:T(8,128)S(1)}, u32[]{:S(2)}, u32[]{:S(2)}) collective-permute-start(f32[6,128,128]{2,1,0:T(8,128)S(1)} %get-tuple-element.46.velo_e.sent_e), channel_id=1, source_target_pairs={{0,4},{4,0},{8,12},{12,8},{16,20},{20,16},{24,28},{28,24},{1,5},{5... | collective-permute-start | bytes 1179656 | tf_op jit(solution)/shard_map/ppermute | solution.py:763
  21.2 22.4 %collective-permute-start.11 = (f32[6,128,128]{2,1,0:T(8,128)S(1)}, f32[6,128,128]{2,1,0:T(8,128)S(1)}, u32[]{:S(2)}, u32[]{:S(2)}) collective-permute-start(f32[6,128,128]{2,1,0:T(8,128)S(1)} %get-tuple-element.47.velo_o.sent_o), channel_id=1, source_target_pairs={{0,28},{4,8},{8,4},{12,16},{16,12},{20,24},{24,20},{28,0},{1,29},{... | collective-permute-start | bytes 1179656 | tf_op jit(solution)/shard_map/ppermute | solution.py:767
  25.6 3.1 %collective-permute-start.5 = (f32[16,128]{1,0:T(8,128)S(1)}, f32[16,128]{1,0:T(8,128)S(1)}, u32[]{:S(2)}, u32[]{:S(2)}) collective-permute-start(f32[16,128]{1,0:T(8,128)S(1)} %get-tuple-element.38), channel_id=1, source_target_pairs={{0,1},{1,2},{2,3},{3,0},{4,5},{5,6},{6,7},{7,4},{8,9},{9,10},{10,1... | collective-permute-start | bytes 24584 | tf_op jit(solution)/shard_map/ppermute | solution.py:768
  25.6 3.1 %collective-permute-start.6 = (f32[16,128]{1,0:T(8,128)S(1)}, f32[16,128]{1,0:T(8,128)S(1)}, u32[]{:S(2)}, u32[]{:S(2)}) collective-permute-start(f32[16,128]{1,0:T(8,128)S(1)} %get-tuple-element.39), channel_id=1, source_target_pairs={{1,0},{2,1},{3,2},{0,3},{5,4},{6,5},{7,6},{4,7},{9,8},{10,9},{11,1... | collective-permute-start | bytes 24584 | tf_op jit(solution)/shard_map/ppermute | solution.py:769
  27.4 9.5 %collective-permute-start.9 = (f32[2,128,128]{2,1,0:T(8,128)S(1)}, f32[2,128,128]{2,1,0:T(8,128)S(1)}, u32[]{:S(2)}, u32[]{:S(2)}) collective-permute-start(f32[2,128,128]{2,1,0:T(8,128)S(1)} %get-tuple-element.44), channel_id=1, source_target_pairs={{0,28},{4,8},{8,4},{12,16},{16,12},{20,24},{24,20},{28,0},{1,29},{... | collective-permute-start | bytes 393224 | tf_op jit(solution)/shard_map/ppermute | solution.py:760
  29.0 16.0 %collective-permute-start.7 = (f32[2,128,128]{2,1,0:T(8,128)S(1)}, f32[2,128,128]{2,1,0:T(8,128)S(1)}, u32[]{:S(2)}, u32[]{:S(2)}) collective-permute-start(f32[2,128,128]{2,1,0:T(8,128)S(1)} %get-tuple-element.42), channel_id=1, source_target_pairs={{0,4},{4,0},{8,12},{12,8},{16,20},{20,16},{24,28},{28,24},{1,5},{5... | collective-permute-start | bytes 393224 | tf_op jit(solution)/shard_map/ppermute | solution.py:771
  29.0 15.9 %collective-permute-start.8 = (f32[2,128,128]{2,1,0:T(8,128)S(1)}, f32[2,128,128]{2,1,0:T(8,128)S(1)}, u32[]{:S(2)}, u32[]{:S(2)}) collective-permute-start(f32[2,128,128]{2,1,0:T(8,128)S(1)} %get-tuple-element.43), channel_id=1, source_target_pairs={{0,28},{4,8},{8,4},{12,16},{16,12},{20,24},{24,20},{28,0},{1,29},{... | collective-permute-start | bytes 393224 | tf_op jit(solution)/shard_map/ppermute | solution.py:772
